TPU v7x, 32 devices: a whole 2x2x4 slice. The times are simulated.
32 devices in a mesh: ta: 8 (over y, x, core), ba: 4 (over z).
Axes of the slice: x: 2, y: 2, z: 4, core: 2. Of those that a mesh axis runs over, the one named last changes fastest.
Arguments:
- search_block: float32 [16, 2, 4, 3, 16, 512], P(None, None, None, None, 'ta'), may hold values from -140 to 140
- kept_basis: float32 [128, 2, 4, 3, 16, 512], P('ba', None, None, None, 'ta'), may hold values from -4 to 4
- gauge_links: float32 [4, 2, 3, 3, 16, 512], P(None, None, None, None, 'ta'), may hold values from -1 to 1, as said below
- clover_term: float32 [2, 2, 6, 6, 16, 512], P(None, None, None, None, 'ta'), may hold values from -0.5 to 1.3, as said below
Outputs:
- ortho_block: float32 [16, 2, 4, 3, 16, 512], P('ba', None, None, None, 'ta')
- correlations: float32 [2, 128, 16], P(None, 'ba')
Inputs may be any that keep to these rules, and one draw needn't show every extreme that they name: `gauge_links`: every link matrix is special unitary. `clover_term`: each 6x6 block of the clover term is Hermitian.
All inputs are finite; a program needn't handle non-finite values.
Results may differ from a plain program's by a relative error of at most 0.0002.
Values sent between devices are 32-bit elements; how exact they have to be, the bound alone decides.
No kernel may reach another device: no remote copies, remote signals or barrier semaphores. Data moves between devices by JAX's collectives and lax.ppermute only.
A program may use at most 128 MiB of HBM per device.

v0:
```python
import jax
import jax.numpy as jnp
import numpy as np
from jax import lax
from jax.sharding import PartitionSpec as P

LS = 8


HOPPING = 0.13
HIGHEST = lax.Precision.HIGHEST


def passed_along(value, axis, steps):
    count = lax.axis_size(axis)
    pairs = [(source, (source + steps) % count) for source in range(count)]
    return lax.ppermute(value, axis, pairs)


def padded_2(cells, sides, width):
    for axis, dim in sides:
        count = lax.axis_size(axis)
        head = lax.slice_in_dim(cells, 0, width, axis=dim)
        tail = lax.slice_in_dim(cells, cells.shape[dim] - width, cells.shape[dim], axis=dim)
        cells = jnp.concatenate(
            [
                lax.ppermute(tail, axis, [(i, (i + 1) % count) for i in range(count)]),
                cells,
                lax.ppermute(head, axis, [((i + 1) % count, i) for i in range(count)]),
            ],
            axis=dim,
        )
    return cells


def gamma_tables():
    gamma_re = np.zeros((4, 4, 4), np.float32)
    gamma_im = np.zeros((4, 4, 4), np.float32)
    gamma_im[0, 0:2, 2:4] = [[0, -1], [-1, 0]]
    gamma_im[0, 2:4, 0:2] = [[0, 1], [1, 0]]
    gamma_re[1, 0:2, 2:4] = [[0, -1], [1, 0]]
    gamma_re[1, 2:4, 0:2] = [[0, 1], [-1, 0]]
    gamma_im[2, 0:2, 2:4] = [[-1, 0], [0, 1]]
    gamma_im[2, 2:4, 0:2] = [[1, 0], [0, -1]]
    gamma_re[3, 0:2, 2:4] = np.eye(2)
    gamma_re[3, 2:4, 0:2] = np.eye(2)
    return (gamma_re, gamma_im)


def gamma_apply(direction, spinor):
    tables_re, tables_im = gamma_tables()
    field_re = spinor[:, 0]
    field_im = spinor[:, 1]
    out_re = jnp.zeros_like(field_re)
    out_im = jnp.zeros_like(field_im)
    if np.any(tables_re[direction]):
        matrix = jnp.asarray(tables_re[direction])
        out_re = out_re + jnp.einsum("as,vsctx->vactx", matrix, field_re, precision=HIGHEST)
        out_im = out_im + jnp.einsum("as,vsctx->vactx", matrix, field_im, precision=HIGHEST)
    if np.any(tables_im[direction]):
        matrix = jnp.asarray(tables_im[direction])
        out_re = out_re - jnp.einsum("as,vsctx->vactx", matrix, field_im, precision=HIGHEST)
        out_im = out_im + jnp.einsum("as,vsctx->vactx", matrix, field_re, precision=HIGHEST)
    return jnp.stack([out_re, out_im], 1)


def gamma_five(spinor):
    return jnp.concatenate([spinor[:, :, :2], -spinor[:, :, 2:]], axis=2)


def colour(link_dir, spinor):
    link_re = link_dir[0][None, None]
    link_im = link_dir[1][None, None]
    field_re = spinor[:, 0][:, :, None]
    field_im = spinor[:, 1][:, :, None]
    out_re = jnp.sum(link_re * field_re - link_im * field_im, axis=3)
    out_im = jnp.sum(link_re * field_im + link_im * field_re, axis=3)
    return jnp.stack([out_re, out_im], 1)


def dagger(link_dir):
    return jnp.stack([link_dir[0].swapaxes(0, 1), -link_dir[1].swapaxes(0, 1)], 0)


def shift_space(values, stride, forward):
    coordinate = jnp.arange(values.shape[-1]) // stride % LS
    if forward:
        return jnp.where(
            coordinate == LS - 1,
            jnp.roll(values, (LS - 1) * stride, axis=-1),
            jnp.roll(values, -stride, axis=-1),
        )
    return jnp.where(
        coordinate == 0,
        jnp.roll(values, -(LS - 1) * stride, axis=-1),
        jnp.roll(values, stride, axis=-1),
    )


def space_hops(spinor, link_field):
    hop_total = jnp.zeros_like(spinor)
    strides = (LS * LS, LS, 1)
    for direction in range(3):
        stride = strides[direction]
        link_dir = link_field[direction]
        ahead_term = colour(link_dir, shift_space(spinor, stride, True))
        behind = colour(
            dagger(shift_space(link_dir, stride, False)), shift_space(spinor, stride, False)
        )
        hop_total = hop_total + (ahead_term + behind) - gamma_apply(direction, ahead_term - behind)
    return hop_total


def clover_apply(clover, spinor):
    vectors = spinor.shape[0]
    pieces = []
    for chiral in range(2):
        chiral_part = spinor[:, :, 2 * chiral : 2 * chiral + 2]
        flat_part = chiral_part.reshape(vectors, 2, 6, chiral_part.shape[-2], chiral_part.shape[-1])
        mat_re = clover[chiral, 0][None]
        mat_im = clover[chiral, 1][None]
        vec_re = flat_part[:, 0][:, None]
        vec_im = flat_part[:, 1][:, None]
        out_re = jnp.sum(mat_re * vec_re - mat_im * vec_im, axis=2)
        out_im = jnp.sum(mat_re * vec_im + mat_im * vec_re, axis=2)
        pieces.append(jnp.stack([out_re, out_im], 1).reshape(chiral_part.shape))
    return jnp.concatenate(pieces, axis=2)


def inner_product(left_re, left_im, right_re, right_im, norm_scale):
    real_part = jnp.einsum("kcn,jcn->kj", left_re, right_re, precision=HIGHEST) + jnp.einsum(
        "kcn,jcn->kj", left_im, right_im, precision=HIGHEST
    )
    imag_part = jnp.einsum("kcn,jcn->kj", left_re, right_im, precision=HIGHEST) - jnp.einsum(
        "kcn,jcn->kj", left_im, right_re, precision=HIGHEST
    )
    return (real_part * norm_scale, imag_part * norm_scale)


def combine_basis(coef_re, coef_im, vec_re, vec_im):
    out_re = jnp.einsum("kj,kcn->jcn", coef_re, vec_re, precision=HIGHEST) - jnp.einsum(
        "kj,kcn->jcn", coef_im, vec_im, precision=HIGHEST
    )
    out_im = jnp.einsum("kj,kcn->jcn", coef_im, vec_re, precision=HIGHEST) + jnp.einsum(
        "kj,kcn->jcn", coef_re, vec_im, precision=HIGHEST
    )
    return (out_re, out_im)


def cholesky_complex(gram_re, gram_im):
    matrix_order = gram_re.shape[0]
    lower_re = jnp.zeros_like(gram_re)
    lower_im = jnp.zeros_like(gram_im)
    index_row = jnp.arange(matrix_order)
    for column in range(matrix_order):
        row_re = lower_re[column]
        row_im = lower_im[column]
        acc_re = gram_re[:, column] - jnp.sum(
            lower_re * row_re[None, :] + lower_im * row_im[None, :], axis=1
        )
        acc_im = gram_im[:, column] - jnp.sum(
            lower_im * row_re[None, :] - lower_re * row_im[None, :], axis=1
        )
        pivot_value = jnp.sqrt(acc_re[column])
        below_mask = index_row > column
        new_re = jnp.where(
            index_row == column, pivot_value, jnp.where(below_mask, acc_re / pivot_value, 0.0)
        )
        new_im = jnp.where(below_mask, acc_im / pivot_value, 0.0)
        lower_re = lower_re.at[:, column].set(new_re)
        lower_im = lower_im.at[:, column].set(new_im)
    return (lower_re, lower_im)


def invert_lower(lower_re, lower_im):
    matrix_order = lower_re.shape[0]
    inverse_re = jnp.zeros_like(lower_re)
    inverse_im = jnp.zeros_like(lower_im)
    index_row = jnp.arange(matrix_order)
    for row_index in range(matrix_order):
        row_re = lower_re[row_index]
        row_im = lower_im[row_index]
        sum_re = jnp.sum(row_re[:, None] * inverse_re - row_im[:, None] * inverse_im, axis=0)
        sum_im = jnp.sum(row_re[:, None] * inverse_im + row_im[:, None] * inverse_re, axis=0)
        unit_row = jnp.where(index_row == row_index, 1.0, 0.0).astype(lower_re.dtype)
        pivot_value = lower_re[row_index, row_index]
        inverse_re = inverse_re.at[row_index].set((unit_row - sum_re) / pivot_value)
        inverse_im = inverse_im.at[row_index].set(-sum_im / pivot_value)
    return (inverse_re, inverse_im)


def per_device(search_block, kept_basis, gauge_links, clover_term):
    time_count = lax.axis_size("ta")
    time_place = lax.axis_index("ta")
    first_sign = jnp.where(time_place == 0, -1.0, 1.0).astype(jnp.float32)
    last_sign = jnp.where(time_place == time_count - 1, -1.0, 1.0).astype(jnp.float32)
    link_time = gauge_links[3]
    rim_link = passed_along(link_time[:, :, :, -1:], "ta", 1)
    link_back = jnp.concatenate([rim_link, link_time[:, :, :, :-1]], axis=3)

    def time_hops(spinor):
        diff_half = spinor[:, :, :2] - spinor[:, :, 2:]
        sum_half = spinor[:, :, :2] + spinor[:, :, 2:]
        padded = padded_2(spinor, (("ta", 4),), 1)
        below_slab = padded[:, :, :, :, 0:1] * first_sign
        above_slab = padded[:, :, :, :, -1:] * last_sign
        above_diff = above_slab[:, :, :2] - above_slab[:, :, 2:]
        below_sum = below_slab[:, :, :2] + below_slab[:, :, 2:]
        ahead_half = colour(
            link_time, jnp.concatenate([diff_half[:, :, :, :, 1:], above_diff], axis=4)
        )
        behind_half = colour(
            dagger(link_back), jnp.concatenate([below_sum, sum_half[:, :, :, :, :-1]], axis=4)
        )
        return jnp.concatenate([ahead_half + behind_half, behind_half - ahead_half], axis=2)

    def local_dirac(spinor):
        hops = space_hops(spinor, gauge_links) + time_hops(spinor)
        return clover_apply(clover_term, spinor) - HOPPING * hops

    first_apply = local_dirac(search_block)
    applied = gamma_five(local_dirac(gamma_five(first_apply)))
    block_size = search_block.shape[0]
    kept_local = kept_basis.shape[0]
    slab_sites = search_block.shape[4] * search_block.shape[5]
    norm_scale = 1.0 / (24.0 * slab_sites * time_count)
    applied_re = applied[:, 0].reshape(block_size, 12, slab_sites)
    applied_im = applied[:, 1].reshape(block_size, 12, slab_sites)
    basis_re = kept_basis[:, 0].reshape(kept_local, 12, slab_sites)
    basis_im = kept_basis[:, 1].reshape(kept_local, 12, slab_sites)
    group_size = lax.axis_size("ba")
    group_place = lax.axis_index("ba")
    out_vectors = block_size // group_size
    part_re, part_im = inner_product(basis_re, basis_im, applied_re, applied_im, norm_scale)
    over_mine_re, over_mine_im = lax.psum((part_re, part_im), "ta")
    proj_re, proj_im = combine_basis(over_mine_re, over_mine_im, basis_re, basis_im)
    full_re, full_im = lax.psum((proj_re, proj_im), "ba")
    rest_re = applied_re - full_re
    rest_im = applied_im - full_im
    gram_part_re, gram_part_im = inner_product(rest_re, rest_im, rest_re, rest_im, norm_scale)
    gram_re, gram_im = lax.psum((gram_part_re, gram_part_im), "ta")
    lower_re, lower_im = cholesky_complex(gram_re, gram_im)
    inverse_re, inverse_im = invert_lower(lower_re, lower_im)
    own_start = group_place * out_vectors
    coef_re = lax.dynamic_slice_in_dim(inverse_re, own_start, out_vectors, 0).T
    coef_im = -lax.dynamic_slice_in_dim(inverse_im, own_start, out_vectors, 0).T
    back_re, back_im = combine_basis(coef_re, coef_im, rest_re, rest_im)
    ortho_out = jnp.stack([back_re, back_im], 1).reshape(
        out_vectors, 2, 4, 3, search_block.shape[4], search_block.shape[5]
    )
    return (ortho_out, jnp.stack([over_mine_re, over_mine_im], 0))


def solution(mesh):
    placed = (
        P(None, None, None, None, "ta", None),
        P("ba", None, None, None, "ta", None),
        P(None, None, None, None, "ta", None),
        P(None, None, None, None, "ta", None),
    )
    return jax.shard_map(
        per_device,
        mesh=mesh,
        in_specs=placed,
        out_specs=(P("ba", None, None, None, "ta", None), P(None, "ba", None)),
        check_vma=False,
    )
```

profile of v0, /device:TPU:0, one launch (start us, length us, event | category | flops | bytes accessed | tf_op | source)
XLA Modules:
  0.0 418.0 jit_solution(5778324458546168435)
XLA Ops:
  7.2 3.5 fusion.202
  13.1 2.6 collective-permute-start.1
  36.0 2.4 convolution_bitcast_fusion.4
  43.3 2.5 fusion.207
  73.8 2.4 convolution_bitcast_fusion.5
  88.1 2.4 fusion.29
  96.9 3.4 reshape_squeeze.13
  102.2 3.4 reshape_squeeze.14
  115.6 4.0 maximum_subtract_fusion
  120.9 2.7 fusion.7
  124.8 2.5 fusion.6
  127.9 2.5 fusion.3
  130.4 2.9 fusion.2
  158.7 2.5 fusion
  177.9 2.4 collective-permute-done.3
  180.7 2.8 collective-permute-done.4
  187.9 4.2 maximum_subtract_fusion.2
  193.4 2.5 fusion.31
  196.0 2.5 fusion.30
  198.5 2.5 fusion.40
  201.1 2.6 fusion.43
  203.6 22.6 %all-reduce.5 = (f32[32,16]{0,1:T(8,128)S(1)}, f32[32,16]{0,1:T(8,128)S(1)}) all-reduce(f32[32,16]{0,1:T(8,128)S(1)} %fusion.43, f32[32,16]{0,1:T(8,128)S(1)} %fusion.40), channel_id=1, replica_groups=mesh['ta'=8,'ba'=4] {'ta'}, use_global_device_ids=true, to_apply=%region_41.42 | all-reduce | flops 1024 | bytes 8192 | tf_op jit(solution)/shard_map/psum | solution.py:235
  244.9 57.7 %all-reduce.9.cloned.1.call-done = (f32[16,12,1024]{2,0,1:T(8,128)}, f32[16,12,1024]{2,0,1:T(8,128)}) async-done(((f32[16,12,1024]{2,0,1:T(8,128)}, f32[16,12,1024]{2,0,1:T(8,128)}), (f32[16,12,1024]{2,0,1:T(8,128)}, f32[16,12,1024]{2,0,1:T(8,128)})) %all-reduce.9.cloned.1.call-update) | async-done | bytes 1572880 | tf_op jit(solution)/shard_map/psum | solution.py:237
  308.7 23.2 %all-reduce.4 = (f32[16,16]{1,0:T(8,128)S(1)}, f32[16,16]{1,0:T(8,128)S(1)}) all-reduce(f32[16,16]{1,0:T(8,128)S(1)} %fusion.35, f32[16,16]{1,0:T(8,128)S(1)} %fusion.37), channel_id=1, replica_groups=mesh['ta'=8,'ba'=4] {'ta'}, use_global_device_ids=true, to_apply=%region_45.46 | all-reduce | flops 512 | bytes 4096 | tf_op jit(solution)/shard_map/psum | solution.py:241
  (689 shorter events, 225.4 us)
Async XLA Ops:
  7.2 295.5 %all-reduce.9.cloned.1.call-start = ((), (), s32[]{:S(2)}) async-start(), calls=%async_computation | async-start | bytes 3145728 | tf_op jit(solution)/shard_map/psum | solution.py:237
  11.9 94.7 %collective-permute-start.2 = (f32[16,2,4,3,1,512]{5,2,4,3,0,1:T(4,128)}, f32[16,2,4,3,1,512]{5,2,4,3,0,1:T(4,128)}, u32[]{:S(2)}, u32[]{:S(2)}) collective-permute-start(f32[16,2,4,3,1,512]{5,2,4,3,0,1:T(4,128)} %copy.397), channel_id=1, source_target_pairs={{0,4},{4,8},{8,12},{12,16},{16,20},{20,24},{24,28},{28,0},{1,5},{5... | collective-permute-start | bytes 2359304 | tf_op jit(solution)/shard_map/ppermute | solution.py:27
  13.1 92.6 %collective-permute-start.1 = (f32[2,3,3,1,512]{4,3,2,1,0:T(1,128)}, f32[2,3,3,1,512]{4,3,2,1,0:T(1,128)}, u32[]{:S(2)}, u32[]{:S(2)}) collective-permute-start(f32[2,3,3,1,512]{4,3,2,1,0:T(1,128)} %get-tuple-element.1017), channel_id=1, source_target_pairs={{0,4},{4,8},{8,12},{12,16},{16,20},{20,24},{24,28},{28,0},{1,5},{5... | collective-permute-start | bytes 110600 | tf_op jit(solution)/shard_map/ppermute | solution.py:17
  16.8 93.2 %collective-permute-start = (f32[16,2,4,3,1,512]{5,2,4,3,0,1:T(4,128)}, f32[16,2,4,3,1,512]{5,2,4,3,0,1:T(4,128)}, u32[]{:S(2)}, u32[]{:S(2)}) collective-permute-start(f32[16,2,4,3,1,512]{5,2,4,3,0,1:T(4,128)} %copy.396), channel_id=1, source_target_pairs={{4,0},{8,4},{12,8},{16,12},{20,16},{24,20},{28,24},{0,28},{5,1},{9... | collective-permute-start | bytes 2359304 | tf_op jit(solution)/shard_map/ppermute | solution.py:29
  23.9 9.5 %copy-start.58 = (f32[3,3,2,512]{3,2,1,0:T(2,128)}, f32[3,3,2,512]{3,2,1,0:T(2,128)S(1)}, u32[]{:S(2)}) copy-start(f32[3,3,2,512]{3,2,1,0:T(2,128)S(1)} %get-tuple-element.1002) | copy-start | bytes 110596
  23.9 9.5 %copy-start.60 = (f32[3,3,2,512]{3,2,1,0:T(2,128)}, f32[3,3,2,512]{3,2,1,0:T(2,128)S(1)}, u32[]{:S(2)}) copy-start(f32[3,3,2,512]{3,2,1,0:T(2,128)S(1)} %get-tuple-element.1003) | copy-start | bytes 110596
  23.9 37.3 %copy-start.62 = (f32[3,3,2,512]{3,2,1,0:T(2,128)}, f32[3,3,2,512]{3,2,1,0:T(2,128)S(1)}, u32[]{:S(2)}) copy-start(f32[3,3,2,512]{3,2,1,0:T(2,128)S(1)} %get-tuple-element.1004) | copy-start | bytes 110596
  23.9 37.3 %copy-start.64 = (f32[3,3,2,512]{3,2,1,0:T(2,128)}, f32[3,3,2,512]{3,2,1,0:T(2,128)S(1)}, u32[]{:S(2)}) copy-start(f32[3,3,2,512]{3,2,1,0:T(2,128)S(1)} %get-tuple-element.1005) | copy-start | bytes 110596
  23.9 46.0 %copy-start.66 = (f32[3,3,2,512]{3,2,1,0:T(2,128)}, f32[3,3,2,512]{3,2,1,0:T(2,128)S(1)}, u32[]{:S(2)}) copy-start(f32[3,3,2,512]{3,2,1,0:T(2,128)S(1)} %get-tuple-element.1006) | copy-start | bytes 110596
  23.9 46.0 %copy-start.68 = (f32[3,3,2,512]{3,2,1,0:T(2,128)}, f32[3,3,2,512]{3,2,1,0:T(2,128)S(1)}, u32[]{:S(2)}) copy-start(f32[3,3,2,512]{3,2,1,0:T(2,128)S(1)} %get-tuple-element.1007) | copy-start | bytes 110596
  40.9 12.2 %copy-start.85 = (pred[512]{0:T(512)(128)(4,1)}, pred[512]{0:T(512)(128)(4,1)S(1)}, u32[]{:S(2)}) copy-start(pred[512]{0:T(512)(128)(4,1)S(1)} %broadcast_compare_fusion) | copy-start | bytes 1540
  46.9 11.9 %copy-start.89 = (pred[512]{0:T(512)(128)(4,1)}, pred[512]{0:T(512)(128)(4,1)S(1)}, u32[]{:S(2)}) copy-start(pred[512]{0:T(512)(128)(4,1)S(1)} %broadcast_compare_fusion.1) | copy-start | bytes 1540
  56.8 16.2 %copy-start.15 = (f32[16,4,3,2,512]{4,1,3,2,0:T(4,128)}, f32[16,4,3,2,512]{4,1,3,2,0:T(4,128)S(1)}, u32[]{:S(2)}) copy-start(f32[16,4,3,2,512]{4,1,3,2,0:T(4,128)S(1)} %copy.522) | copy-start | bytes 2359300
  57.6 15.4 %copy-start.17 = (f32[16,4,3,2,512]{4,1,3,2,0:T(4,128)}, f32[16,4,3,2,512]{4,1,3,2,0:T(4,128)S(1)}, u32[]{:S(2)}) copy-start(f32[16,4,3,2,512]{4,1,3,2,0:T(4,128)S(1)} %copy.523) | copy-start | bytes 2359300
  62.4 10.7 %copy-start.19 = (f32[16,4,3,2,512]{4,1,3,2,0:T(4,128)}, f32[16,4,3,2,512]{4,1,3,2,0:T(4,128)S(1)}, u32[]{:S(2)}) copy-start(f32[16,4,3,2,512]{4,1,3,2,0:T(4,128)S(1)} %copy.524) | copy-start | bytes 2359300
  62.9 10.2 %copy-start.21 = (f32[16,4,3,2,512]{4,1,3,2,0:T(4,128)}, f32[16,4,3,2,512]{4,1,3,2,0:T(4,128)S(1)}, u32[]{:S(2)}) copy-start(f32[16,4,3,2,512]{4,1,3,2,0:T(4,128)S(1)} %copy.525) | copy-start | bytes 2359300
  67.0 11.3 %copy-start.23 = (f32[16,4,3,2,512]{4,1,3,2,0:T(4,128)}, f32[16,4,3,2,512]{4,1,3,2,0:T(4,128)S(1)}, u32[]{:S(2)}) copy-start(f32[16,4,3,2,512]{4,1,3,2,0:T(4,128)S(1)} %copy.526) | copy-start | bytes 2359300
  67.5 10.8 %copy-start.25 = (f32[16,4,3,2,512]{4,1,3,2,0:T(4,128)}, f32[16,4,3,2,512]{4,1,3,2,0:T(4,128)S(1)}, u32[]{:S(2)}) copy-start(f32[16,4,3,2,512]{4,1,3,2,0:T(4,128)S(1)} %copy.527) | copy-start | bytes 2359300
  71.9 8.6 %copy-start.49 = (f32[6,6,2,512]{3,2,1,0:T(2,128)}, f32[6,6,2,512]{3,2,1,0:T(2,128)S(1)}, u32[]{:S(2)}) copy-start(f32[6,6,2,512]{3,2,1,0:T(2,128)S(1)} %get-tuple-element.999) | copy-start | bytes 442372
  162.2 18.1 %collective-permute-start.3 = (f32[16,2,4,3,1,512]{5,2,4,3,0,1:T(4,128)S(1)}, f32[16,2,4,3,1,512]{5,2,4,3,0,1:T(4,128)S(1)}, u32[]{:S(2)}, u32[]{:S(2)}) collective-permute-start(f32[16,2,4,3,1,512]{5,2,4,3,0,1:T(4,128)S(1)} %get-tuple-element.911), channel_id=1, source_target_pairs={{4,0},{8,4},{12,8},{16,12},{20,16},{24,20},{28,24},{0,28},{5,1},{9... | collective-permute-start | bytes 2359304 | tf_op jit(solution)/shard_map/ppermute | solution.py:29
  163.0 20.5 %collective-permute-start.4 = (f32[16,2,4,3,1,512]{5,2,4,3,0,1:T(4,128)S(1)}, f32[16,2,4,3,1,512]{5,2,4,3,0,1:T(4,128)S(1)}, u32[]{:S(2)}, u32[]{:S(2)}) collective-permute-start(f32[16,2,4,3,1,512]{5,2,4,3,0,1:T(4,128)S(1)} %get-tuple-element.912), channel_id=1, source_target_pairs={{0,4},{4,8},{8,12},{12,16},{16,20},{20,24},{24,28},{28,0},{1,5},{5... | collective-permute-start | bytes 2359304 | tf_op jit(solution)/shard_map/ppermute | solution.py:27
  201.1 25.1 %copy-start.1 = (f32[32,12,1024]{2,0,1:T(8,128)S(1)}, f32[32,12,1024]{2,0,1:T(8,128)}, u32[]{:S(2)}) copy-start(f32[32,12,1024]{2,0,1:T(8,128)} %reshape_squeeze.13) | copy-start | bytes 4718596
  232.0 10.1 %copy-start.6 = (f32[16,1,4,3,2,512]{5,2,4,3,0,1:T(4,128)S(1)}, f32[16,1,4,3,2,512]{5,2,4,3,0,1:T(4,128)}, u32[]{:S(2)}) copy-start(f32[16,1,4,3,2,512]{5,2,4,3,0,1:T(4,128)} %copy-done.5) | copy-start | bytes 2359300
  232.0 10.5 %copy-start.4 = (f32[16,1,4,3,2,512]{5,2,4,3,0,1:T(4,128)S(1)}, f32[16,1,4,3,2,512]{5,2,4,3,0,1:T(4,128)}, u32[]{:S(2)}) copy-start(f32[16,1,4,3,2,512]{5,2,4,3,0,1:T(4,128)} %copy-done.3) | copy-start | bytes 2359300
  (73 other events, 208.0 us)
Sparse Core Ops, SparseCore 0:
  232.2 70.4 all-reduce.8
where the time goes:
time: 422 us; the launch traced here: 418 us
  other arithmetic  127 us (30%)
  local copies, waits for them, and re-layouts  102 us (24%)
  waiting for transfers between devices  62.9 us (15%)
  blocking collectives  45.8 us (11%)
  matrix products  45.6 us (11%)
  between operations  30 us (7%)
  starting transfers between devices  4.33 us (1%)
    psum x1, waiting for transfers between devices, per_device(): full_re, full_im = lax.psum((proj_re, proj_im), 'ba')  57.7 us
    another operation x44, other arithmetic  30.4 us
    psum x1, blocking collectives, per_device(): gram_re, gram_im = lax.psum((gram_part_re, gram_part_im), 'ta')  23.2 us
    psum x1, blocking collectives, per_device(): over_mine_re, over_mine_im = lax.psum((part_re, part_im), 'ta')  22.6 us
    concatenate x12, other arithmetic, gamma_five(): return jnp.concatenate([spinor[:, :, :2], -spinor[:, :, 2:]], axis=2)  17.4 us
    mul x41, local copies, waits for them, and re-layouts, colour(): out_re = jnp.sum(link_re * field_re - link_im * field_im, axis=3)  15.6 us
    dot_general x6, matrix products, gamma_apply(): jnp.einsum('as,vsctx->vactx', matrix, field_im, precision=HIGHEST)  11.9 us
    dot_general x6, matrix products, gamma_apply(): jnp.einsum('as,vsctx->vactx', matrix, field_re, precision=HIGHEST)  11.6 us
  transfers between devices with their start and end apart: 6, of which 3 were waited for; matrix products, arithmetic and copies ran while one was open for 29% of the time, Pallas kernels for 0%

commit v1 on v0

v1 whole, which is shorter than its diff:
```python
import functools
import math

import jax
import jax.numpy as jnp
from jax import lax
from jax.experimental import pallas as pl
from jax.experimental.pallas import tpu as pltpu
from jax.sharding import PartitionSpec as P

HOPPING = 0.13
LANES = 128
COMPS = 12
PROJECT = (
    ((1, 1), (0, 1)),
    ((1, 0), (0, 2)),
    ((0, 1), (1, 3)),
    ((0, 2), (1, 2)),
)
REBUILD = (
    ((1, 3), (0, 3)),
    ((1, 0), (0, 2)),
    ((0, 3), (1, 1)),
    ((0, 2), (1, 2)),
)


def add_phase(left, right, phase):
    a, b = left
    c, d = right
    phase %= 4
    if phase == 0:
        return a + c, b + d
    if phase == 1:
        return a - d, b + c
    if phase == 2:
        return a - c, b - d
    return a + d, b - c


def plus(left, right):
    return left[0] + right[0], left[1] + right[1]


def minus(left, right):
    return left[0] - right[0], left[1] - right[1]


def rolled(value, shift, axis):
    shift %= value.shape[axis]
    return pltpu.roll(value, shift, axis) if shift else value


class Lattice:
    def __init__(self, slices, sites):
        self.slices = slices
        self.side = round(sites ** (1 / 3))
        self.rows = slices * sites // LANES
        self.shape = (self.rows, LANES)
        if self.side**3 != sites or LANES % (self.side * self.side) or COMPS % slices:
            raise ValueError("lattice shape")

    def masks(self):
        lane = lax.broadcasted_iota(jnp.int32, self.shape, 1)
        row = lax.broadcasted_iota(jnp.int32, self.shape, 0)
        side = self.side
        self.time = row % self.slices
        self.x_low = lane // (side * side)
        self.y = lane // side % side
        self.z = lane % side

    def shift(self, value, direction, ahead):
        side, area = self.side, self.side * self.side
        if direction == 0:
            step = 1 if ahead else -1
            edge = self.x_low == (0 if ahead else LANES // area - 1)
            mixed = jnp.where(edge, rolled(value, -step * self.slices, 0), value)
            return rolled(mixed, -step * area, 1)
        if direction < 3:
            place, unit = (self.y, side) if direction == 1 else (self.z, 1)
            edge = place == (side - 1 if ahead else 0)
            step = unit if ahead else -unit
            return jnp.where(
                edge, rolled(value, (side - 1) * step, 1), rolled(value, -step, 1)
            )
        if ahead:
            return jnp.where(self.time == self.slices - 1, 0.0, rolled(value, -1, 0))
        return jnp.where(self.time == 0, 0.0, rolled(value, 1, 0))


def load_spinor(ref, vector):
    def at(spin, colour):
        place = vector * (2 * COMPS) + spin * 3 + colour
        return ref[place], ref[place + COMPS]

    return at


def link_at(links, direction):
    def at(row, column):
        place = direction * 18 + row * 3 + column
        return links[place], links[place + 9]

    return at


def times_link(link, half):
    out = []
    for row in range(3):
        re = im = None
        for column in range(3):
            u, v = link(row, column)
            a, b = half[column]
            re = u * a - v * b if re is None else re + u * a - v * b
            im = u * b + v * a if im is None else im + u * b + v * a
        out.append((re, im))
    return out


def times_dagger(link, half):
    out = []
    for row in range(3):
        re = im = None
        for column in range(3):
            u, v = link(column, row)
            a, b = half[column]
            re = u * a + v * b if re is None else re + u * a + v * b
            im = u * b - v * a if im is None else im + u * b - v * a
        out.append((re, im))
    return out


def half_spinor(spinor, direction, spin, ahead):
    other, phase = PROJECT[direction][spin]
    phase = phase if ahead else phase + 2
    return [add_phase(spinor(spin, c), spinor(2 + other, c), phase) for c in range(3)]


def pack_rim(lattice, spinor, links, ahead_ref, behind_ref, vector):
    slices = lattice.slices
    ahead, behind = [], []
    for spin in range(2):
        ahead += half_spinor(spinor, 3, spin, True)
        behind += times_dagger(link_at(links, 3), half_spinor(spinor, 3, spin, False))
    for values, origin, ref in ((ahead, 0, ahead_ref), (behind, slices - 1, behind_ref)):
        flat = [part for pair in values for part in pair]
        for group in range(COMPS // slices):
            tile = None
            for place in range(slices):
                moved = rolled(flat[group * slices + place], place - origin, 0)
                tile = moved if tile is None else jnp.where(lattice.time == place, moved, tile)
            ref[vector * (COMPS // slices) + group] = tile


def unpack_rim(lattice, ref, vector, ahead, sign):
    slices = lattice.slices
    target = slices - 1 if ahead else 0
    flat = []
    for comp in range(COMPS):
        tile = ref[vector * (COMPS // slices) + comp // slices]
        moved = rolled(tile, target - comp % slices, 0)
        flat.append(jnp.where(lattice.time == target, moved * sign, 0.0))
    return [(flat[2 * i], flat[2 * i + 1]) for i in range(COMPS // 2)]


def pack_kernel(lattice, vectors, psi, links, ahead_ref, behind_ref):
    lattice.masks()

    def body(vector, carry):
        pack_rim(lattice, load_spinor(psi, vector), links, ahead_ref, behind_ref, vector)
        return carry

    lax.fori_loop(0, vectors, body, 0)


def local_kernel(lattice, vectors, psi, links, clover, out):
    lattice.masks()

    def body(vector, carry):
        spinor = load_spinor(psi, vector)
        upper = [[None] * 3 for _ in range(2)]
        lower = [[None] * 3 for _ in range(2)]
        for direction in range(4):
            link = link_at(links, direction)
            for spin in range(2):
                half = half_spinor(spinor, direction, spin, True)
                half = [tuple(lattice.shift(p, direction, True) for p in h) for h in half]
                ahead = times_link(link, half)
                half = half_spinor(spinor, direction, spin, False)
                behind = times_dagger(link, half)
                behind = [tuple(lattice.shift(p, direction, False) for p in h) for h in behind]
                place, phase = REBUILD[direction][spin]
                for c in range(3):
                    total, diff = plus(ahead[c], behind[c]), minus(ahead[c], behind[c])
                    if upper[spin][c] is None:
                        upper[spin][c] = total
                    else:
                        upper[spin][c] = plus(upper[spin][c], total)
                    if lower[place][c] is None:
                        zero = jnp.zeros_like(diff[0])
                        lower[place][c] = add_phase((zero, zero), diff, phase)
                    else:
                        lower[place][c] = add_phase(lower[place][c], diff, phase)
        for chiral, hops in ((0, upper), (1, lower)):
            for row in range(6):
                re = im = None
                for column in range(6):
                    place = chiral * 72 + row * 6 + column
                    u, v = clover[place], clover[place + 36]
                    a, b = spinor(2 * chiral + column // 3, column % 3)
                    re = u * a - v * b if re is None else re + u * a - v * b
                    im = u * b + v * a if im is None else im + u * b + v * a
                place = vector * (2 * COMPS) + chiral * 6 + row
                out[place] = re - HOPPING * hops[row // 3][row % 3][0]
                out[place + COMPS] = im - HOPPING * hops[row // 3][row % 3][1]
        return carry

    lax.fori_loop(0, vectors, body, 0)


def rim_signs():
    count, here = lax.axis_size("ta"), lax.axis_index("ta")
    one = jnp.float32(1.0)
    return jnp.where(here == count - 1, -one, one), jnp.where(here == 0, -one, one)


def finish(lattice, links, part, rim_ahead, rim_behind, vector, signs, store):
    ahead_all = unpack_rim(lattice, rim_ahead, vector, True, signs[0])
    behind_all = unpack_rim(lattice, rim_behind, vector, False, signs[1])
    for spin in range(2):
        ahead = times_link(link_at(links, 3), ahead_all[3 * spin : 3 * spin + 3])
        behind = behind_all[3 * spin : 3 * spin + 3]
        for c in range(3):
            for ri in range(2):
                f, b = ahead[c][ri], behind[c][ri]
                place = vector * (2 * COMPS) + ri * COMPS + spin * 3 + c
                store(place, part[place] - HOPPING * (f + b))
                store(place + 6, -(part[place + 6] + HOPPING * (f - b)))


def middle_kernel(
    lattice, vectors, part, links, rim_ahead, rim_behind, out, ahead_ref, behind_ref
):
    lattice.masks()
    signs = rim_signs()

    def body(vector, carry):
        values = {}

        def store(place, value):
            out[place] = value

        finish(lattice, links, part, rim_ahead, rim_behind, vector, signs, store)
        pack_rim(lattice, load_spinor(out, vector), links, ahead_ref, behind_ref, vector)
        return carry

    lax.fori_loop(0, vectors, body, 0)


def two_halves(value):
    high = value.astype(jnp.bfloat16)
    return high, (value - high.astype(jnp.float32)).astype(jnp.bfloat16)


def basis_kernel(groups, kept, blocks, basis, out):
    per = blocks // groups

    def body(block, carry):
        rows = jnp.concatenate(
            [
                basis[pl.ds(block, kept, stride=2 * blocks), :],
                basis[pl.ds(blocks + block, kept, stride=2 * blocks), :],
            ],
            axis=0,
        )
        high, low = two_halves(rows)
        lanes = pl.ds(pl.multiple_of(block % per * LANES, LANES), LANES)
        out[block // per, : 2 * kept, lanes] = high
        out[block // per, 2 * kept :, lanes] = low
        return carry

    lax.fori_loop(0, blocks, body, 0, unroll=2)


def correlate_kernel(
    lattice, groups, vectors, kept, blocks, scale,
    part, links, rim_ahead, rim_behind, basis, applied, over, field,
):
    lattice.masks()
    signs = rim_signs()
    rows = lattice.rows

    def body(vector, carry):
        def store(place, value):
            start = place * rows
            field[pl.ds(start if isinstance(start, int) else pl.multiple_of(start, rows), rows), :] = value

        finish(lattice, links, part, rim_ahead, rim_behind, vector, signs, store)
        return carry

    lax.fori_loop(0, vectors, body, 0)
    per = blocks // groups

    def relay(block, carry):
        lanes = pl.ds(pl.multiple_of(block % per * LANES, LANES), LANES)
        for ri in range(2):
            start = ri * blocks + block
            applied[block // per, ri * vectors : (ri + 1) * vectors, lanes] = field[
                pl.ds(start, vectors, stride=2 * blocks), :
            ]
        return carry

    lax.fori_loop(0, blocks, relay, 0, unroll=2)
    total = None
    for group in range(groups):
        both = jnp.concatenate(two_halves(applied[group]), axis=0)
        term = lax.dot_general(
            both, basis[group], (((1,), (1,)), ((), ())), preferred_element_type=jnp.float32
        )
        total = term if total is None else total + term
    total = total[: 2 * vectors] + total[2 * vectors :]
    total = total[:, : 2 * kept] + total[:, 2 * kept :]
    real, imag = total[:vectors], total[vectors:]
    over[:vectors, :] = scale * (real[:, :kept] + imag[:, kept:])
    over[vectors:, :] = scale * (imag[:, :kept] - real[:, kept:])


def partner(here, step, count):
    if count & (count - 1) == 0:
        return here ^ step
    return (here + step) % count


def source(here, step, count):
    if count & (count - 1) == 0:
        return here ^ step
    return (here + count - step) % count


def exchanged(values, axis):
    count = lax.axis_size(axis)
    out = [values[0]]
    for step in range(1, count):
        pairs = [(i, partner(i, step, count)) for i in range(count)]
        out.append(lax.ppermute(values[step], axis, pairs))
    return out


def summed(value, axis):
    count = lax.axis_size(axis)
    if count & (count - 1):
        return lax.psum(value, axis)
    step = 1
    while step < count:
        value = value + lax.ppermute(value, axis, [(i, i ^ step) for i in range(count)])
        step *= 2
    return value


def project_kernel(groups, vectors, kept, over, basis, *outs):
    here = lax.axis_index("ba")
    real, imag = over[:vectors, :], over[vectors:, :]
    weight = jnp.concatenate(
        [
            jnp.concatenate([real, -imag], axis=1),
            jnp.concatenate([imag, real], axis=1),
        ],
        axis=0,
    )
    high, low = two_halves(weight)
    weight = jnp.concatenate(
        [jnp.concatenate([high, high], axis=1), jnp.concatenate([low, low], axis=1)], axis=0
    )
    for step in range(groups):
        both = jnp.dot(
            weight, basis[partner(here, step, groups)], preferred_element_type=jnp.float32
        )
        outs[step][...] = both[: 2 * vectors] + both[2 * vectors :]


def rest_kernel(groups, vectors, scale, applied, *refs):
    parts, (rest_ref, gram) = refs[:groups], refs[groups:]
    here = lax.axis_index("ba")
    rest = applied[here]
    total = parts[0][...]
    for part in parts[1:]:
        total = total + part[...]
    rest = rest - total
    rest_ref[...] = rest
    both = jnp.concatenate(two_halves(rest), axis=0)
    full = lax.dot_general(
        both, both, (((1,), (1,)), ((), ())), preferred_element_type=jnp.float32
    )
    full = full[: 2 * vectors] + full[2 * vectors :]
    full = full[:, : 2 * vectors] + full[:, 2 * vectors :]
    real, imag = full[:vectors], full[vectors:]
    gram[:, :vectors] = scale * (real[:, :vectors] + imag[:, vectors:])
    gram[:, vectors:] = scale * (real[:, vectors:] - imag[:, :vectors])


def ortho_kernel(groups, vectors, gram, rest, *outs):
    here = lax.axis_index("ba")
    work = outs[-1]
    outs = outs[:-1]
    shape = (vectors, 2 * vectors)
    row = lax.broadcasted_iota(jnp.int32, shape, 0)
    lane = lax.broadcasted_iota(jnp.int32, shape, 1)
    unit = jnp.where(lane == row + vectors, 1.0, 0.0)
    re = jnp.where(lane < vectors, gram[...], unit)
    im = jnp.where(lane < vectors, pltpu.roll(gram[...], vectors, 1), 0.0) if False else None
    im = jnp.concatenate([gram[:, vectors:], jnp.zeros((vectors, vectors), jnp.float32)], axis=1)
    for pivot in range(vectors):
        scale = 1.0 / jnp.sqrt(re[pivot : pivot + 1, pivot : pivot + 1])
        row_re, row_im = re[pivot : pivot + 1] * scale, im[pivot : pivot + 1] * scale
        col_re, col_im = re[:, pivot : pivot + 1] * scale, im[:, pivot : pivot + 1] * scale
        below = row > pivot
        new_re = re - (col_re * row_re - col_im * row_im)
        new_im = im - (col_re * row_im + col_im * row_re)
        re = jnp.where(below, new_re, jnp.where(row == pivot, row_re, re))
        im = jnp.where(below, new_im, jnp.where(row == pivot, row_im, im))
    inv_re, inv_im = re[:, vectors:], im[:, vectors:]
    weight = jnp.concatenate(
        [
            jnp.concatenate([inv_re, inv_im], axis=1),
            jnp.concatenate([-inv_im, inv_re], axis=1),
        ],
        axis=0,
    )
    high, low = two_halves(weight)
    weight = jnp.concatenate(
        [jnp.concatenate([high, high], axis=1), jnp.concatenate([low, low], axis=1)], axis=0
    )
    both = jnp.concatenate(two_halves(rest[...]), axis=0)
    full = jnp.dot(weight, both, preferred_element_type=jnp.float32)
    full = full[: 2 * vectors] + full[2 * vectors :]
    own = vectors // groups
    for group in range(groups):
        for ri in range(2):
            start = ri * vectors + group * own
            work[group, ri * own : (ri + 1) * own, :] = full[start : start + own]
    for step in range(groups):
        outs[step][...] = work[partner(here, step, groups)]


def place_kernel(groups, own, blocks, *refs):
    parts, out = refs[:groups], refs[groups]
    here = lax.axis_index("ba")
    per = blocks // groups
    for step in range(groups):
        first = source(here, step, groups) * per
        for block in range(per):
            for ri in range(2):
                value = parts[step][ri * own : (ri + 1) * own, block * LANES : (block + 1) * LANES]
                out[pl.ds(first + block + ri * blocks, own, stride=2 * blocks), :] = value


def call(kernel, outs, *args, scratch=(), flops=0):
    nbytes = sum(a.size * a.dtype.itemsize for a in (*args, *outs))
    spec = pl.BlockSpec(memory_space=pltpu.VMEM)
    return pl.pallas_call(
        kernel,
        out_shape=tuple(outs),
        in_specs=[spec] * len(args),
        out_specs=tuple([spec] * len(outs)),
        scratch_shapes=list(scratch),
        compiler_params=pltpu.CompilerParams(vmem_limit_bytes=40 * 1024 * 1024),
        cost_estimate=pl.CostEstimate(flops=flops, bytes_accessed=nbytes, transcendentals=0),
    )(*args)


def shape_of(*dims):
    return jax.ShapeDtypeStruct(dims, jnp.float32)


def tiles_of(value, leading):
    slices, sites = value.shape[-2:]
    value = value.reshape(leading, slices, sites // LANES, LANES)
    return value.swapaxes(1, 2).reshape(leading, slices * sites // LANES, LANES)


def per_device(search_block, kept_basis, gauge_links, clover_term):
    vectors, kept = search_block.shape[0], kept_basis.shape[0]
    slices, sites = search_block.shape[-2:]
    groups, places = lax.axis_size("ba"), lax.axis_size("ta")
    lattice = Lattice(slices, sites)
    rows = lattice.rows
    blocks = COMPS * rows
    per = blocks // groups
    own = vectors // groups
    scale = 1.0 / (2 * COMPS * slices * sites * places)
    psi = tiles_of(search_block, vectors * 2 * COMPS)
    basis = tiles_of(kept_basis, kept * 2 * COMPS).reshape(kept * 2 * blocks, LANES)
    links = tiles_of(gauge_links, 72)
    clover = tiles_of(clover_term, 144)
    rim = shape_of(vectors * COMPS // slices, rows, LANES)
    field = shape_of(vectors * 2 * COMPS, rows, LANES)
    work = vectors * rows * LANES

    def swap(ahead, behind):
        down = [(i, (i + places - 1) % places) for i in range(places)]
        up = [(i, (i + 1) % places) for i in range(places)]
        return lax.ppermute(ahead, "ta", down), lax.ppermute(behind, "ta", up)

    ahead, behind = call(
        functools.partial(pack_kernel, lattice, vectors), (rim, rim), psi, links, flops=200 * work
    )
    rims = swap(ahead, behind)
    local = functools.partial(local_kernel, lattice, vectors)
    (part,) = call(local, (field,), psi, links, clover, flops=2000 * work)
    (rows_of_basis,) = call(
        functools.partial(basis_kernel, groups, kept, blocks),
        (jax.ShapeDtypeStruct((groups, 4 * kept, per * LANES), jnp.bfloat16),),
        basis,
    )
    first, ahead, behind = call(
        functools.partial(middle_kernel, lattice, vectors),
        (field, rim, rim),
        part,
        links,
        *rims,
        flops=400 * work,
    )
    rims = swap(ahead, behind)
    (part,) = call(local, (field,), first, links, clover, flops=2000 * work)
    applied, over = call(
        functools.partial(correlate_kernel, lattice, groups, vectors, kept, blocks, scale),
        (shape_of(groups, 2 * vectors, per * LANES), shape_of(2 * vectors, kept)),
        part,
        links,
        *rims,
        rows_of_basis,
        scratch=[pltpu.VMEM((vectors * 2 * blocks, LANES), jnp.float32)],
        flops=400 * work,
    )
    over = summed(over, "ta")
    quarter = shape_of(2 * vectors, per * LANES)
    parts = call(
        functools.partial(project_kernel, groups, vectors, kept),
        (quarter,) * groups,
        over,
        rows_of_basis,
    )
    parts = exchanged(parts, "ba")
    rest, gram = call(
        functools.partial(rest_kernel, groups, vectors, scale),
        (quarter, shape_of(vectors, 2 * vectors)),
        applied,
        *parts,
    )
    gram = summed(summed(gram, "ta"), "ba")
    piece = shape_of(2 * own, per * LANES)
    pieces = call(
        functools.partial(ortho_kernel, groups, vectors),
        (piece,) * groups,
        gram,
        rest,
        scratch=[pltpu.VMEM((groups, 2 * own, per * LANES), jnp.float32)],
    )
    pieces = exchanged(pieces, "ba")
    (ortho,) = call(
        functools.partial(place_kernel, groups, own, blocks),
        (shape_of(own * 2 * blocks, LANES),),
        *pieces,
    )
    ortho = ortho.reshape(own * 2 * COMPS, sites // LANES, slices, LANES).swapaxes(1, 2)
    ortho = ortho.reshape(own, *search_block.shape[1:])
    return ortho, over.reshape(2, vectors, kept).swapaxes(1, 2)


def solution(mesh):
    placed = (
        P(None, None, None, None, "ta", None),
        P("ba", None, None, None, "ta", None),
        P(None, None, None, None, "ta", None),
        P(None, None, None, None, "ta", None),
    )
    return jax.shard_map(
        per_device,
        mesh=mesh,
        in_specs=placed,
        out_specs=(P("ba", None, None, None, "ta", None), P(None, "ba", None)),
        check_vma=False,
    )
```

time: 422 us -> 108 us (0.26)
  other arithmetic: 127 us -> 0.03 us
  local copies, waits for them, and re-layouts: 102 us -> 2.38 us
  blocking collectives: 45.8 us -> 0 us
  matrix products: 45.6 us -> 0 us
  between operations: 30 us -> 0.74 us
  Pallas kernels: 0 us -> 21.9 us
  starting transfers between devices: 4.33 us -> 24 us
  waiting for transfers between devices: 62.9 us -> 58.5 us
    psum x1 -> x0, waiting for transfers between devices: 57.7 us -> none  [per_device(): full_re, full_im = lax.psum((proj_re, proj_im), 'ba')]
    ppermute x5 -> x18, waiting for transfers between devices: 5.23 us -> 58.5 us  [the longest x6 32.1 us: exchanged(): out.append(lax.ppermute(values[step], axis, pairs))]
    psum x2 -> x0, blocking collectives: 45.8 us -> none  [the longest x1 23.2 us: per_device(): gram_re, gram_im = lax.psum((gram_part_re, gram_part_im), 'ta')]
    dot_general x28 -> x0, matrix products: 45.6 us -> none  [the longest x6 11.9 us: gamma_apply(): jnp.einsum('as,vsctx->vactx', matrix, field_im, precision=HIGHEST)]
    slice x47 -> x0, local copies, waits for them, and re-layouts: 38.8 us -> none  [the longest x16 9.34 us: cholesky_complex(): pivot_value = jnp.sqrt(acc_re[column])]
    another operation x46 -> x0, other arithmetic: 31.2 us -> none
    pallas_call x0 -> x10, Pallas kernels: none -> 21.9 us  [call(): pl.pallas_call(kernel, out_shape=tuple(outs), in_specs=[spec] * len(args)...]
    div x31 -> x0, other arithmetic: 20 us -> none  [the longest x16 10.6 us: invert_lower(): inverse_re = inverse_re.at[row_index].set((unit_row - sum_re) / pivot_value)]
  transfers between devices with their start and end apart: 6 -> 18, of which waited for: 3 -> 16; matrix products, arithmetic and copies ran while one was open for 29% -> 0% of each run, Pallas kernels for 0% -> 12%
where the time goes in v1:
time: 108 us
  waiting for transfers between devices  58.5 us (54%)
  starting transfers between devices  24 us (22%)
  Pallas kernels  21.9 us (20%)
  local copies, waits for them, and re-layouts  2.38 us (2%)
    ppermute x6, waiting for transfers between devices, exchanged(): out.append(lax.ppermute(values[step], axis, pairs))  32.1 us
    pallas_call x10, Pallas kernels, call(): pl.pallas_call(kernel, out_shape=tuple(outs), in_specs=[spec] * len(args)...  21.9 us
    ppermute x8, waiting for transfers between devices, summed(): lax.ppermute(value, axis, [(i, i ^ step) for i in range(count)])  18.4 us
    ppermute x8, starting transfers between devices, summed(): lax.ppermute(value, axis, [(i, i ^ step) for i in range(count)])  10.7 us
    ppermute x6, starting transfers between devices, exchanged(): out.append(lax.ppermute(values[step], axis, pairs))  8.91 us
    ppermute x4, waiting for transfers between devices, swap(): return (lax.ppermute(ahead, 'ta', down), lax.ppermute(behind, 'ta', up))  8.1 us
    ppermute x4, starting transfers between devices, swap(): return (lax.ppermute(ahead, 'ta', down), lax.ppermute(behind, 'ta', up))  4.36 us
    unnamed x12, local copies, waits for them, and re-layouts  2.38 us
  transfers between devices with their start and end apart: 18, of which 16 were waited for; matrix products, arithmetic and copies ran while one was open for 0% of the time, Pallas kernels for 12%

profile of v1, /device:TPU:0, one launch (start us, length us, event | category | flops | bytes accessed | tf_op | source)
XLA Modules:
  0.0 107.6 jit_solution(13842381748263662170)
XLA Ops:
  1.6 1.4 %copy-done.2 = f32[16,2,4,3,2,512]{5,4,3,2,1,0:T(2,128)S(1)} copy-done((f32[16,2,4,3,2,512]{5,4,3,2,1,0:T(2,128)S(1)}, f32[16,2,4,3,2,512]{5,4,3,2,1,0:T(2,128)}, u32[]{:S(2)}) %copy-start.2) | copy-done | bytes 1572888
  3.5 3.4 %collective-permute-start = (f32[96,8,128]{2,1,0:T(8,128)S(1)}, f32[96,8,128]{2,1,0:T(8,128)S(1)}, u32[]{:S(2)}, u32[]{:S(2)}) collective-permute-start(f32[96,8,128]{2,1,0:T(8,128)S(1)} %get-tuple-element.19), channel_id=1, source_target_pairs={{0,28},{4,0},{8,4},{12,8},{16,12},{20,16},{24,20},{28,24},{1,29},{... | collective-permute-start | bytes 1179656 | tf_op jit(solution)/shard_map/ppermute | solution.py:502
  6.9 4.9 %shard_map.59.part = f32[384,8,128]{2,1,0:T(8,128)S(1)} custom-call(f32[384,8,128]{2,1,0:T(8,128)S(1)} %bitcast.34, f32[72,8,128]{2,1,0:T(8,128)S(1)} %bitcast.29, f32[144,8,128]{2,1,0:T(8,128)S(1)} %bitcast.36), custom_call_target="tpu_custom_call" | custom-call | flops 32768000 | bytes 4030464 | tf_op jit(solution)/shard_map/pallas_call | solution.py:460
  11.8 3.7 %collective-permute-done.rim_ahead = f32[96,8,128]{2,1,0:T(8,128)S(1)} collective-permute-done((f32[96,8,128]{2,1,0:T(8,128)S(1)}, f32[96,8,128]{2,1,0:T(8,128)S(1)}, u32[]{:S(2)}, u32[]{:S(2)}) %collective-permute-start) | collective-permute-done | bytes 393248 | tf_op jit(solution)/shard_map/ppermute | solution.py:502
  15.5 1.9 %collective-permute-done.1.rim_behind = f32[96,8,128]{2,1,0:T(8,128)S(1)} collective-permute-done((f32[96,8,128]{2,1,0:T(8,128)S(1)}, f32[96,8,128]{2,1,0:T(8,128)S(1)}, u32[]{:S(2)}, u32[]{:S(2)}) %collective-permute-start.1) | collective-permute-done | bytes 393248 | tf_op jit(solution)/shard_map/ppermute | solution.py:502
  19.4 3.0 %shard_map.63.basis = bf16[4,128,3072]{2,1,0:T(8,128)(2,1)S(1)} custom-call(f32[6144,128]{1,0:T(8,128)S(1)} %bitcast.35), custom_call_target="tpu_custom_call" | custom-call | bytes 6291456 | tf_op jit(solution)/shard_map/pallas_call | solution.py:460
  22.5 4.9 %shard_map.62.part = f32[384,8,128]{2,1,0:T(8,128)S(1)} custom-call(f32[384,8,128]{2,1,0:T(8,128)S(1)} %get-tuple-element.21.psi, f32[72,8,128]{2,1,0:T(8,128)S(1)} %bitcast.31, f32[144,8,128]{2,1,0:T(8,128)S(1)} %bitcast.37), custom_call_target="tpu_custom_call" | custom-call | flops 32768000 | bytes 4030464 | tf_op jit(solution)/shard_map/pallas_call | solution.py:460
  27.9 2.0 %collective-permute-done.3.rim_behind = f32[96,8,128]{2,1,0:T(8,128)S(1)} collective-permute-done((f32[96,8,128]{2,1,0:T(8,128)S(1)}, f32[96,8,128]{2,1,0:T(8,128)S(1)}, u32[]{:S(2)}, u32[]{:S(2)}) %collective-permute-start.3) | collective-permute-done | bytes 393248 | tf_op jit(solution)/shard_map/ppermute | solution.py:502
  29.9 3.5 %shard_map.64 = (f32[4,32,3072]{2,1,0:T(8,128)S(1)}, f32[32,32]{1,0:T(8,128)S(1)}) custom-call(f32[384,8,128]{2,1,0:T(8,128)S(1)} %shard_map.62.part, f32[72,8,128]{2,1,0:T(8,128)S(1)} %bitcast.32, f32[96,8,128]{2,1,0:T(8,128)S(1)} %collective-permute-done.2.rim_ahead, f32[96,8,128]{2,1,0:T(8,128)S(1)} %collective-permute-done.3.rim_behind, ...), custom_call_target="tpu_custom_call" | custom-call | flops 6553600 | bytes 7376896 | tf_op jit(solution)/shard_map/pallas_call | solution.py:460
  35.7 2.7 %collective-permute-done.5 = f32[32,32]{1,0:T(8,128)S(1)} collective-permute-done((f32[32,32]{1,0:T(8,128)S(1)}, f32[32,32]{1,0:T(8,128)S(1)}, u32[]{:S(2)}, u32[]{:S(2)}) %collective-permute-start.5) | collective-permute-done | bytes 4128 | tf_op jit(solution)/shard_map/ppermute | solution.py:355
  38.4 3.7 %collective-permute-done.6 = f32[32,32]{1,0:T(8,128)S(1)} collective-permute-done((f32[32,32]{1,0:T(8,128)S(1)}, f32[32,32]{1,0:T(8,128)S(1)}, u32[]{:S(2)}, u32[]{:S(2)}) %collective-permute-start.6) | collective-permute-done | bytes 4128 | tf_op jit(solution)/shard_map/ppermute | solution.py:355
  42.8 1.6 %collective-permute-start.7 = (f32[32,3072]{1,0:T(8,128)S(1)}, f32[32,3072]{1,0:T(8,128)S(1)}, u32[]{:S(2)}, u32[]{:S(2)}) collective-permute-start(f32[32,3072]{1,0:T(8,128)S(1)} %get-tuple-element.27), channel_id=1, source_target_pairs={{0,1},{1,0},{2,3},{3,2},{4,5},{5,4},{6,7},{7,6},{8,9},{9,8},{10,11... | collective-permute-start | bytes 1179656 | tf_op jit(solution)/shard_map/ppermute | solution.py:345
  44.5 2.6 %collective-permute-start.8 = (f32[32,3072]{1,0:T(8,128)S(1)}, f32[32,3072]{1,0:T(8,128)S(1)}, u32[]{:S(2)}, u32[]{:S(2)}) collective-permute-start(f32[32,3072]{1,0:T(8,128)S(1)} %get-tuple-element.28), channel_id=1, source_target_pairs={{0,2},{1,3},{2,0},{3,1},{4,6},{5,7},{6,4},{7,5},{8,10},{9,11},{10,... | collective-permute-start | bytes 1179656 | tf_op jit(solution)/shard_map/ppermute | solution.py:345
  47.3 11.2 %collective-permute-done.7.refs_1_ = f32[32,3072]{1,0:T(8,128)S(1)} collective-permute-done((f32[32,3072]{1,0:T(8,128)S(1)}, f32[32,3072]{1,0:T(8,128)S(1)}, u32[]{:S(2)}, u32[]{:S(2)}) %collective-permute-start.7) | collective-permute-done | bytes 393248 | tf_op jit(solution)/shard_map/ppermute | solution.py:345
  58.5 15.7 %collective-permute-done.8.refs_2_ = f32[32,3072]{1,0:T(8,128)S(1)} collective-permute-done((f32[32,3072]{1,0:T(8,128)S(1)}, f32[32,3072]{1,0:T(8,128)S(1)}, u32[]{:S(2)}, u32[]{:S(2)}) %collective-permute-start.8) | collective-permute-done | bytes 393248 | tf_op jit(solution)/shard_map/ppermute | solution.py:345
  76.8 2.7 %collective-permute-done.11 = f32[16,32]{1,0:T(8,128)S(1)} collective-permute-done((f32[16,32]{1,0:T(8,128)S(1)}, f32[16,32]{1,0:T(8,128)S(1)}, u32[]{:S(2)}, u32[]{:S(2)}) %collective-permute-start.11) | collective-permute-done | bytes 2080 | tf_op jit(solution)/shard_map/ppermute | solution.py:355
  79.5 3.6 %collective-permute-done.12 = f32[16,32]{1,0:T(8,128)S(1)} collective-permute-done((f32[16,32]{1,0:T(8,128)S(1)}, f32[16,32]{1,0:T(8,128)S(1)}, u32[]{:S(2)}, u32[]{:S(2)}) %collective-permute-start.12) | collective-permute-done | bytes 2080 | tf_op jit(solution)/shard_map/ppermute | solution.py:355
  83.2 5.6 %collective-permute-start.13 = (f32[16,32]{1,0:T(8,128)S(1)}, f32[16,32]{1,0:T(8,128)S(1)}, u32[]{:S(2)}, u32[]{:S(2)}) collective-permute-start(f32[16,32]{1,0:T(8,128)S(1)} %add.29), channel_id=1, source_target_pairs={{0,1},{1,0},{2,3},{3,2},{4,5},{5,4},{6,7},{7,6},{8,9},{9,8},{10,11... | collective-permute-start | bytes 6152 | tf_op jit(solution)/shard_map/ppermute | solution.py:355
  88.8 1.6 %collective-permute-done.13 = f32[16,32]{1,0:T(8,128)S(1)} collective-permute-done((f32[16,32]{1,0:T(8,128)S(1)}, f32[16,32]{1,0:T(8,128)S(1)}, u32[]{:S(2)}, u32[]{:S(2)}) %collective-permute-start.13) | collective-permute-done | bytes 2080 | tf_op jit(solution)/shard_map/ppermute | solution.py:355
  90.4 3.0 %collective-permute-start.14 = (f32[16,32]{1,0:T(8,128)S(1)}, f32[16,32]{1,0:T(8,128)S(1)}, u32[]{:S(2)}, u32[]{:S(2)}) collective-permute-start(f32[16,32]{1,0:T(8,128)S(1)} %add.30), channel_id=1, source_target_pairs={{0,2},{1,3},{2,0},{3,1},{4,6},{5,7},{6,4},{7,5},{8,10},{9,11},{10,... | collective-permute-start | bytes 6152 | tf_op jit(solution)/shard_map/ppermute | solution.py:355
  93.5 1.6 %collective-permute-done.14 = f32[16,32]{1,0:T(8,128)S(1)} collective-permute-done((f32[16,32]{1,0:T(8,128)S(1)}, f32[16,32]{1,0:T(8,128)S(1)}, u32[]{:S(2)}, u32[]{:S(2)}) %collective-permute-start.14) | collective-permute-done | bytes 2080 | tf_op jit(solution)/shard_map/ppermute | solution.py:355
  95.1 1.9 %shard_map.67 = (f32[8,3072]{1,0:T(8,128)S(1)}, f32[8,3072]{1,0:T(8,128)S(1)}, f32[8,3072]{1,0:T(8,128)S(1)}, f32[8,3072]{1,0:T(8,128)S(1)}) custom-call(f32[16,32]{1,0:T(8,128)S(1)} %add.31.gram, f32[32,3072]{1,0:T(8,128)S(1)} %get-tuple-element.31.rest), custom_call_target="tpu_custom_call" | custom-call | bytes 788480 | tf_op jit(solution)/shard_map/pallas_call | solution.py:460
  97.0 2.0 %collective-permute-start.15 = (f32[8,3072]{1,0:T(8,128)S(1)}, f32[8,3072]{1,0:T(8,128)S(1)}, u32[]{:S(2)}, u32[]{:S(2)}) collective-permute-start(f32[8,3072]{1,0:T(8,128)S(1)} %get-tuple-element.33), channel_id=1, source_target_pairs={{0,1},{1,0},{2,3},{3,2},{4,5},{5,4},{6,7},{7,6},{8,9},{9,8},{10,11... | collective-permute-start | bytes 294920 | tf_op jit(solution)/shard_map/ppermute | solution.py:345
  102.0 4.6 %collective-permute-done.16.refs_2_ = f32[8,3072]{1,0:T(8,128)S(1)} collective-permute-done((f32[8,3072]{1,0:T(8,128)S(1)}, f32[8,3072]{1,0:T(8,128)S(1)}, u32[]{:S(2)}, u32[]{:S(2)}) %collective-permute-start.16) | collective-permute-done | bytes 98336 | tf_op jit(solution)/shard_map/ppermute | solution.py:345
  (42 shorter events, 13.6 us)
Async XLA Ops:
  0.6 1.0 copy-start
  1.6 1.4 %copy-start.2 = (f32[16,2,4,3,2,512]{5,4,3,2,1,0:T(2,128)S(1)}, f32[16,2,4,3,2,512]{5,4,3,2,1,0:T(2,128)}, u32[]{:S(2)}) copy-start(f32[16,2,4,3,2,512]{5,4,3,2,1,0:T(2,128)} %param.4) | copy-start | bytes 4718596
  3.0 3.9 %copy-start.4 = (f32[2,2,6,6,2,512]{5,4,3,2,1,0:T(2,128)S(1)}, f32[2,2,6,6,2,512]{5,4,3,2,1,0:T(2,128)}, u32[]{:S(2)}) copy-start(f32[2,2,6,6,2,512]{5,4,3,2,1,0:T(2,128)} %param.7) | copy-start | bytes 1769476
  3.5 12.0 %collective-permute-start = (f32[96,8,128]{2,1,0:T(8,128)S(1)}, f32[96,8,128]{2,1,0:T(8,128)S(1)}, u32[]{:S(2)}, u32[]{:S(2)}) collective-permute-start(f32[96,8,128]{2,1,0:T(8,128)S(1)} %get-tuple-element.19), channel_id=1, source_target_pairs={{0,28},{4,0},{8,4},{12,8},{16,12},{20,16},{24,20},{28,24},{1,29},{... | collective-permute-start | bytes 1179656 | tf_op jit(solution)/shard_map/ppermute | solution.py:502
  6.9 10.5 %collective-permute-start.1 = (f32[96,8,128]{2,1,0:T(8,128)S(1)}, f32[96,8,128]{2,1,0:T(8,128)S(1)}, u32[]{:S(2)}, u32[]{:S(2)}) collective-permute-start(f32[96,8,128]{2,1,0:T(8,128)S(1)} %get-tuple-element.20), channel_id=1, source_target_pairs={{0,4},{4,8},{8,12},{12,16},{16,20},{20,24},{24,28},{28,0},{1,5},{5... | collective-permute-start | bytes 1179656 | tf_op jit(solution)/shard_map/ppermute | solution.py:502
  6.9 10.5 %copy-start.1 = (f32[4,2,3,3,2,512]{5,4,3,2,1,0:T(2,128)S(1)}, f32[4,2,3,3,2,512]{5,4,3,2,1,0:T(2,128)}, u32[]{:S(2)}) copy-start(f32[4,2,3,3,2,512]{5,4,3,2,1,0:T(2,128)} %param.6) | copy-start | bytes 884740
  6.9 12.5 %copy-start.3 = (f32[32,2,4,3,2,512]{5,4,3,2,1,0:T(2,128)S(1)}, f32[32,2,4,3,2,512]{5,4,3,2,1,0:T(2,128)}, u32[]{:S(2)}) copy-start(f32[32,2,4,3,2,512]{5,4,3,2,1,0:T(2,128)} %param.5) | copy-start | bytes 9437188
  18.5 9.4 %collective-permute-start.2 = (f32[96,8,128]{2,1,0:T(8,128)S(1)}, f32[96,8,128]{2,1,0:T(8,128)S(1)}, u32[]{:S(2)}, u32[]{:S(2)}) collective-permute-start(f32[96,8,128]{2,1,0:T(8,128)S(1)} %get-tuple-element.22), channel_id=1, source_target_pairs={{0,28},{4,0},{8,4},{12,8},{16,12},{20,16},{24,20},{28,24},{1,29},{... | collective-permute-start | bytes 1179656 | tf_op jit(solution)/shard_map/ppermute | solution.py:502
  19.4 10.5 %collective-permute-start.3 = (f32[96,8,128]{2,1,0:T(8,128)S(1)}, f32[96,8,128]{2,1,0:T(8,128)S(1)}, u32[]{:S(2)}, u32[]{:S(2)}) collective-permute-start(f32[96,8,128]{2,1,0:T(8,128)S(1)} %get-tuple-element.23), channel_id=1, source_target_pairs={{0,4},{4,8},{8,12},{12,16},{16,20},{20,24},{24,28},{28,0},{1,5},{5... | collective-permute-start | bytes 1179656 | tf_op jit(solution)/shard_map/ppermute | solution.py:502
  33.4 1.2 %collective-permute-start.4 = (f32[32,32]{1,0:T(8,128)S(1)}, f32[32,32]{1,0:T(8,128)S(1)}, u32[]{:S(2)}, u32[]{:S(2)}) collective-permute-start(f32[32,32]{1,0:T(8,128)S(1)} %get-tuple-element.25), channel_id=1, source_target_pairs={{0,4},{4,0},{8,12},{12,8},{16,20},{20,16},{24,28},{28,24},{1,5},{5... | collective-permute-start | bytes 12296 | tf_op jit(solution)/shard_map/ppermute | solution.py:355
  34.7 3.7 %collective-permute-start.5 = (f32[32,32]{1,0:T(8,128)S(1)}, f32[32,32]{1,0:T(8,128)S(1)}, u32[]{:S(2)}, u32[]{:S(2)}) collective-permute-start(f32[32,32]{1,0:T(8,128)S(1)} %add.24), channel_id=1, source_target_pairs={{0,8},{4,12},{8,0},{12,4},{16,24},{20,28},{24,16},{28,20},{1,9},{5... | collective-permute-start | bytes 12296 | tf_op jit(solution)/shard_map/ppermute | solution.py:355
  38.4 3.7 %collective-permute-start.6 = (f32[32,32]{1,0:T(8,128)S(1)}, f32[32,32]{1,0:T(8,128)S(1)}, u32[]{:S(2)}, u32[]{:S(2)}) collective-permute-start(f32[32,32]{1,0:T(8,128)S(1)} %add.25), channel_id=1, source_target_pairs={{0,16},{4,20},{8,24},{12,28},{16,0},{20,4},{24,8},{28,12},{1,17},{... | collective-permute-start | bytes 12296 | tf_op jit(solution)/shard_map/ppermute | solution.py:355
  42.1 0.7 copy-start.5
  42.8 15.7 %collective-permute-start.7 = (f32[32,3072]{1,0:T(8,128)S(1)}, f32[32,3072]{1,0:T(8,128)S(1)}, u32[]{:S(2)}, u32[]{:S(2)}) collective-permute-start(f32[32,3072]{1,0:T(8,128)S(1)} %get-tuple-element.27), channel_id=1, source_target_pairs={{0,1},{1,0},{2,3},{3,2},{4,5},{5,4},{6,7},{7,6},{8,9},{9,8},{10,11... | collective-permute-start | bytes 1179656 | tf_op jit(solution)/shard_map/ppermute | solution.py:345
  44.5 29.7 %collective-permute-start.8 = (f32[32,3072]{1,0:T(8,128)S(1)}, f32[32,3072]{1,0:T(8,128)S(1)}, u32[]{:S(2)}, u32[]{:S(2)}) collective-permute-start(f32[32,3072]{1,0:T(8,128)S(1)} %get-tuple-element.28), channel_id=1, source_target_pairs={{0,2},{1,3},{2,0},{3,1},{4,6},{5,7},{6,4},{7,5},{8,10},{9,11},{10,... | collective-permute-start | bytes 1179656 | tf_op jit(solution)/shard_map/ppermute | solution.py:345
  47.1 27.2 %collective-permute-start.9 = (f32[32,3072]{1,0:T(8,128)S(1)}, f32[32,3072]{1,0:T(8,128)S(1)}, u32[]{:S(2)}, u32[]{:S(2)}) collective-permute-start(f32[32,3072]{1,0:T(8,128)S(1)} %get-tuple-element.29), channel_id=1, source_target_pairs={{0,3},{1,2},{2,1},{3,0},{4,7},{5,6},{6,5},{7,4},{8,11},{9,10},{10,... | collective-permute-start | bytes 1179656 | tf_op jit(solution)/shard_map/ppermute | solution.py:345
  74.6 1.2 %collective-permute-start.10 = (f32[16,32]{1,0:T(8,128)S(1)}, f32[16,32]{1,0:T(8,128)S(1)}, u32[]{:S(2)}, u32[]{:S(2)}) collective-permute-start(f32[16,32]{1,0:T(8,128)S(1)} %get-tuple-element.30), channel_id=1, source_target_pairs={{0,4},{4,0},{8,12},{12,8},{16,20},{20,16},{24,28},{28,24},{1,5},{5... | collective-permute-start | bytes 6152 | tf_op jit(solution)/shard_map/ppermute | solution.py:355
  75.8 3.7 %collective-permute-start.11 = (f32[16,32]{1,0:T(8,128)S(1)}, f32[16,32]{1,0:T(8,128)S(1)}, u32[]{:S(2)}, u32[]{:S(2)}) collective-permute-start(f32[16,32]{1,0:T(8,128)S(1)} %add.27), channel_id=1, source_target_pairs={{0,8},{4,12},{8,0},{12,4},{16,24},{20,28},{24,16},{28,20},{1,9},{5... | collective-permute-start | bytes 6152 | tf_op jit(solution)/shard_map/ppermute | solution.py:355
  79.5 3.7 %collective-permute-start.12 = (f32[16,32]{1,0:T(8,128)S(1)}, f32[16,32]{1,0:T(8,128)S(1)}, u32[]{:S(2)}, u32[]{:S(2)}) collective-permute-start(f32[16,32]{1,0:T(8,128)S(1)} %add.28), channel_id=1, source_target_pairs={{0,16},{4,20},{8,24},{12,28},{16,0},{20,4},{24,8},{28,12},{1,17},{... | collective-permute-start | bytes 6152 | tf_op jit(solution)/shard_map/ppermute | solution.py:355
  83.2 7.3 %collective-permute-start.13 = (f32[16,32]{1,0:T(8,128)S(1)}, f32[16,32]{1,0:T(8,128)S(1)}, u32[]{:S(2)}, u32[]{:S(2)}) collective-permute-start(f32[16,32]{1,0:T(8,128)S(1)} %add.29), channel_id=1, source_target_pairs={{0,1},{1,0},{2,3},{3,2},{4,5},{5,4},{6,7},{7,6},{8,9},{9,8},{10,11... | collective-permute-start | bytes 6152 | tf_op jit(solution)/shard_map/ppermute | solution.py:355
  90.4 4.7 %collective-permute-start.14 = (f32[16,32]{1,0:T(8,128)S(1)}, f32[16,32]{1,0:T(8,128)S(1)}, u32[]{:S(2)}, u32[]{:S(2)}) collective-permute-start(f32[16,32]{1,0:T(8,128)S(1)} %add.30), channel_id=1, source_target_pairs={{0,2},{1,3},{2,0},{3,1},{4,6},{5,7},{6,4},{7,5},{8,10},{9,11},{10,... | collective-permute-start | bytes 6152 | tf_op jit(solution)/shard_map/ppermute | solution.py:355
  97.0 5.0 %collective-permute-start.15 = (f32[8,3072]{1,0:T(8,128)S(1)}, f32[8,3072]{1,0:T(8,128)S(1)}, u32[]{:S(2)}, u32[]{:S(2)}) collective-permute-start(f32[8,3072]{1,0:T(8,128)S(1)} %get-tuple-element.33), channel_id=1, source_target_pairs={{0,1},{1,0},{2,3},{3,2},{4,5},{5,4},{6,7},{7,6},{8,9},{9,8},{10,11... | collective-permute-start | bytes 294920 | tf_op jit(solution)/shard_map/ppermute | solution.py:345
  99.0 7.6 %collective-permute-start.16 = (f32[8,3072]{1,0:T(8,128)S(1)}, f32[8,3072]{1,0:T(8,128)S(1)}, u32[]{:S(2)}, u32[]{:S(2)}) collective-permute-start(f32[8,3072]{1,0:T(8,128)S(1)} %get-tuple-element.34), channel_id=1, source_target_pairs={{0,2},{1,3},{2,0},{3,1},{4,6},{5,7},{6,4},{7,5},{8,10},{9,11},{10,... | collective-permute-start | bytes 294920 | tf_op jit(solution)/shard_map/ppermute | solution.py:345
  100.1 6.5 %collective-permute-start.17 = (f32[8,3072]{1,0:T(8,128)S(1)}, f32[8,3072]{1,0:T(8,128)S(1)}, u32[]{:S(2)}, u32[]{:S(2)}) collective-permute-start(f32[8,3072]{1,0:T(8,128)S(1)} %get-tuple-element.35), channel_id=1, source_target_pairs={{0,3},{1,2},{2,1},{3,0},{4,7},{5,6},{6,5},{7,4},{8,11},{9,10},{10,... | collective-permute-start | bytes 294920 | tf_op jit(solution)/shard_map/ppermute | solution.py:345

commit v2 on v1

--- a/solution.py
+++ b/solution.py
@@ -1,5 +1,4 @@
 import functools
-import math
 
 import jax
 import jax.numpy as jnp
@@ -7,6 +6,7 @@
 from jax.experimental import pallas as pl
 from jax.experimental.pallas import tpu as pltpu
 from jax.sharding import PartitionSpec as P
+
 
 HOPPING = 0.13
 LANES = 128
@@ -245,8 +245,6 @@
     signs = rim_signs()
 
     def body(vector, carry):
-        values = {}
-
         def store(place, value):
             out[place] = value
 
@@ -357,35 +355,74 @@
     return value
 
 
-def project_kernel(groups, vectors, kept, over, basis, *outs):
+def weight_rows(real, imag):
+    weight = jnp.concatenate(
+        [jnp.concatenate([real, -imag], axis=1), jnp.concatenate([imag, real], axis=1)], axis=0
+    )
+    high, low = two_halves(weight)
+    return jnp.concatenate(
+        [jnp.concatenate([high, high], axis=1), jnp.concatenate([low, low], axis=1)], axis=0
+    )
+
+
+def weighted(weight, basis):
+    both = jnp.dot(weight, basis, preferred_element_type=jnp.float32)
+    half = both.shape[0] // 2
+    return both[:half] + both[half:]
+
+
+def slice_kernel(groups, rows, ship, basis, *outs):
     here = lax.axis_index("ba")
-    real, imag = over[:vectors, :], over[vectors:, :]
-    weight = jnp.concatenate(
-        [
-            jnp.concatenate([real, -imag], axis=1),
-            jnp.concatenate([imag, real], axis=1),
-        ],
-        axis=0,
-    )
-    high, low = two_halves(weight)
-    weight = jnp.concatenate(
-        [jnp.concatenate([high, high], axis=1), jnp.concatenate([low, low], axis=1)], axis=0
-    )
+    per = basis.shape[1] // groups
+    for step in range(1, groups):
+        start = pl.multiple_of(partner(here, step, groups) * per, rows)
+        outs[step - 1][...] = basis[:, pl.ds(start, ship), :]
+
+
+def relay_kernel(kept, blocks, *refs):
+    count = len(refs) // 2
+    for part, out in zip(refs[:count], refs[count:]):
+
+        def body(block, carry, part=part, out=out):
+            lanes = pl.ds(pl.multiple_of(block * LANES, LANES), LANES)
+            for ri in range(2):
+                high, low = two_halves(part[pl.ds(ri * blocks + block, kept, stride=2 * blocks), :])
+                out[ri * kept : (ri + 1) * kept, lanes] = high
+                out[(2 + ri) * kept : (3 + ri) * kept, lanes] = low
+            return carry
+
+        lax.fori_loop(0, blocks, body, 0, unroll=2)
+
+
+def project_kernel(groups, vectors, kept, shipped, over, basis, *outs):
+    here = lax.axis_index("ba")
+    weight = weight_rows(over[:vectors, :], over[vectors:, :])
     for step in range(groups):
-        both = jnp.dot(
-            weight, basis[partner(here, step, groups)], preferred_element_type=jnp.float32
+        other = partner(here, step, groups)
+        value = weighted(weight, basis[other, :, shipped:])
+        width = value.shape[1]
+        outs[step][:, :width] = value
+        outs[step][:, width:] = jnp.zeros((2 * vectors, LANES), jnp.float32)
+        outs[step][:, width : width + kept] = over[...]
+
+
+def rest_kernel(groups, vectors, kept, shipped, scale, over, basis, applied, *refs):
+    parts, refs = refs[:groups], refs[groups:]
+    pieces, (rest_ref, gram) = refs[:-2], refs[-2:]
+    here = lax.axis_index("ba")
+    width = parts[0].shape[1] - LANES
+    total = parts[0][:, :width]
+    for part in parts[1:]:
+        total = total + part[:, :width]
+    if shipped:
+        head = weighted(
+            weight_rows(over[:vectors, :], over[vectors:, :]), basis[here, :, :shipped]
         )
-        outs[step][...] = both[: 2 * vectors] + both[2 * vectors :]
-
-
-def rest_kernel(groups, vectors, scale, applied, *refs):
-    parts, (rest_ref, gram) = refs[:groups], refs[groups:]
-    here = lax.axis_index("ba")
-    rest = applied[here]
-    total = parts[0][...]
-    for part in parts[1:]:
-        total = total + part[...]
-    rest = rest - total
+        for part, piece in zip(parts[1:], pieces):
+            there = part[:, width : width + kept]
+            head = head + weighted(weight_rows(there[:vectors], there[vectors:]), piece[...])
+        total = jnp.concatenate([head, total], axis=1)
+    rest = applied[here] - total
     rest_ref[...] = rest
     both = jnp.concatenate(two_halves(rest), axis=0)
     full = lax.dot_general(
@@ -407,7 +444,6 @@
     lane = lax.broadcasted_iota(jnp.int32, shape, 1)
     unit = jnp.where(lane == row + vectors, 1.0, 0.0)
     re = jnp.where(lane < vectors, gram[...], unit)
-    im = jnp.where(lane < vectors, pltpu.roll(gram[...], vectors, 1), 0.0) if False else None
     im = jnp.concatenate([gram[:, vectors:], jnp.zeros((vectors, vectors), jnp.float32)], axis=1)
     for pivot in range(vectors):
         scale = 1.0 / jnp.sqrt(re[pivot : pivot + 1, pivot : pivot + 1])
@@ -419,20 +455,9 @@
         re = jnp.where(below, new_re, jnp.where(row == pivot, row_re, re))
         im = jnp.where(below, new_im, jnp.where(row == pivot, row_im, im))
     inv_re, inv_im = re[:, vectors:], im[:, vectors:]
-    weight = jnp.concatenate(
-        [
-            jnp.concatenate([inv_re, inv_im], axis=1),
-            jnp.concatenate([-inv_im, inv_re], axis=1),
-        ],
-        axis=0,
-    )
-    high, low = two_halves(weight)
-    weight = jnp.concatenate(
-        [jnp.concatenate([high, high], axis=1), jnp.concatenate([low, low], axis=1)], axis=0
-    )
+    weight = weight_rows(inv_re, -inv_im)
     both = jnp.concatenate(two_halves(rest[...]), axis=0)
-    full = jnp.dot(weight, both, preferred_element_type=jnp.float32)
-    full = full[: 2 * vectors] + full[2 * vectors :]
+    full = weighted(weight, both)
     own = vectors // groups
     for group in range(groups):
         for ri in range(2):
@@ -454,7 +479,7 @@
                 out[pl.ds(first + block + ri * blocks, own, stride=2 * blocks), :] = value
 
 
-def call(kernel, outs, *args, scratch=(), flops=0):
+def call(kernel, outs, *args, scratch=(), flops=0, grant=6):
     nbytes = sum(a.size * a.dtype.itemsize for a in (*args, *outs))
     spec = pl.BlockSpec(memory_space=pltpu.VMEM)
     return pl.pallas_call(
@@ -463,7 +488,7 @@
         in_specs=[spec] * len(args),
         out_specs=tuple([spec] * len(outs)),
         scratch_shapes=list(scratch),
-        compiler_params=pltpu.CompilerParams(vmem_limit_bytes=40 * 1024 * 1024),
+        compiler_params=pltpu.CompilerParams(vmem_limit_bytes=grant << 20),
         cost_estimate=pl.CostEstimate(flops=flops, bytes_accessed=nbytes, transcendentals=0),
     )(*args)
 
@@ -490,6 +515,9 @@
     scale = 1.0 / (2 * COMPS * slices * sites * places)
     psi = tiles_of(search_block, vectors * 2 * COMPS)
     basis = tiles_of(kept_basis, kept * 2 * COMPS).reshape(kept * 2 * blocks, LANES)
+    ahead_comps = 2 * (COMPS // groups) // 3 if COMPS % groups == 0 else 0
+    ship = ahead_comps * rows
+    shipped = ship * LANES
     links = tiles_of(gauge_links, 72)
     clover = tiles_of(clover_term, 144)
     rim = shape_of(vectors * COMPS // slices, rows, LANES)
@@ -505,6 +533,14 @@
         functools.partial(pack_kernel, lattice, vectors), (rim, rim), psi, links, flops=200 * work
     )
     rims = swap(ahead, behind)
+    pieces = []
+    if ship:
+        pieces = call(
+            functools.partial(slice_kernel, groups, rows, ship),
+            (shape_of(2 * kept, ship, LANES),) * (groups - 1),
+            basis.reshape(2 * kept, blocks, LANES),
+        )
+        pieces = exchanged([None, *pieces], "ba")[1:]
     local = functools.partial(local_kernel, lattice, vectors)
     (part,) = call(local, (field,), psi, links, clover, flops=2000 * work)
     (rows_of_basis,) = call(
@@ -533,19 +569,27 @@
         flops=400 * work,
     )
     over = summed(over, "ta")
-    quarter = shape_of(2 * vectors, per * LANES)
     parts = call(
-        functools.partial(project_kernel, groups, vectors, kept),
-        (quarter,) * groups,
+        functools.partial(project_kernel, groups, vectors, kept, shipped),
+        (shape_of(2 * vectors, (per + 1) * LANES - shipped),) * groups,
         over,
         rows_of_basis,
     )
     parts = exchanged(parts, "ba")
+    if ship:
+        pieces = call(
+            functools.partial(relay_kernel, kept, ship),
+            (jax.ShapeDtypeStruct((4 * kept, shipped), jnp.bfloat16),) * (groups - 1),
+            *(piece.reshape(2 * kept * ship, LANES) for piece in pieces),
+        )
     rest, gram = call(
-        functools.partial(rest_kernel, groups, vectors, scale),
-        (quarter, shape_of(vectors, 2 * vectors)),
+        functools.partial(rest_kernel, groups, vectors, kept, shipped, scale),
+        (shape_of(2 * vectors, per * LANES), shape_of(vectors, 2 * vectors)),
+        over,
+        rows_of_basis,
         applied,
         *parts,
+        *pieces,
     )
     gram = summed(summed(gram, "ta"), "ba")
     piece = shape_of(2 * own, per * LANES)
@@ -574,6 +618,7 @@
         P(None, None, None, None, "ta", None),
         P(None, None, None, None, "ta", None),
     )
+
     return jax.shard_map(
         per_device,
         mesh=mesh,

time: 108 us -> 110 us (1.019)
  waiting for transfers between devices: 58.5 us -> 49.8 us
  starting transfers between devices: 24 us -> 31.6 us
  local copies, waits for them, and re-layouts: 2.38 us -> 4.27 us
  Pallas kernels: 21.9 us -> 23.6 us
    ppermute x4, waiting for transfers between devices: 8.1 us -> 1.94 us  [swap(): return (lax.ppermute(ahead, 'ta', down), lax.ppermute(behind, 'ta', up))]
    ppermute x6 -> x9, starting transfers between devices: 8.91 us -> 14.6 us  [exchanged(): out.append(lax.ppermute(values[step], axis, pairs))]
    ppermute x8, waiting for transfers between devices: 18.4 us -> 14.3 us  [summed(): lax.ppermute(value, axis, [(i, i ^ step) for i in range(count)])]
    ppermute x8, starting transfers between devices: 10.7 us -> 12.7 us  [summed(): lax.ppermute(value, axis, [(i, i ^ step) for i in range(count)])]
    unnamed x12 -> x16, local copies, waits for them, and re-layouts: 2.38 us -> 4.27 us
    pallas_call x10 -> x12, Pallas kernels: 21.9 us -> 23.6 us  [call(): pl.pallas_call(kernel, out_shape=tuple(outs), in_specs=[spec] * len(args)...]
    ppermute x6 -> x9, waiting for transfers between devices: 32.1 us -> 33.5 us  [exchanged(): out.append(lax.ppermute(values[step], axis, pairs))]
  transfers between devices with their start and end apart: 18 -> 21, of which waited for: 16 -> 14; matrix products, arithmetic and copies ran while one was open for 0% -> 0% of each run, Pallas kernels for 12% -> 17%
where the time goes in v2:
time: 110 us
  waiting for transfers between devices  49.8 us (45%)
  starting transfers between devices  31.6 us (29%)
  Pallas kernels  23.6 us (21%)
  local copies, waits for them, and re-layouts  4.27 us (4%)
    ppermute x9, waiting for transfers between devices, exchanged(): out.append(lax.ppermute(values[step], axis, pairs))  33.5 us
    pallas_call x12, Pallas kernels, call(): pl.pallas_call(kernel, out_shape=tuple(outs), in_specs=[spec] * len(args)...  23.6 us
    ppermute x9, starting transfers between devices, exchanged(): out.append(lax.ppermute(values[step], axis, pairs))  14.6 us
    ppermute x8, waiting for transfers between devices, summed(): lax.ppermute(value, axis, [(i, i ^ step) for i in range(count)])  14.3 us
    ppermute x8, starting transfers between devices, summed(): lax.ppermute(value, axis, [(i, i ^ step) for i in range(count)])  12.7 us
    ppermute x4, starting transfers between devices, swap(): return (lax.ppermute(ahead, 'ta', down), lax.ppermute(behind, 'ta', up))  4.36 us
    unnamed x16, local copies, waits for them, and re-layouts  4.27 us
  transfers between devices with their start and end apart: 21, of which 14 were waited for; matrix products, arithmetic and copies ran while one was open for 0% of the time, Pallas kernels for 17%

profile of v2, /device:TPU:0, one launch (start us, length us, event | category | flops | bytes accessed | tf_op | source)
XLA Modules:
  0.0 110.1 jit_solution(509045915919061156)
XLA Ops:
  3.5 3.4 %collective-permute-start = (f32[96,8,128]{2,1,0:T(8,128)S(1)}, f32[96,8,128]{2,1,0:T(8,128)S(1)}, u32[]{:S(2)}, u32[]{:S(2)}) collective-permute-start(f32[96,8,128]{2,1,0:T(8,128)S(1)} %get-tuple-element.25), channel_id=1, source_target_pairs={{0,28},{4,0},{8,4},{12,8},{16,12},{20,16},{24,20},{28,24},{1,29},{... | collective-permute-start | bytes 1179656 | tf_op jit(solution)/shard_map/ppermute | solution.py:530
  6.9 1.9 %copy-done = f32[32,2,4,3,2,512]{5,4,3,2,1,0:T(2,128)S(1)} copy-done((f32[32,2,4,3,2,512]{5,4,3,2,1,0:T(2,128)S(1)}, f32[32,2,4,3,2,512]{5,4,3,2,1,0:T(2,128)}, u32[]{:S(2)}) %copy-start) | copy-done | bytes 3145752
  8.9 1.6 %collective-permute-start.10 = (f32[64,16,128]{2,1,0:T(8,128)S(1)}, f32[64,16,128]{2,1,0:T(8,128)S(1)}, u32[]{:S(2)}, u32[]{:S(2)}) collective-permute-start(f32[64,16,128]{2,1,0:T(8,128)S(1)} %get-tuple-element.36), channel_id=1, source_target_pairs={{0,1},{1,0},{2,3},{3,2},{4,5},{5,4},{6,7},{7,6},{8,9},{9,8},{10,11... | collective-permute-start | bytes 1572872 | tf_op jit(solution)/shard_map/ppermute | solution.py:343
  10.6 4.9 %shard_map.59.part = f32[384,8,128]{2,1,0:T(8,128)S(1)} custom-call(f32[384,8,128]{2,1,0:T(8,128)S(1)} %bitcast.41, f32[72,8,128]{2,1,0:T(8,128)S(1)} %bitcast.36, f32[144,8,128]{2,1,0:T(8,128)S(1)} %bitcast.42), custom_call_target="tpu_custom_call" | custom-call | flops 32768000 | bytes 4030464 | tf_op jit(solution)/shard_map/pallas_call | solution.py:485
  15.5 1.9 %collective-permute-done.1.rim_behind = f32[96,8,128]{2,1,0:T(8,128)S(1)} collective-permute-done((f32[96,8,128]{2,1,0:T(8,128)S(1)}, f32[96,8,128]{2,1,0:T(8,128)S(1)}, u32[]{:S(2)}, u32[]{:S(2)}) %collective-permute-start.1) | collective-permute-done | bytes 393248 | tf_op jit(solution)/shard_map/ppermute | solution.py:530
  19.4 2.6 %collective-permute-start.11 = (f32[64,16,128]{2,1,0:T(8,128)S(1)}, f32[64,16,128]{2,1,0:T(8,128)S(1)}, u32[]{:S(2)}, u32[]{:S(2)}) collective-permute-start(f32[64,16,128]{2,1,0:T(8,128)S(1)} %get-tuple-element.37), channel_id=1, source_target_pairs={{0,2},{1,3},{2,0},{3,1},{4,6},{5,7},{6,4},{7,5},{8,10},{9,11},{10,... | collective-permute-start | bytes 1572872 | tf_op jit(solution)/shard_map/ppermute | solution.py:343
  23.4 3.0 %shard_map.63.basis = bf16[4,128,3072]{2,1,0:T(8,128)(2,1)S(1)} custom-call(f32[6144,128]{1,0:T(8,128)S(1)} %bitcast.34), custom_call_target="tpu_custom_call" | custom-call | bytes 6291456 | tf_op jit(solution)/shard_map/pallas_call | solution.py:485
  26.4 4.9 %shard_map.62.part = f32[384,8,128]{2,1,0:T(8,128)S(1)} custom-call(f32[384,8,128]{2,1,0:T(8,128)S(1)} %get-tuple-element.27.psi, f32[72,8,128]{2,1,0:T(8,128)S(1)} %bitcast.38, f32[144,8,128]{2,1,0:T(8,128)S(1)} %bitcast.43), custom_call_target="tpu_custom_call" | custom-call | flops 32768000 | bytes 4030464 | tf_op jit(solution)/shard_map/pallas_call | solution.py:485
  31.3 3.5 %shard_map.64 = (f32[4,32,3072]{2,1,0:T(8,128)S(1)}, f32[32,32]{1,0:T(8,128)S(1)}) custom-call(f32[384,8,128]{2,1,0:T(8,128)S(1)} %shard_map.62.part, f32[72,8,128]{2,1,0:T(8,128)S(1)} %bitcast.39, f32[96,8,128]{2,1,0:T(8,128)S(1)} %collective-permute-done.2.rim_ahead, f32[96,8,128]{2,1,0:T(8,128)S(1)} %collective-permute-done.3.rim_behind, ...), custom_call_target="tpu_custom_call" | custom-call | flops 6553600 | bytes 7376896 | tf_op jit(solution)/shard_map/pallas_call | solution.py:485
  36.1 2.0 %collective-permute-start.5 = (f32[32,32]{1,0:T(8,128)S(1)}, f32[32,32]{1,0:T(8,128)S(1)}, u32[]{:S(2)}, u32[]{:S(2)}) collective-permute-start(f32[32,32]{1,0:T(8,128)S(1)} %add.24), channel_id=1, source_target_pairs={{0,8},{4,12},{8,0},{12,4},{16,24},{20,28},{24,16},{28,20},{1,9},{5... | collective-permute-start | bytes 12296 | tf_op jit(solution)/shard_map/ppermute | solution.py:353
  38.1 1.8 %collective-permute-done.5 = f32[32,32]{1,0:T(8,128)S(1)} collective-permute-done((f32[32,32]{1,0:T(8,128)S(1)}, f32[32,32]{1,0:T(8,128)S(1)}, u32[]{:S(2)}, u32[]{:S(2)}) %collective-permute-start.5) | collective-permute-done | bytes 4128 | tf_op jit(solution)/shard_map/ppermute | solution.py:353
  41.1 2.4 %collective-permute-done.6 = f32[32,32]{1,0:T(8,128)S(1)} collective-permute-done((f32[32,32]{1,0:T(8,128)S(1)}, f32[32,32]{1,0:T(8,128)S(1)}, u32[]{:S(2)}, u32[]{:S(2)}) %collective-permute-start.6) | collective-permute-done | bytes 4128 | tf_op jit(solution)/shard_map/ppermute | solution.py:353
  44.5 2.6 %collective-permute-start.8 = (f32[32,1152]{1,0:T(8,128)S(1)}, f32[32,1152]{1,0:T(8,128)S(1)}, u32[]{:S(2)}, u32[]{:S(2)}) collective-permute-start(f32[32,1152]{1,0:T(8,128)S(1)} %get-tuple-element.34), channel_id=1, source_target_pairs={{0,2},{1,3},{2,0},{3,1},{4,6},{5,7},{6,4},{7,5},{8,10},{9,11},{10,... | collective-permute-start | bytes 442376 | tf_op jit(solution)/shard_map/ppermute | solution.py:343
  48.5 15.3 %collective-permute-done.11 = f32[64,16,128]{2,1,0:T(8,128)S(1)} collective-permute-done((f32[64,16,128]{2,1,0:T(8,128)S(1)}, f32[64,16,128]{2,1,0:T(8,128)S(1)}, u32[]{:S(2)}, u32[]{:S(2)}) %collective-permute-start.11) | collective-permute-done | bytes 524320 | tf_op jit(solution)/shard_map/ppermute | solution.py:343
  65.0 13.2 %collective-permute-done.8.refs_2_ = f32[32,1152]{1,0:T(8,128)S(1)} collective-permute-done((f32[32,1152]{1,0:T(8,128)S(1)}, f32[32,1152]{1,0:T(8,128)S(1)}, u32[]{:S(2)}, u32[]{:S(2)}) %collective-permute-start.8) | collective-permute-done | bytes 147488 | tf_op jit(solution)/shard_map/ppermute | solution.py:343
  81.7 2.4 %collective-permute-done.14 = f32[16,32]{1,0:T(8,128)S(1)} collective-permute-done((f32[16,32]{1,0:T(8,128)S(1)}, f32[16,32]{1,0:T(8,128)S(1)}, u32[]{:S(2)}, u32[]{:S(2)}) %collective-permute-start.14) | collective-permute-done | bytes 2080 | tf_op jit(solution)/shard_map/ppermute | solution.py:353
  85.6 2.2 %collective-permute-done.15 = f32[16,32]{1,0:T(8,128)S(1)} collective-permute-done((f32[16,32]{1,0:T(8,128)S(1)}, f32[16,32]{1,0:T(8,128)S(1)}, u32[]{:S(2)}, u32[]{:S(2)}) %collective-permute-start.15) | collective-permute-done | bytes 2080 | tf_op jit(solution)/shard_map/ppermute | solution.py:353
  87.7 2.7 %collective-permute-start.16 = (f32[16,32]{1,0:T(8,128)S(1)}, f32[16,32]{1,0:T(8,128)S(1)}, u32[]{:S(2)}, u32[]{:S(2)}) collective-permute-start(f32[16,32]{1,0:T(8,128)S(1)} %add.29), channel_id=1, source_target_pairs={{0,1},{1,0},{2,3},{3,2},{4,5},{5,4},{6,7},{7,6},{8,9},{9,8},{10,11... | collective-permute-start | bytes 6152 | tf_op jit(solution)/shard_map/ppermute | solution.py:353
  90.4 1.6 %collective-permute-done.16 = f32[16,32]{1,0:T(8,128)S(1)} collective-permute-done((f32[16,32]{1,0:T(8,128)S(1)}, f32[16,32]{1,0:T(8,128)S(1)}, u32[]{:S(2)}, u32[]{:S(2)}) %collective-permute-start.16) | collective-permute-done | bytes 2080 | tf_op jit(solution)/shard_map/ppermute | solution.py:353
  92.0 3.9 %collective-permute-start.17 = (f32[16,32]{1,0:T(8,128)S(1)}, f32[16,32]{1,0:T(8,128)S(1)}, u32[]{:S(2)}, u32[]{:S(2)}) collective-permute-start(f32[16,32]{1,0:T(8,128)S(1)} %add.30), channel_id=1, source_target_pairs={{0,2},{1,3},{2,0},{3,1},{4,6},{5,7},{6,4},{7,5},{8,10},{9,11},{10,... | collective-permute-start | bytes 6152 | tf_op jit(solution)/shard_map/ppermute | solution.py:353
  97.6 1.9 %shard_map.69 = (f32[8,3072]{1,0:T(8,128)S(1)}, f32[8,3072]{1,0:T(8,128)S(1)}, f32[8,3072]{1,0:T(8,128)S(1)}, f32[8,3072]{1,0:T(8,128)S(1)}) custom-call(f32[16,32]{1,0:T(8,128)S(1)} %add.31.gram, f32[32,3072]{1,0:T(8,128)S(1)} %get-tuple-element.43.rest), custom_call_target="tpu_custom_call" | custom-call | bytes 788480 | tf_op jit(solution)/shard_map/pallas_call | solution.py:485
  100.6 2.1 %collective-permute-start.19 = (f32[8,3072]{1,0:T(8,128)S(1)}, f32[8,3072]{1,0:T(8,128)S(1)}, u32[]{:S(2)}, u32[]{:S(2)}) collective-permute-start(f32[8,3072]{1,0:T(8,128)S(1)} %get-tuple-element.46), channel_id=1, source_target_pairs={{0,2},{1,3},{2,0},{3,1},{4,6},{5,7},{6,4},{7,5},{8,10},{9,11},{10,... | collective-permute-start | bytes 294920 | tf_op jit(solution)/shard_map/ppermute | solution.py:343
  104.4 1.7 %collective-permute-done.19.refs_2_ = f32[8,3072]{1,0:T(8,128)S(1)} collective-permute-done((f32[8,3072]{1,0:T(8,128)S(1)}, f32[8,3072]{1,0:T(8,128)S(1)}, u32[]{:S(2)}, u32[]{:S(2)}) %collective-permute-start.19) | collective-permute-done | bytes 98336 | tf_op jit(solution)/shard_map/ppermute | solution.py:343
  106.1 3.0 %collective-permute-done.20.refs_3_ = f32[8,3072]{1,0:T(8,128)S(1)} collective-permute-done((f32[8,3072]{1,0:T(8,128)S(1)}, f32[8,3072]{1,0:T(8,128)S(1)}, u32[]{:S(2)}, u32[]{:S(2)}) %collective-permute-start.20) | collective-permute-done | bytes 98336 | tf_op jit(solution)/shard_map/ppermute | solution.py:343
  (54 shorter events, 22.8 us)
Async XLA Ops:
  3.5 12.0 %collective-permute-start = (f32[96,8,128]{2,1,0:T(8,128)S(1)}, f32[96,8,128]{2,1,0:T(8,128)S(1)}, u32[]{:S(2)}, u32[]{:S(2)}) collective-permute-start(f32[96,8,128]{2,1,0:T(8,128)S(1)} %get-tuple-element.25), channel_id=1, source_target_pairs={{0,28},{4,0},{8,4},{12,8},{16,12},{20,16},{24,20},{28,24},{1,29},{... | collective-permute-start | bytes 1179656 | tf_op jit(solution)/shard_map/ppermute | solution.py:530
  6.9 10.5 %collective-permute-start.1 = (f32[96,8,128]{2,1,0:T(8,128)S(1)}, f32[96,8,128]{2,1,0:T(8,128)S(1)}, u32[]{:S(2)}, u32[]{:S(2)}) collective-permute-start(f32[96,8,128]{2,1,0:T(8,128)S(1)} %get-tuple-element.26), channel_id=1, source_target_pairs={{0,4},{4,8},{8,12},{12,16},{16,20},{20,24},{24,28},{28,0},{1,5},{5... | collective-permute-start | bytes 1179656 | tf_op jit(solution)/shard_map/ppermute | solution.py:530
  6.9 1.9 %copy-start = (f32[32,2,4,3,2,512]{5,4,3,2,1,0:T(2,128)S(1)}, f32[32,2,4,3,2,512]{5,4,3,2,1,0:T(2,128)}, u32[]{:S(2)}) copy-start(f32[32,2,4,3,2,512]{5,4,3,2,1,0:T(2,128)} %param.5) | copy-start | bytes 9437188
  8.9 38.2 %collective-permute-start.10 = (f32[64,16,128]{2,1,0:T(8,128)S(1)}, f32[64,16,128]{2,1,0:T(8,128)S(1)}, u32[]{:S(2)}, u32[]{:S(2)}) collective-permute-start(f32[64,16,128]{2,1,0:T(8,128)S(1)} %get-tuple-element.36), channel_id=1, source_target_pairs={{0,1},{1,0},{2,3},{3,2},{4,5},{5,4},{6,7},{7,6},{8,9},{9,8},{10,11... | collective-permute-start | bytes 1572872 | tf_op jit(solution)/shard_map/ppermute | solution.py:343
  10.6 12.8 %copy-start.1 = (f32[32,2,4,3,2,512]{5,4,3,2,1,0:T(2,128)S(1)}, f32[32,2,4,3,2,512]{5,4,3,2,1,0:T(2,128)}, u32[]{:S(2)}) copy-start(f32[32,2,4,3,2,512]{5,4,3,2,1,0:T(2,128)} %param.5) | copy-start | bytes 9437188
  18.5 12.8 %collective-permute-start.2 = (f32[96,8,128]{2,1,0:T(8,128)S(1)}, f32[96,8,128]{2,1,0:T(8,128)S(1)}, u32[]{:S(2)}, u32[]{:S(2)}) collective-permute-start(f32[96,8,128]{2,1,0:T(8,128)S(1)} %get-tuple-element.28), channel_id=1, source_target_pairs={{0,28},{4,0},{8,4},{12,8},{16,12},{20,16},{24,20},{28,24},{1,29},{... | collective-permute-start | bytes 1179656 | tf_op jit(solution)/shard_map/ppermute | solution.py:530
  19.4 11.9 %collective-permute-start.3 = (f32[96,8,128]{2,1,0:T(8,128)S(1)}, f32[96,8,128]{2,1,0:T(8,128)S(1)}, u32[]{:S(2)}, u32[]{:S(2)}) collective-permute-start(f32[96,8,128]{2,1,0:T(8,128)S(1)} %get-tuple-element.29), channel_id=1, source_target_pairs={{0,4},{4,8},{8,12},{12,16},{16,20},{20,24},{24,28},{28,0},{1,5},{5... | collective-permute-start | bytes 1179656 | tf_op jit(solution)/shard_map/ppermute | solution.py:530
  19.4 44.4 %collective-permute-start.11 = (f32[64,16,128]{2,1,0:T(8,128)S(1)}, f32[64,16,128]{2,1,0:T(8,128)S(1)}, u32[]{:S(2)}, u32[]{:S(2)}) collective-permute-start(f32[64,16,128]{2,1,0:T(8,128)S(1)} %get-tuple-element.37), channel_id=1, source_target_pairs={{0,2},{1,3},{2,0},{3,1},{4,6},{5,7},{6,4},{7,5},{8,10},{9,11},{10,... | collective-permute-start | bytes 1572872 | tf_op jit(solution)/shard_map/ppermute | solution.py:343
  22.0 41.8 %collective-permute-start.12 = (f32[64,16,128]{2,1,0:T(8,128)S(1)}, f32[64,16,128]{2,1,0:T(8,128)S(1)}, u32[]{:S(2)}, u32[]{:S(2)}) collective-permute-start(f32[64,16,128]{2,1,0:T(8,128)S(1)} %get-tuple-element.38), channel_id=1, source_target_pairs={{0,3},{1,2},{2,1},{3,0},{4,7},{5,6},{6,5},{7,4},{8,11},{9,10},{10,... | collective-permute-start | bytes 1572872 | tf_op jit(solution)/shard_map/ppermute | solution.py:343
  34.9 1.2 %collective-permute-start.4 = (f32[32,32]{1,0:T(8,128)S(1)}, f32[32,32]{1,0:T(8,128)S(1)}, u32[]{:S(2)}, u32[]{:S(2)}) collective-permute-start(f32[32,32]{1,0:T(8,128)S(1)} %get-tuple-element.30), channel_id=1, source_target_pairs={{0,4},{4,0},{8,12},{12,8},{16,20},{20,16},{24,28},{28,24},{1,5},{5... | collective-permute-start | bytes 12296 | tf_op jit(solution)/shard_map/ppermute | solution.py:353
  36.1 3.7 %collective-permute-start.5 = (f32[32,32]{1,0:T(8,128)S(1)}, f32[32,32]{1,0:T(8,128)S(1)}, u32[]{:S(2)}, u32[]{:S(2)}) collective-permute-start(f32[32,32]{1,0:T(8,128)S(1)} %add.24), channel_id=1, source_target_pairs={{0,8},{4,12},{8,0},{12,4},{16,24},{20,28},{24,16},{28,20},{1,9},{5... | collective-permute-start | bytes 12296 | tf_op jit(solution)/shard_map/ppermute | solution.py:353
  39.9 3.7 %collective-permute-start.6 = (f32[32,32]{1,0:T(8,128)S(1)}, f32[32,32]{1,0:T(8,128)S(1)}, u32[]{:S(2)}, u32[]{:S(2)}) collective-permute-start(f32[32,32]{1,0:T(8,128)S(1)} %add.25), channel_id=1, source_target_pairs={{0,16},{4,20},{8,24},{12,28},{16,0},{20,4},{24,8},{28,12},{1,17},{... | collective-permute-start | bytes 12296 | tf_op jit(solution)/shard_map/ppermute | solution.py:353
  43.6 34.6 %copy-start.7 = (f32[32,32]{1,0:T(8,128)}, f32[32,32]{1,0:T(8,128)S(1)}, u32[]{:S(2)}) copy-start(f32[32,32]{1,0:T(8,128)S(1)} %add.26.over) | copy-start | bytes 12292
  44.0 21.0 %collective-permute-start.7 = (f32[32,1152]{1,0:T(8,128)S(1)}, f32[32,1152]{1,0:T(8,128)S(1)}, u32[]{:S(2)}, u32[]{:S(2)}) collective-permute-start(f32[32,1152]{1,0:T(8,128)S(1)} %get-tuple-element.33), channel_id=1, source_target_pairs={{0,1},{1,0},{2,3},{3,2},{4,5},{5,4},{6,7},{7,6},{8,9},{9,8},{10,11... | collective-permute-start | bytes 442376 | tf_op jit(solution)/shard_map/ppermute | solution.py:343
  44.5 33.6 %collective-permute-start.8 = (f32[32,1152]{1,0:T(8,128)S(1)}, f32[32,1152]{1,0:T(8,128)S(1)}, u32[]{:S(2)}, u32[]{:S(2)}) collective-permute-start(f32[32,1152]{1,0:T(8,128)S(1)} %get-tuple-element.34), channel_id=1, source_target_pairs={{0,2},{1,3},{2,0},{3,1},{4,6},{5,7},{6,4},{7,5},{8,10},{9,11},{10,... | collective-permute-start | bytes 442376 | tf_op jit(solution)/shard_map/ppermute | solution.py:343
  47.1 31.1 %collective-permute-start.9 = (f32[32,1152]{1,0:T(8,128)S(1)}, f32[32,1152]{1,0:T(8,128)S(1)}, u32[]{:S(2)}, u32[]{:S(2)}) collective-permute-start(f32[32,1152]{1,0:T(8,128)S(1)} %get-tuple-element.35), channel_id=1, source_target_pairs={{0,3},{1,2},{2,1},{3,0},{4,7},{5,6},{6,5},{7,4},{8,11},{9,10},{10,... | collective-permute-start | bytes 442376 | tf_op jit(solution)/shard_map/ppermute | solution.py:343
  79.2 1.2 %collective-permute-start.13 = (f32[16,32]{1,0:T(8,128)S(1)}, f32[16,32]{1,0:T(8,128)S(1)}, u32[]{:S(2)}, u32[]{:S(2)}) collective-permute-start(f32[16,32]{1,0:T(8,128)S(1)} %get-tuple-element.42), channel_id=1, source_target_pairs={{0,4},{4,0},{8,12},{12,8},{16,20},{20,16},{24,28},{28,24},{1,5},{5... | collective-permute-start | bytes 6152 | tf_op jit(solution)/shard_map/ppermute | solution.py:353
  80.4 3.7 %collective-permute-start.14 = (f32[16,32]{1,0:T(8,128)S(1)}, f32[16,32]{1,0:T(8,128)S(1)}, u32[]{:S(2)}, u32[]{:S(2)}) collective-permute-start(f32[16,32]{1,0:T(8,128)S(1)} %add.27), channel_id=1, source_target_pairs={{0,8},{4,12},{8,0},{12,4},{16,24},{20,28},{24,16},{28,20},{1,9},{5... | collective-permute-start | bytes 6152 | tf_op jit(solution)/shard_map/ppermute | solution.py:353
  84.1 3.7 %collective-permute-start.15 = (f32[16,32]{1,0:T(8,128)S(1)}, f32[16,32]{1,0:T(8,128)S(1)}, u32[]{:S(2)}, u32[]{:S(2)}) collective-permute-start(f32[16,32]{1,0:T(8,128)S(1)} %add.28), channel_id=1, source_target_pairs={{0,16},{4,20},{8,24},{12,28},{16,0},{20,4},{24,8},{28,12},{1,17},{... | collective-permute-start | bytes 6152 | tf_op jit(solution)/shard_map/ppermute | solution.py:353
  87.7 4.3 %collective-permute-start.16 = (f32[16,32]{1,0:T(8,128)S(1)}, f32[16,32]{1,0:T(8,128)S(1)}, u32[]{:S(2)}, u32[]{:S(2)}) collective-permute-start(f32[16,32]{1,0:T(8,128)S(1)} %add.29), channel_id=1, source_target_pairs={{0,1},{1,0},{2,3},{3,2},{4,5},{5,4},{6,7},{7,6},{8,9},{9,8},{10,11... | collective-permute-start | bytes 6152 | tf_op jit(solution)/shard_map/ppermute | solution.py:353
  92.0 5.6 %collective-permute-start.17 = (f32[16,32]{1,0:T(8,128)S(1)}, f32[16,32]{1,0:T(8,128)S(1)}, u32[]{:S(2)}, u32[]{:S(2)}) collective-permute-start(f32[16,32]{1,0:T(8,128)S(1)} %add.30), channel_id=1, source_target_pairs={{0,2},{1,3},{2,0},{3,1},{4,6},{5,7},{6,4},{7,5},{8,10},{9,11},{10,... | collective-permute-start | bytes 6152 | tf_op jit(solution)/shard_map/ppermute | solution.py:353
  99.5 4.9 %collective-permute-start.18 = (f32[8,3072]{1,0:T(8,128)S(1)}, f32[8,3072]{1,0:T(8,128)S(1)}, u32[]{:S(2)}, u32[]{:S(2)}) collective-permute-start(f32[8,3072]{1,0:T(8,128)S(1)} %get-tuple-element.45), channel_id=1, source_target_pairs={{0,1},{1,0},{2,3},{3,2},{4,5},{5,4},{6,7},{7,6},{8,9},{9,8},{10,11... | collective-permute-start | bytes 294920 | tf_op jit(solution)/shard_map/ppermute | solution.py:343
  100.6 5.5 %collective-permute-start.19 = (f32[8,3072]{1,0:T(8,128)S(1)}, f32[8,3072]{1,0:T(8,128)S(1)}, u32[]{:S(2)}, u32[]{:S(2)}) collective-permute-start(f32[8,3072]{1,0:T(8,128)S(1)} %get-tuple-element.46), channel_id=1, source_target_pairs={{0,2},{1,3},{2,0},{3,1},{4,6},{5,7},{6,4},{7,5},{8,10},{9,11},{10,... | collective-permute-start | bytes 294920 | tf_op jit(solution)/shard_map/ppermute | solution.py:343
  102.7 6.4 %collective-permute-start.20 = (f32[8,3072]{1,0:T(8,128)S(1)}, f32[8,3072]{1,0:T(8,128)S(1)}, u32[]{:S(2)}, u32[]{:S(2)}) collective-permute-start(f32[8,3072]{1,0:T(8,128)S(1)} %get-tuple-element.47), channel_id=1, source_target_pairs={{0,3},{1,2},{2,1},{3,0},{4,7},{5,6},{6,5},{7,4},{8,11},{9,10},{10,... | collective-permute-start | bytes 294920 | tf_op jit(solution)/shard_map/ppermute | solution.py:343
  (5 other events, 7.6 us)

commit v3 on v2

--- a/solution.py
+++ b/solution.py
@@ -136,12 +136,12 @@
     return [add_phase(spinor(spin, c), spinor(2 + other, c), phase) for c in range(3)]
 
 
-def pack_rim(lattice, spinor, links, ahead_ref, behind_ref, vector):
+def pack_rim(lattice, spinor, links, direction, ahead_ref, behind_ref, vector):
     slices = lattice.slices
     ahead, behind = [], []
     for spin in range(2):
         ahead += half_spinor(spinor, 3, spin, True)
-        behind += times_dagger(link_at(links, 3), half_spinor(spinor, 3, spin, False))
+        behind += times_dagger(link_at(links, direction), half_spinor(spinor, 3, spin, False))
     for values, origin, ref in ((ahead, 0, ahead_ref), (behind, slices - 1, behind_ref)):
         flat = [part for pair in values for part in pair]
         for group in range(COMPS // slices):
@@ -163,14 +163,65 @@
     return [(flat[2 * i], flat[2 * i + 1]) for i in range(COMPS // 2)]
 
 
-def pack_kernel(lattice, vectors, psi, links, ahead_ref, behind_ref):
+def open_kernel(
+    lattice, groups, vectors, kept, ship,
+    psi_ref, links_ref, basis, ahead_ref, behind_ref, *refs,
+):
+    pieces = refs[: groups - 1]
+    psi, links, held, sems = refs[groups - 1 :]
+    here = lax.axis_index("ba")
+    rows, per = lattice.rows, basis.shape[2] // groups
+    count = links.shape[0]
+    fields = pltpu.make_async_copy(psi_ref, psi, sems.at[0])
+    links_in = pltpu.make_async_copy(links_ref.at[pl.ds(3 * count, count)], links, sems.at[1])
+    kept_in = []
+    for step in range(1, groups if ship else 1):
+        start = pl.multiple_of(partner(here, step, groups) * per, rows)
+        kept_in.append(
+            pltpu.make_async_copy(
+                basis.at[:, :, pl.ds(start, held.shape[3]), :], held.at[step - 1], sems.at[1 + step]
+            )
+        )
+    for copy in (links_in, fields, *kept_in):
+        copy.start()
     lattice.masks()
+    links_in.wait()
+    fields.wait()
 
     def body(vector, carry):
-        pack_rim(lattice, load_spinor(psi, vector), links, ahead_ref, behind_ref, vector)
+        pack_rim(lattice, load_spinor(psi, vector), links, 0, ahead_ref, behind_ref, vector)
         return carry
 
     lax.fori_loop(0, vectors, body, 0)
+    for step, copy in enumerate(kept_in):
+        copy.wait()
+
+        def turn(group, carry, step=step):
+            first = pl.multiple_of(group * 8, 8)
+            for ri in range(2):
+                for start in range(0, ship, rows):
+                    tile = held[step, pl.ds(first, 8), ri, start : start + rows, :]
+                    tile = jnp.swapaxes(tile, 0, 1)
+                    size = min(rows, ship - start)
+                    pieces[step][start : start + size, pl.ds(ri * kept + first, 8), :] = tile[:size]
+            return carry
+
+        lax.fori_loop(0, kept // 8, turn, 0)
+
+
+def basis_kernel(rows, kept, basis, out):
+    def body(tile, carry):
+        blocks = pl.ds(pl.multiple_of(tile * rows, rows), rows)
+        for ri in range(2):
+            for first in range(0, kept, 16):
+                value = jnp.swapaxes(basis[first : first + 16, ri, blocks, :], 0, 1)
+                high, low = two_halves(value)
+                start = ri * kept + first
+                out[blocks, start : start + 16, :] = high
+                out[blocks, 2 * kept + start : 2 * kept + start + 16, :] = low
+        return carry
+
+    lax.fori_loop(0, basis.shape[2] // rows, body, 0)
 
 
 def local_kernel(lattice, vectors, psi, links, clover, out):
@@ -249,7 +300,7 @@
             out[place] = value
 
         finish(lattice, links, part, rim_ahead, rim_behind, vector, signs, store)
-        pack_rim(lattice, load_spinor(out, vector), links, ahead_ref, behind_ref, vector)
+        pack_rim(lattice, load_spinor(out, vector), links, 3, ahead_ref, behind_ref, vector)
         return carry
 
     lax.fori_loop(0, vectors, body, 0)
@@ -260,28 +311,16 @@
     return high, (value - high.astype(jnp.float32)).astype(jnp.bfloat16)
 
 
-def basis_kernel(groups, kept, blocks, basis, out):
-    per = blocks // groups
-
-    def body(block, carry):
-        rows = jnp.concatenate(
-            [
-                basis[pl.ds(block, kept, stride=2 * blocks), :],
-                basis[pl.ds(blocks + block, kept, stride=2 * blocks), :],
-            ],
-            axis=0,
-        )
-        high, low = two_halves(rows)
-        lanes = pl.ds(pl.multiple_of(block % per * LANES, LANES), LANES)
-        out[block // per, : 2 * kept, lanes] = high
-        out[block // per, 2 * kept :, lanes] = low
-        return carry
-
-    lax.fori_loop(0, blocks, body, 0, unroll=2)
+def pair_of(ref, block):
+    return jnp.concatenate([ref[block], ref[block + 1]], axis=1)
+
+
+def row_pairs(ref, block):
+    return jnp.concatenate(two_halves(pair_of(ref, block)), axis=0)
 
 
 def correlate_kernel(
-    lattice, groups, vectors, kept, blocks, scale,
+    lattice, vectors, kept, scale,
     part, links, rim_ahead, rim_behind, basis, applied, over, field,
 ):
     lattice.masks()
@@ -290,32 +329,33 @@
 
     def body(vector, carry):
         def store(place, value):
-            start = place * rows
-            field[pl.ds(start if isinstance(start, int) else pl.multiple_of(start, rows), rows), :] = value
+            field[place] = value
 
         finish(lattice, links, part, rim_ahead, rim_behind, vector, signs, store)
         return carry
 
     lax.fori_loop(0, vectors, body, 0)
-    per = blocks // groups
-
-    def relay(block, carry):
-        lanes = pl.ds(pl.multiple_of(block % per * LANES, LANES), LANES)
+
+    def add(comp, total):
+        blocks_here = pl.ds(pl.multiple_of(comp * rows, rows), rows)
         for ri in range(2):
-            start = ri * blocks + block
-            applied[block // per, ri * vectors : (ri + 1) * vectors, lanes] = field[
-                pl.ds(start, vectors, stride=2 * blocks), :
-            ]
-        return carry
-
-    lax.fori_loop(0, blocks, relay, 0, unroll=2)
-    total = None
-    for group in range(groups):
-        both = jnp.concatenate(two_halves(applied[group]), axis=0)
-        term = lax.dot_general(
-            both, basis[group], (((1,), (1,)), ((), ())), preferred_element_type=jnp.float32
-        )
-        total = term if total is None else total + term
+            for first in range(0, vectors, 8):
+                tiles = jnp.stack(
+                    [field[(first + i) * 2 * COMPS + ri * COMPS + comp] for i in range(8)]
+                )
+                start = ri * vectors + first
+                applied[blocks_here, start : start + 8, :] = jnp.swapaxes(tiles, 0, 1)
+        for place in range(0, rows, 2):
+            block = comp * rows + place
+            total = total + lax.dot_general(
+                row_pairs(applied, block),
+                pair_of(basis, block),
+                (((1,), (1,)), ((), ())),
+                preferred_element_type=jnp.float32,
+            )
+        return total
+
+    total = lax.fori_loop(0, COMPS, add, jnp.zeros((4 * vectors, 4 * kept), jnp.float32))
     total = total[: 2 * vectors] + total[2 * vectors :]
     total = total[:, : 2 * kept] + total[:, 2 * kept :]
     real, imag = total[:vectors], total[vectors:]
@@ -344,14 +384,20 @@
     return out
 
 
-def summed(value, axis):
+def summed(value, axis, radix):
     count = lax.axis_size(axis)
     if count & (count - 1):
         return lax.psum(value, axis)
-    step = 1
-    while step < count:
-        value = value + lax.ppermute(value, axis, [(i, i ^ step) for i in range(count)])
-        step *= 2
+    stride = 1
+    while stride < count:
+        size, radix = min(radix[0], count // stride), radix[1:] or radix
+        total = value
+        for step in range(1, size):
+            total = total + lax.ppermute(
+                value, axis, [(i, i ^ (step * stride)) for i in range(count)]
+            )
+        value = total
+        stride *= size
     return value
 
 
@@ -371,63 +417,50 @@
     return both[:half] + both[half:]
 
 
-def slice_kernel(groups, rows, ship, basis, *outs):
+def project_kernel(groups, vectors, kept, ship, over, basis, *outs):
     here = lax.axis_index("ba")
-    per = basis.shape[1] // groups
-    for step in range(1, groups):
-        start = pl.multiple_of(partner(here, step, groups) * per, rows)
-        outs[step - 1][...] = basis[:, pl.ds(start, ship), :]
-
-
-def relay_kernel(kept, blocks, *refs):
-    count = len(refs) // 2
-    for part, out in zip(refs[:count], refs[count:]):
-
-        def body(block, carry, part=part, out=out):
-            lanes = pl.ds(pl.multiple_of(block * LANES, LANES), LANES)
-            for ri in range(2):
-                high, low = two_halves(part[pl.ds(ri * blocks + block, kept, stride=2 * blocks), :])
-                out[ri * kept : (ri + 1) * kept, lanes] = high
-                out[(2 + ri) * kept : (3 + ri) * kept, lanes] = low
-            return carry
-
-        lax.fori_loop(0, blocks, body, 0, unroll=2)
-
-
-def project_kernel(groups, vectors, kept, shipped, over, basis, *outs):
-    here = lax.axis_index("ba")
+    per = basis.shape[0] // groups
     weight = weight_rows(over[:vectors, :], over[vectors:, :])
     for step in range(groups):
-        other = partner(here, step, groups)
-        value = weighted(weight, basis[other, :, shipped:])
-        width = value.shape[1]
-        outs[step][:, :width] = value
-        outs[step][:, width:] = jnp.zeros((2 * vectors, LANES), jnp.float32)
-        outs[step][:, width : width + kept] = over[...]
-
-
-def rest_kernel(groups, vectors, kept, shipped, scale, over, basis, applied, *refs):
+        first = partner(here, step, groups) * per + ship
+        for block in range(0, per - ship, 2):
+            value = weighted(weight, pair_of(basis, first + block))
+            outs[step][block] = value[:, :LANES]
+            outs[step][block + 1] = value[:, LANES:]
+        outs[step][per - ship] = jnp.zeros((2 * vectors, LANES), jnp.float32)
+        outs[step][per - ship, :, :kept] = over[...]
+
+
+def rest_kernel(groups, vectors, kept, ship, scale, over, basis, applied, *refs):
     parts, refs = refs[:groups], refs[groups:]
     pieces, (rest_ref, gram) = refs[:-2], refs[-2:]
     here = lax.axis_index("ba")
-    width = parts[0].shape[1] - LANES
-    total = parts[0][:, :width]
+    per = basis.shape[0] // groups
+    weights = [weight_rows(over[:vectors, :], over[vectors:, :])]
     for part in parts[1:]:
-        total = total + part[:, :width]
-    if shipped:
-        head = weighted(
-            weight_rows(over[:vectors, :], over[vectors:, :]), basis[here, :, :shipped]
+        there = part[per - ship, :, :kept]
+        weights.append(weight_rows(there[:vectors], there[vectors:]))
+    full = None
+    for block in range(0, per, 2):
+        mine = here * per + block
+        if block < ship:
+            total = weighted(weights[0], pair_of(basis, mine))
+            for weight, piece in zip(weights[1:], pieces):
+                total = total + weighted(weight, row_pairs(piece, block))
+        else:
+            total = [
+                sum((part[block + i - ship] for part in parts[1:]), parts[0][block + i - ship])
+                for i in range(2)
+            ]
+            total = jnp.concatenate(total, axis=1)
+        rest = pair_of(applied, mine) - total
+        rest_ref[block] = rest[:, :LANES]
+        rest_ref[block + 1] = rest[:, LANES:]
+        both = jnp.concatenate(two_halves(rest), axis=0)
+        term = lax.dot_general(
+            both, both, (((1,), (1,)), ((), ())), preferred_element_type=jnp.float32
         )
-        for part, piece in zip(parts[1:], pieces):
-            there = part[:, width : width + kept]
-            head = head + weighted(weight_rows(there[:vectors], there[vectors:]), piece[...])
-        total = jnp.concatenate([head, total], axis=1)
-    rest = applied[here] - total
-    rest_ref[...] = rest
-    both = jnp.concatenate(two_halves(rest), axis=0)
-    full = lax.dot_general(
-        both, both, (((1,), (1,)), ((), ())), preferred_element_type=jnp.float32
-    )
+        full = term if full is None else full + term
     full = full[: 2 * vectors] + full[2 * vectors :]
     full = full[:, : 2 * vectors] + full[:, 2 * vectors :]
     real, imag = full[:vectors], full[vectors:]
@@ -456,13 +489,17 @@
         im = jnp.where(below, new_im, jnp.where(row == pivot, row_im, im))
     inv_re, inv_im = re[:, vectors:], im[:, vectors:]
     weight = weight_rows(inv_re, -inv_im)
-    both = jnp.concatenate(two_halves(rest[...]), axis=0)
-    full = weighted(weight, both)
     own = vectors // groups
-    for group in range(groups):
-        for ri in range(2):
-            start = ri * vectors + group * own
-            work[group, ri * own : (ri + 1) * own, :] = full[start : start + own]
+    for block in range(0, rest.shape[0], 2):
+        full = weighted(weight, row_pairs(rest, block))
+        for i in range(2):
+            value = full[:, i * LANES : (i + 1) * LANES]
+            for group in range(groups):
+                for ri in range(2):
+                    start = ri * vectors + group * own
+                    work[group, block + i, ri * own : (ri + 1) * own, :] = value[
+                        start : start + own
+                    ]
     for step in range(groups):
         outs[step][...] = work[partner(here, step, groups)]
 
@@ -475,17 +512,18 @@
         first = source(here, step, groups) * per
         for block in range(per):
             for ri in range(2):
-                value = parts[step][ri * own : (ri + 1) * own, block * LANES : (block + 1) * LANES]
+                value = parts[step][block, ri * own : (ri + 1) * own, :]
                 out[pl.ds(first + block + ri * blocks, own, stride=2 * blocks), :] = value
 
 
-def call(kernel, outs, *args, scratch=(), flops=0, grant=6):
+def call(kernel, outs, *args, scratch=(), flops=0, grant=6, remote=()):
     nbytes = sum(a.size * a.dtype.itemsize for a in (*args, *outs))
     spec = pl.BlockSpec(memory_space=pltpu.VMEM)
+    anywhere = pl.BlockSpec(memory_space=pltpu.HBM)
     return pl.pallas_call(
         kernel,
         out_shape=tuple(outs),
-        in_specs=[spec] * len(args),
+        in_specs=[anywhere if i in remote else spec for i in range(len(args))],
         out_specs=tuple([spec] * len(outs)),
         scratch_shapes=list(scratch),
         compiler_params=pltpu.CompilerParams(vmem_limit_bytes=grant << 20),
@@ -514,12 +552,11 @@
     own = vectors // groups
     scale = 1.0 / (2 * COMPS * slices * sites * places)
     psi = tiles_of(search_block, vectors * 2 * COMPS)
-    basis = tiles_of(kept_basis, kept * 2 * COMPS).reshape(kept * 2 * blocks, LANES)
-    ahead_comps = 2 * (COMPS // groups) // 3 if COMPS % groups == 0 else 0
-    ship = ahead_comps * rows
-    shipped = ship * LANES
+    basis = tiles_of(kept_basis, kept * 2 * COMPS).reshape(kept, 2, blocks, LANES)
+    ship = per // 2 if per % rows == 0 else 0
     links = tiles_of(gauge_links, 72)
     clover = tiles_of(clover_term, 144)
+    local = functools.partial(local_kernel, lattice, vectors)
     rim = shape_of(vectors * COMPS // slices, rows, LANES)
     field = shape_of(vectors * 2 * COMPS, rows, LANES)
     work = vectors * rows * LANES
@@ -529,25 +566,28 @@
         up = [(i, (i + 1) % places) for i in range(places)]
         return lax.ppermute(ahead, "ta", down), lax.ppermute(behind, "ta", up)
 
-    ahead, behind = call(
-        functools.partial(pack_kernel, lattice, vectors), (rim, rim), psi, links, flops=200 * work
+    ahead, behind, *pieces = call(
+        functools.partial(open_kernel, lattice, groups, vectors, kept, ship),
+        (rim, rim) + (shape_of(max(ship, 1), 2 * kept, LANES),) * (groups - 1),
+        psi,
+        links,
+        basis,
+        scratch=[
+            pltpu.VMEM(psi.shape, jnp.float32),
+            pltpu.VMEM((18, rows, LANES), jnp.float32),
+            pltpu.VMEM((groups - 1, kept, 2, -(-ship // rows) * rows or rows, LANES), jnp.float32),
+            pltpu.SemaphoreType.DMA((groups + 1,)),
+        ],
+        flops=200 * work,
+        grant=60,
+        remote=(0, 1, 2),
     )
     rims = swap(ahead, behind)
-    pieces = []
     if ship:
-        pieces = call(
-            functools.partial(slice_kernel, groups, rows, ship),
-            (shape_of(2 * kept, ship, LANES),) * (groups - 1),
-            basis.reshape(2 * kept, blocks, LANES),
-        )
         pieces = exchanged([None, *pieces], "ba")[1:]
-    local = functools.partial(local_kernel, lattice, vectors)
+    else:
+        pieces = []
     (part,) = call(local, (field,), psi, links, clover, flops=2000 * work)
-    (rows_of_basis,) = call(
-        functools.partial(basis_kernel, groups, kept, blocks),
-        (jax.ShapeDtypeStruct((groups, 4 * kept, per * LANES), jnp.bfloat16),),
-        basis,
-    )
     first, ahead, behind = call(
         functools.partial(middle_kernel, lattice, vectors),
         (field, rim, rim),
@@ -558,47 +598,46 @@
     )
     rims = swap(ahead, behind)
     (part,) = call(local, (field,), first, links, clover, flops=2000 * work)
+    (basis_rows,) = call(
+        functools.partial(basis_kernel, rows, kept),
+        (jax.ShapeDtypeStruct((blocks, 4 * kept, LANES), jnp.bfloat16),),
+        basis,
+    )
     applied, over = call(
-        functools.partial(correlate_kernel, lattice, groups, vectors, kept, blocks, scale),
-        (shape_of(groups, 2 * vectors, per * LANES), shape_of(2 * vectors, kept)),
+        functools.partial(correlate_kernel, lattice, vectors, kept, scale),
+        (shape_of(blocks, 2 * vectors, LANES), shape_of(2 * vectors, kept)),
         part,
         links,
         *rims,
-        rows_of_basis,
-        scratch=[pltpu.VMEM((vectors * 2 * blocks, LANES), jnp.float32)],
+        basis_rows,
+        scratch=[pltpu.VMEM(psi.shape, jnp.float32)],
         flops=400 * work,
     )
-    over = summed(over, "ta")
+    over = summed(over, "ta", (2, 4))
     parts = call(
-        functools.partial(project_kernel, groups, vectors, kept, shipped),
-        (shape_of(2 * vectors, (per + 1) * LANES - shipped),) * groups,
+        functools.partial(project_kernel, groups, vectors, kept, ship),
+        (shape_of(per - ship + 1, 2 * vectors, LANES),) * groups,
         over,
-        rows_of_basis,
+        basis_rows,
     )
     parts = exchanged(parts, "ba")
-    if ship:
-        pieces = call(
-            functools.partial(relay_kernel, kept, ship),
-            (jax.ShapeDtypeStruct((4 * kept, shipped), jnp.bfloat16),) * (groups - 1),
-            *(piece.reshape(2 * kept * ship, LANES) for piece in pieces),
-        )
     rest, gram = call(
-        functools.partial(rest_kernel, groups, vectors, kept, shipped, scale),
-        (shape_of(2 * vectors, per * LANES), shape_of(vectors, 2 * vectors)),
+        functools.partial(rest_kernel, groups, vectors, kept, ship, scale),
+        (shape_of(per, 2 * vectors, LANES), shape_of(vectors, 2 * vectors)),
         over,
-        rows_of_basis,
+        basis_rows,
         applied,
         *parts,
         *pieces,
     )
-    gram = summed(summed(gram, "ta"), "ba")
-    piece = shape_of(2 * own, per * LANES)
+    gram = summed(summed(gram, "ta", (2, 4)), "ba", (4,))
+    piece = shape_of(per, 2 * own, LANES)
     pieces = call(
         functools.partial(ortho_kernel, groups, vectors),
         (piece,) * groups,
         gram,
         rest,
-        scratch=[pltpu.VMEM((groups, 2 * own, per * LANES), jnp.float32)],
+        scratch=[pltpu.VMEM((groups, per, 2 * own, LANES), jnp.float32)],
     )
     pieces = exchanged(pieces, "ba")
     (ortho,) = call(

time: 110 us -> 122 us (1.11)
  waiting for transfers between devices: 49.8 us -> 64.1 us
  local copies, waits for them, and re-layouts: 4.27 us -> 0.04 us
  starting transfers between devices: 31.6 us -> 33.3 us
    ppermute x9, waiting for transfers between devices: 33.5 us -> 47.1 us  [exchanged(): out.append(lax.ppermute(values[step], axis, pairs))]
    ppermute x4, waiting for transfers between devices: 1.94 us -> 8.79 us  [swap(): return (lax.ppermute(ahead, 'ta', down), lax.ppermute(behind, 'ta', up))]
    ppermute x8 -> x11, waiting for transfers between devices: 14.3 us -> 8.28 us  [summed(): lax.ppermute(value, axis, [(i, i ^ step * stride) for i in range(count)])]
    unnamed x16, local copies, waits for them, and re-layouts: 4.27 us -> 0.04 us
    ppermute x8 -> x11, starting transfers between devices: 12.7 us -> 13.7 us  [summed(): lax.ppermute(value, axis, [(i, i ^ step * stride) for i in range(count)])]
    pallas_call x12 -> x10, Pallas kernels: 23.6 us -> 23.2 us  [call(): pl.pallas_call(kernel, out_shape=tuple(outs), in_specs=[anywhere if i in...]
  transfers between devices with their start and end apart: 21 -> 24, of which waited for: 14 -> 16; matrix products, arithmetic and copies ran while one was open for 0% -> 0% of each run, Pallas kernels for 17% -> 12%
where the time goes in v3:
time: 122 us
  waiting for transfers between devices  64.1 us (53%)
  starting transfers between devices  33.3 us (27%)
  Pallas kernels  23.2 us (19%)
    ppermute x9, waiting for transfers between devices, exchanged(): out.append(lax.ppermute(values[step], axis, pairs))  47.1 us
    pallas_call x10, Pallas kernels, call(): pl.pallas_call(kernel, out_shape=tuple(outs), in_specs=[anywhere if i in...  23.2 us
    ppermute x9, starting transfers between devices, exchanged(): out.append(lax.ppermute(values[step], axis, pairs))  15.3 us
    ppermute x11, starting transfers between devices, summed(): lax.ppermute(value, axis, [(i, i ^ step * stride) for i in range(count)])  13.7 us
    ppermute x4, waiting for transfers between devices, swap(): return (lax.ppermute(ahead, 'ta', down), lax.ppermute(behind, 'ta', up))  8.79 us
    ppermute x11, waiting for transfers between devices, summed(): lax.ppermute(value, axis, [(i, i ^ step * stride) for i in range(count)])  8.28 us
    ppermute x4, starting transfers between devices, swap(): return (lax.ppermute(ahead, 'ta', down), lax.ppermute(behind, 'ta', up))  4.36 us
  transfers between devices with their start and end apart: 24, of which 16 were waited for; matrix products, arithmetic and copies ran while one was open for 0% of the time, Pallas kernels for 12%

profile of v3, /device:TPU:0, one launch (start us, length us, event | category | flops | bytes accessed | tf_op | source)
XLA Modules:
  0.0 121.6 jit_solution(1750783253367657212)
XLA Ops:
  0.7 3.7 %shard_map.60 = (f32[96,8,128]{2,1,0:T(8,128)}, f32[96,8,128]{2,1,0:T(8,128)}, f32[12,64,128]{2,1,0:T(8,128)}, f32[12,64,128]{2,1,0:T(8,128)}, f32[12,64,128]{2,1,0:T(8,128)}) custom-call(f32[384,8,128]{2,1,0:T(8,128)} %bitcast.35, f32[72,8,128]{2,1,0:T(8,128)} %bitcast.30, f32[32,2,96,128]{3,2,1,0:T(8,128)} %bitcast.28), custom_call_target="tpu_custom_call" | custom-call | flops 3276800 | bytes 6979584 | tf_op jit(solution)/shard_map/pallas_call | solution.py:523
  4.3 3.4 %collective-permute-start = (f32[96,8,128]{2,1,0:T(8,128)}, f32[96,8,128]{2,1,0:T(8,128)S(1)}, u32[]{:S(2)}, u32[]{:S(2)}) collective-permute-start(f32[96,8,128]{2,1,0:T(8,128)} %get-tuple-element.22), channel_id=1, source_target_pairs={{0,28},{4,0},{8,4},{12,8},{16,12},{20,16},{24,20},{28,24},{1,29},{... | collective-permute-start | bytes 1179656 | tf_op jit(solution)/shard_map/ppermute | solution.py:567
  7.8 4.9 %shard_map.59.part = f32[384,8,128]{2,1,0:T(8,128)S(1)} custom-call(f32[384,8,128]{2,1,0:T(8,128)S(1)} %bitcast.36, f32[72,8,128]{2,1,0:T(8,128)S(1)} %bitcast.31, f32[144,8,128]{2,1,0:T(8,128)S(1)} %bitcast.37), custom_call_target="tpu_custom_call" | custom-call | flops 32768000 | bytes 4030464 | tf_op jit(solution)/shard_map/pallas_call | solution.py:523
  12.7 4.0 %collective-permute-done.rim_ahead = f32[96,8,128]{2,1,0:T(8,128)S(1)} collective-permute-done((f32[96,8,128]{2,1,0:T(8,128)}, f32[96,8,128]{2,1,0:T(8,128)S(1)}, u32[]{:S(2)}, u32[]{:S(2)}) %collective-permute-start) | collective-permute-done | bytes 393248 | tf_op jit(solution)/shard_map/ppermute | solution.py:567
  16.7 1.8 %collective-permute-done.1.rim_behind = f32[96,8,128]{2,1,0:T(8,128)S(1)} collective-permute-done((f32[96,8,128]{2,1,0:T(8,128)}, f32[96,8,128]{2,1,0:T(8,128)S(1)}, u32[]{:S(2)}, u32[]{:S(2)}) %collective-permute-start.1) | collective-permute-done | bytes 393248 | tf_op jit(solution)/shard_map/ppermute | solution.py:567
  23.0 4.9 %shard_map.62.part = f32[384,8,128]{2,1,0:T(8,128)S(1)} custom-call(f32[384,8,128]{2,1,0:T(8,128)S(1)} %get-tuple-element.24.psi, f32[72,8,128]{2,1,0:T(8,128)S(1)} %bitcast.33, f32[144,8,128]{2,1,0:T(8,128)S(1)} %bitcast.38), custom_call_target="tpu_custom_call" | custom-call | flops 32768000 | bytes 4030464 | tf_op jit(solution)/shard_map/pallas_call | solution.py:523
  28.9 2.0 %collective-permute-done.3.rim_behind = f32[96,8,128]{2,1,0:T(8,128)S(1)} collective-permute-done((f32[96,8,128]{2,1,0:T(8,128)S(1)}, f32[96,8,128]{2,1,0:T(8,128)S(1)}, u32[]{:S(2)}, u32[]{:S(2)}) %collective-permute-start.3) | collective-permute-done | bytes 393248 | tf_op jit(solution)/shard_map/ppermute | solution.py:567
  30.9 3.3 %shard_map.64 = (f32[96,32,128]{2,1,0:T(8,128)S(1)}, f32[32,32]{1,0:T(8,128)S(1)}) custom-call(f32[384,8,128]{2,1,0:T(8,128)S(1)} %shard_map.62.part, f32[72,8,128]{2,1,0:T(8,128)S(1)} %bitcast.34, f32[96,8,128]{2,1,0:T(8,128)S(1)} %collective-permute-done.2.rim_ahead, f32[96,8,128]{2,1,0:T(8,128)S(1)} %collective-permute-done.3.rim_behind, ...), custom_call_target="tpu_custom_call" | custom-call | flops 6553600 | bytes 7376896 | tf_op jit(solution)/shard_map/pallas_call | solution.py:523
  36.3 1.6 %collective-permute-start.6 = (f32[32,32]{1,0:T(8,128)S(1)}, f32[32,32]{1,0:T(8,128)S(1)}, u32[]{:S(2)}, u32[]{:S(2)}) collective-permute-start(f32[32,32]{1,0:T(8,128)S(1)} %add.33), channel_id=1, source_target_pairs={{0,16},{4,20},{8,24},{12,28},{16,0},{20,4},{24,8},{28,12},{1,17},{... | collective-permute-start | bytes 12296 | tf_op jit(solution)/shard_map/ppermute | solution.py:396
  39.0 2.6 %collective-permute-start.12 = (f32[12,64,128]{2,1,0:T(8,128)S(1)}, f32[12,64,128]{2,1,0:T(8,128)S(1)}, u32[]{:S(2)}, u32[]{:S(2)}) collective-permute-start(f32[12,64,128]{2,1,0:T(8,128)S(1)} %copy-done.6), channel_id=1, source_target_pairs={{0,2},{1,3},{2,0},{3,1},{4,6},{5,7},{6,4},{7,5},{8,10},{9,11},{10,... | collective-permute-start | bytes 1179656 | tf_op jit(solution)/shard_map/ppermute | solution.py:383
  41.6 2.3 %collective-permute-start.13 = (f32[12,64,128]{2,1,0:T(8,128)S(1)}, f32[12,64,128]{2,1,0:T(8,128)S(1)}, u32[]{:S(2)}, u32[]{:S(2)}) collective-permute-start(f32[12,64,128]{2,1,0:T(8,128)S(1)} %copy-done.5), channel_id=1, source_target_pairs={{0,3},{1,2},{2,1},{3,0},{4,7},{5,6},{6,5},{7,4},{8,11},{9,10},{10,... | collective-permute-start | bytes 1179656 | tf_op jit(solution)/shard_map/ppermute | solution.py:383
  44.4 2.1 %collective-permute-start.9 = (f32[13,32,128]{2,1,0:T(8,128)S(1)}, f32[13,32,128]{2,1,0:T(8,128)S(1)}, u32[]{:S(2)}, u32[]{:S(2)}) collective-permute-start(f32[13,32,128]{2,1,0:T(8,128)S(1)} %get-tuple-element.31), channel_id=1, source_target_pairs={{0,2},{1,3},{2,0},{3,1},{4,6},{5,7},{6,4},{7,5},{8,10},{9,11},{10,... | collective-permute-start | bytes 638984 | tf_op jit(solution)/shard_map/ppermute | solution.py:383
  46.6 2.2 %collective-permute-start.10 = (f32[13,32,128]{2,1,0:T(8,128)S(1)}, f32[13,32,128]{2,1,0:T(8,128)S(1)}, u32[]{:S(2)}, u32[]{:S(2)}) collective-permute-start(f32[13,32,128]{2,1,0:T(8,128)S(1)} %get-tuple-element.32), channel_id=1, source_target_pairs={{0,3},{1,2},{2,1},{3,0},{4,7},{5,6},{6,5},{7,4},{8,11},{9,10},{10,... | collective-permute-start | bytes 638984 | tf_op jit(solution)/shard_map/ppermute | solution.py:383
  48.8 28.5 %collective-permute-done.12.refs_5_ = f32[12,64,128]{2,1,0:T(8,128)S(1)} collective-permute-done((f32[12,64,128]{2,1,0:T(8,128)S(1)}, f32[12,64,128]{2,1,0:T(8,128)S(1)}, u32[]{:S(2)}, u32[]{:S(2)}) %collective-permute-start.12) | collective-permute-done | bytes 393248 | tf_op jit(solution)/shard_map/ppermute | solution.py:383
  77.3 13.0 %collective-permute-done.9.refs_2_ = f32[13,32,128]{2,1,0:T(8,128)S(1)} collective-permute-done((f32[13,32,128]{2,1,0:T(8,128)S(1)}, f32[13,32,128]{2,1,0:T(8,128)S(1)}, u32[]{:S(2)}, u32[]{:S(2)}) %collective-permute-start.9) | collective-permute-done | bytes 213024 | tf_op jit(solution)/shard_map/ppermute | solution.py:383
  93.6 1.6 %collective-permute-start.16 = (f32[16,32]{1,0:T(8,128)S(1)}, f32[16,32]{1,0:T(8,128)S(1)}, u32[]{:S(2)}, u32[]{:S(2)}) collective-permute-start(f32[16,32]{1,0:T(8,128)S(1)} %add.37), channel_id=1, source_target_pairs={{0,16},{4,20},{8,24},{12,28},{16,0},{20,4},{24,8},{28,12},{1,17},{... | collective-permute-start | bytes 6152 | tf_op jit(solution)/shard_map/ppermute | solution.py:396
  97.3 1.6 %collective-permute-done.15 = f32[16,32]{1,0:T(8,128)S(1)} collective-permute-done((f32[16,32]{1,0:T(8,128)S(1)}, f32[16,32]{1,0:T(8,128)S(1)}, u32[]{:S(2)}, u32[]{:S(2)}) %collective-permute-start.15) | collective-permute-done | bytes 2080 | tf_op jit(solution)/shard_map/ppermute | solution.py:396
  98.9 2.5 %collective-permute-start.20 = (f32[16,32]{1,0:T(8,128)S(1)}, f32[16,32]{1,0:T(8,128)S(1)}, u32[]{:S(2)}, u32[]{:S(2)}) collective-permute-start(f32[16,32]{1,0:T(8,128)S(1)} %add_add_fusion.2), channel_id=1, source_target_pairs={{0,3},{1,2},{2,1},{3,0},{4,7},{5,6},{6,5},{7,4},{8,11},{9,10},{10,... | collective-permute-start | bytes 6152 | tf_op jit(solution)/shard_map/ppermute | solution.py:396
  101.4 3.6 %collective-permute-start.19 = (f32[16,32]{1,0:T(8,128)S(1)}, f32[16,32]{1,0:T(8,128)S(1)}, u32[]{:S(2)}, u32[]{:S(2)}) collective-permute-start(f32[16,32]{1,0:T(8,128)S(1)} %add_add_fusion.2), channel_id=1, source_target_pairs={{0,2},{1,3},{2,0},{3,1},{4,6},{5,7},{6,4},{7,5},{8,10},{9,11},{10,... | collective-permute-start | bytes 6152 | tf_op jit(solution)/shard_map/ppermute | solution.py:396
  106.7 2.0 %collective-permute-done.18 = f32[16,32]{1,0:T(8,128)S(1)} collective-permute-done((f32[16,32]{1,0:T(8,128)S(1)}, f32[16,32]{1,0:T(8,128)S(1)}, u32[]{:S(2)}, u32[]{:S(2)}) %collective-permute-start.18) | collective-permute-done | bytes 2080 | tf_op jit(solution)/shard_map/ppermute | solution.py:396
  108.7 1.9 %shard_map.67 = (f32[24,8,128]{2,1,0:T(8,128)S(1)}, f32[24,8,128]{2,1,0:T(8,128)S(1)}, f32[24,8,128]{2,1,0:T(8,128)S(1)}, f32[24,8,128]{2,1,0:T(8,128)S(1)}) custom-call(f32[16,32]{1,0:T(8,128)S(1)} %add_add_fusion.1.gram, f32[24,32,128]{2,1,0:T(8,128)S(1)} %get-tuple-element.37.rest), custom_call_target="tpu_custom_call" | custom-call | bytes 788480 | tf_op jit(solution)/shard_map/pallas_call | solution.py:523
  112.0 2.0 %collective-permute-start.22 = (f32[24,8,128]{2,1,0:T(8,128)S(1)}, f32[24,8,128]{2,1,0:T(8,128)S(1)}, u32[]{:S(2)}, u32[]{:S(2)}) collective-permute-start(f32[24,8,128]{2,1,0:T(8,128)S(1)} %get-tuple-element.40), channel_id=1, source_target_pairs={{0,2},{1,3},{2,0},{3,1},{4,6},{5,7},{6,4},{7,5},{8,10},{9,11},{10,... | collective-permute-start | bytes 294920 | tf_op jit(solution)/shard_map/ppermute | solution.py:383
  116.6 2.1 %collective-permute-done.22.refs_2_ = f32[24,8,128]{2,1,0:T(8,128)S(1)} collective-permute-done((f32[24,8,128]{2,1,0:T(8,128)S(1)}, f32[24,8,128]{2,1,0:T(8,128)S(1)}, u32[]{:S(2)}, u32[]{:S(2)}) %collective-permute-start.22) | collective-permute-done | bytes 98336 | tf_op jit(solution)/shard_map/ppermute | solution.py:383
  118.7 1.9 %collective-permute-done.23.refs_3_ = f32[24,8,128]{2,1,0:T(8,128)S(1)} collective-permute-done((f32[24,8,128]{2,1,0:T(8,128)S(1)}, f32[24,8,128]{2,1,0:T(8,128)S(1)}, u32[]{:S(2)}, u32[]{:S(2)}) %collective-permute-start.23) | collective-permute-done | bytes 98336 | tf_op jit(solution)/shard_map/ppermute | solution.py:383
  (55 shorter events, 21.0 us)
Async XLA Ops:
  4.3 12.3 %collective-permute-start = (f32[96,8,128]{2,1,0:T(8,128)}, f32[96,8,128]{2,1,0:T(8,128)S(1)}, u32[]{:S(2)}, u32[]{:S(2)}) collective-permute-start(f32[96,8,128]{2,1,0:T(8,128)} %get-tuple-element.22), channel_id=1, source_target_pairs={{0,28},{4,0},{8,4},{12,8},{16,12},{20,16},{24,20},{28,24},{1,29},{... | collective-permute-start | bytes 1179656 | tf_op jit(solution)/shard_map/ppermute | solution.py:567
  7.7 10.7 %collective-permute-start.1 = (f32[96,8,128]{2,1,0:T(8,128)}, f32[96,8,128]{2,1,0:T(8,128)S(1)}, u32[]{:S(2)}, u32[]{:S(2)}) collective-permute-start(f32[96,8,128]{2,1,0:T(8,128)} %get-tuple-element.23), channel_id=1, source_target_pairs={{0,4},{4,8},{8,12},{12,16},{16,20},{20,24},{24,28},{28,0},{1,5},{5... | collective-permute-start | bytes 1179656 | tf_op jit(solution)/shard_map/ppermute | solution.py:567
  19.5 9.4 %collective-permute-start.2 = (f32[96,8,128]{2,1,0:T(8,128)S(1)}, f32[96,8,128]{2,1,0:T(8,128)S(1)}, u32[]{:S(2)}, u32[]{:S(2)}) collective-permute-start(f32[96,8,128]{2,1,0:T(8,128)S(1)} %get-tuple-element.25), channel_id=1, source_target_pairs={{0,28},{4,0},{8,4},{12,8},{16,12},{20,16},{24,20},{28,24},{1,29},{... | collective-permute-start | bytes 1179656 | tf_op jit(solution)/shard_map/ppermute | solution.py:567
  20.5 10.5 %collective-permute-start.3 = (f32[96,8,128]{2,1,0:T(8,128)S(1)}, f32[96,8,128]{2,1,0:T(8,128)S(1)}, u32[]{:S(2)}, u32[]{:S(2)}) collective-permute-start(f32[96,8,128]{2,1,0:T(8,128)S(1)} %get-tuple-element.26), channel_id=1, source_target_pairs={{0,4},{4,8},{8,12},{12,16},{16,20},{20,24},{24,28},{28,0},{1,5},{5... | collective-permute-start | bytes 1179656 | tf_op jit(solution)/shard_map/ppermute | solution.py:567
  20.5 26.1 %collective-permute-start.11 = (f32[12,64,128]{2,1,0:T(8,128)S(1)}, f32[12,64,128]{2,1,0:T(8,128)S(1)}, u32[]{:S(2)}, u32[]{:S(2)}) collective-permute-start(f32[12,64,128]{2,1,0:T(8,128)S(1)} %copy-done.7), channel_id=1, source_target_pairs={{0,1},{1,0},{2,3},{3,2},{4,5},{5,4},{6,7},{7,6},{8,9},{9,8},{10,11... | collective-permute-start | bytes 1179656 | tf_op jit(solution)/shard_map/ppermute | solution.py:383
  34.3 1.2 collective-permute-start.4
  35.5 6.1 %collective-permute-start.7 = (f32[32,32]{1,0:T(8,128)S(1)}, f32[32,32]{1,0:T(8,128)S(1)}, u32[]{:S(2)}, u32[]{:S(2)}) collective-permute-start(f32[32,32]{1,0:T(8,128)S(1)} %add.33), channel_id=1, source_target_pairs={{0,24},{4,28},{8,16},{12,20},{16,8},{20,12},{24,0},{28,4},{1,25},{... | collective-permute-start | bytes 12296 | tf_op jit(solution)/shard_map/ppermute | solution.py:396
  36.3 7.5 %collective-permute-start.6 = (f32[32,32]{1,0:T(8,128)S(1)}, f32[32,32]{1,0:T(8,128)S(1)}, u32[]{:S(2)}, u32[]{:S(2)}) collective-permute-start(f32[32,32]{1,0:T(8,128)S(1)} %add.33), channel_id=1, source_target_pairs={{0,16},{4,20},{8,24},{12,28},{16,0},{20,4},{24,8},{28,12},{1,17},{... | collective-permute-start | bytes 12296 | tf_op jit(solution)/shard_map/ppermute | solution.py:396
  38.0 5.9 %collective-permute-start.5 = (f32[32,32]{1,0:T(8,128)S(1)}, f32[32,32]{1,0:T(8,128)S(1)}, u32[]{:S(2)}, u32[]{:S(2)}) collective-permute-start(f32[32,32]{1,0:T(8,128)S(1)} %add.33), channel_id=1, source_target_pairs={{0,8},{4,12},{8,0},{12,4},{16,24},{20,28},{24,16},{28,20},{1,9},{5... | collective-permute-start | bytes 12296 | tf_op jit(solution)/shard_map/ppermute | solution.py:396
  39.0 38.3 %collective-permute-start.12 = (f32[12,64,128]{2,1,0:T(8,128)S(1)}, f32[12,64,128]{2,1,0:T(8,128)S(1)}, u32[]{:S(2)}, u32[]{:S(2)}) collective-permute-start(f32[12,64,128]{2,1,0:T(8,128)S(1)} %copy-done.6), channel_id=1, source_target_pairs={{0,2},{1,3},{2,0},{3,1},{4,6},{5,7},{6,4},{7,5},{8,10},{9,11},{10,... | collective-permute-start | bytes 1179656 | tf_op jit(solution)/shard_map/ppermute | solution.py:383
  41.6 35.7 %collective-permute-start.13 = (f32[12,64,128]{2,1,0:T(8,128)S(1)}, f32[12,64,128]{2,1,0:T(8,128)S(1)}, u32[]{:S(2)}, u32[]{:S(2)}) collective-permute-start(f32[12,64,128]{2,1,0:T(8,128)S(1)} %copy-done.5), channel_id=1, source_target_pairs={{0,3},{1,2},{2,1},{3,0},{4,7},{5,6},{6,5},{7,4},{8,11},{9,10},{10,... | collective-permute-start | bytes 1179656 | tf_op jit(solution)/shard_map/ppermute | solution.py:383
  44.3 33.0 %collective-permute-start.8 = (f32[13,32,128]{2,1,0:T(8,128)S(1)}, f32[13,32,128]{2,1,0:T(8,128)S(1)}, u32[]{:S(2)}, u32[]{:S(2)}) collective-permute-start(f32[13,32,128]{2,1,0:T(8,128)S(1)} %get-tuple-element.30), channel_id=1, source_target_pairs={{0,1},{1,0},{2,3},{3,2},{4,5},{5,4},{6,7},{7,6},{8,9},{9,8},{10,11... | collective-permute-start | bytes 638984 | tf_op jit(solution)/shard_map/ppermute | solution.py:383
  44.4 45.9 %collective-permute-start.9 = (f32[13,32,128]{2,1,0:T(8,128)S(1)}, f32[13,32,128]{2,1,0:T(8,128)S(1)}, u32[]{:S(2)}, u32[]{:S(2)}) collective-permute-start(f32[13,32,128]{2,1,0:T(8,128)S(1)} %get-tuple-element.31), channel_id=1, source_target_pairs={{0,2},{1,3},{2,0},{3,1},{4,6},{5,7},{6,4},{7,5},{8,10},{9,11},{10,... | collective-permute-start | bytes 638984 | tf_op jit(solution)/shard_map/ppermute | solution.py:383
  46.6 43.8 %collective-permute-start.10 = (f32[13,32,128]{2,1,0:T(8,128)S(1)}, f32[13,32,128]{2,1,0:T(8,128)S(1)}, u32[]{:S(2)}, u32[]{:S(2)}) collective-permute-start(f32[13,32,128]{2,1,0:T(8,128)S(1)} %get-tuple-element.32), channel_id=1, source_target_pairs={{0,3},{1,2},{2,1},{3,0},{4,7},{5,6},{6,5},{7,4},{8,11},{9,10},{10,... | collective-permute-start | bytes 638984 | tf_op jit(solution)/shard_map/ppermute | solution.py:383
  91.4 1.2 %collective-permute-start.14 = (f32[16,32]{1,0:T(8,128)S(1)}, f32[16,32]{1,0:T(8,128)S(1)}, u32[]{:S(2)}, u32[]{:S(2)}) collective-permute-start(f32[16,32]{1,0:T(8,128)S(1)} %get-tuple-element.36), channel_id=1, source_target_pairs={{0,4},{4,0},{8,12},{12,8},{16,20},{20,16},{24,28},{28,24},{1,5},{5... | collective-permute-start | bytes 6152 | tf_op jit(solution)/shard_map/ppermute | solution.py:396
  92.6 4.5 %collective-permute-start.17 = (f32[16,32]{1,0:T(8,128)S(1)}, f32[16,32]{1,0:T(8,128)S(1)}, u32[]{:S(2)}, u32[]{:S(2)}) collective-permute-start(f32[16,32]{1,0:T(8,128)S(1)} %add.37), channel_id=1, source_target_pairs={{0,24},{4,28},{8,16},{12,20},{16,8},{20,12},{24,0},{28,4},{1,25},{... | collective-permute-start | bytes 6152 | tf_op jit(solution)/shard_map/ppermute | solution.py:396
  93.6 3.7 %collective-permute-start.16 = (f32[16,32]{1,0:T(8,128)S(1)}, f32[16,32]{1,0:T(8,128)S(1)}, u32[]{:S(2)}, u32[]{:S(2)}) collective-permute-start(f32[16,32]{1,0:T(8,128)S(1)} %add.37), channel_id=1, source_target_pairs={{0,16},{4,20},{8,24},{12,28},{16,0},{20,4},{24,8},{28,12},{1,17},{... | collective-permute-start | bytes 6152 | tf_op jit(solution)/shard_map/ppermute | solution.py:396
  95.2 3.7 %collective-permute-start.15 = (f32[16,32]{1,0:T(8,128)S(1)}, f32[16,32]{1,0:T(8,128)S(1)}, u32[]{:S(2)}, u32[]{:S(2)}) collective-permute-start(f32[16,32]{1,0:T(8,128)S(1)} %add.37), channel_id=1, source_target_pairs={{0,8},{4,12},{8,0},{12,4},{16,24},{20,28},{24,16},{28,20},{1,9},{5... | collective-permute-start | bytes 6152 | tf_op jit(solution)/shard_map/ppermute | solution.py:396
  98.9 6.6 %collective-permute-start.20 = (f32[16,32]{1,0:T(8,128)S(1)}, f32[16,32]{1,0:T(8,128)S(1)}, u32[]{:S(2)}, u32[]{:S(2)}) collective-permute-start(f32[16,32]{1,0:T(8,128)S(1)} %add_add_fusion.2), channel_id=1, source_target_pairs={{0,3},{1,2},{2,1},{3,0},{4,7},{5,6},{6,5},{7,4},{8,11},{9,10},{10,... | collective-permute-start | bytes 6152 | tf_op jit(solution)/shard_map/ppermute | solution.py:396
  101.4 5.3 %collective-permute-start.19 = (f32[16,32]{1,0:T(8,128)S(1)}, f32[16,32]{1,0:T(8,128)S(1)}, u32[]{:S(2)}, u32[]{:S(2)}) collective-permute-start(f32[16,32]{1,0:T(8,128)S(1)} %add_add_fusion.2), channel_id=1, source_target_pairs={{0,2},{1,3},{2,0},{3,1},{4,6},{5,7},{6,4},{7,5},{8,10},{9,11},{10,... | collective-permute-start | bytes 6152 | tf_op jit(solution)/shard_map/ppermute | solution.py:396
  105.0 3.7 %collective-permute-start.18 = (f32[16,32]{1,0:T(8,128)S(1)}, f32[16,32]{1,0:T(8,128)S(1)}, u32[]{:S(2)}, u32[]{:S(2)}) collective-permute-start(f32[16,32]{1,0:T(8,128)S(1)} %add_add_fusion.2), channel_id=1, source_target_pairs={{0,1},{1,0},{2,3},{3,2},{4,5},{5,4},{6,7},{7,6},{8,9},{9,8},{10,11... | collective-permute-start | bytes 6152 | tf_op jit(solution)/shard_map/ppermute | solution.py:396
  110.6 6.0 %collective-permute-start.21 = (f32[24,8,128]{2,1,0:T(8,128)S(1)}, f32[24,8,128]{2,1,0:T(8,128)S(1)}, u32[]{:S(2)}, u32[]{:S(2)}) collective-permute-start(f32[24,8,128]{2,1,0:T(8,128)S(1)} %get-tuple-element.39), channel_id=1, source_target_pairs={{0,1},{1,0},{2,3},{3,2},{4,5},{5,4},{6,7},{7,6},{8,9},{9,8},{10,11... | collective-permute-start | bytes 294920 | tf_op jit(solution)/shard_map/ppermute | solution.py:383
  112.0 6.6 %collective-permute-start.22 = (f32[24,8,128]{2,1,0:T(8,128)S(1)}, f32[24,8,128]{2,1,0:T(8,128)S(1)}, u32[]{:S(2)}, u32[]{:S(2)}) collective-permute-start(f32[24,8,128]{2,1,0:T(8,128)S(1)} %get-tuple-element.40), channel_id=1, source_target_pairs={{0,2},{1,3},{2,0},{3,1},{4,6},{5,7},{6,4},{7,5},{8,10},{9,11},{10,... | collective-permute-start | bytes 294920 | tf_op jit(solution)/shard_map/ppermute | solution.py:383
  114.1 6.5 %collective-permute-start.23 = (f32[24,8,128]{2,1,0:T(8,128)S(1)}, f32[24,8,128]{2,1,0:T(8,128)S(1)}, u32[]{:S(2)}, u32[]{:S(2)}) collective-permute-start(f32[24,8,128]{2,1,0:T(8,128)S(1)} %get-tuple-element.41), channel_id=1, source_target_pairs={{0,3},{1,2},{2,1},{3,0},{4,7},{5,6},{6,5},{7,4},{8,11},{9,10},{10,... | collective-permute-start | bytes 294920 | tf_op jit(solution)/shard_map/ppermute | solution.py:383
  (8 other events, 114.6 us)

commit v4 on v3

--- a/solution.py
+++ b/solution.py
@@ -10,6 +10,7 @@
 
 HOPPING = 0.13
 LANES = 128
+HALVES = 2
 COMPS = 12
 PROJECT = (
     ((1, 1), (0, 1)),
@@ -99,34 +100,62 @@
 def link_at(links, direction):
     def at(row, column):
         place = direction * 18 + row * 3 + column
-        return links[place], links[place + 9]
+        u, v = links[place], links[place + 9]
+        return u, v + u, v - u
 
     return at
 
 
-def times_link(link, half):
-    out = []
+def entry_sums(values, size, sums):
+    for matrix in range(values.shape[0] // (2 * size)):
+        for entry in range(size):
+            u = values[matrix * 2 * size + entry]
+            v = values[matrix * 2 * size + size + entry]
+            sums[matrix * 2 * size + entry] = v + u
+            sums[matrix * 2 * size + size + entry] = v - u
+
+
+def summed_link_at(links, sums, direction):
+    def at(row, column):
+        place = direction * 18 + row * 3 + column
+        return links[place], sums[place], sums[place + 9]
+
+    return at
+
+
+def sums_of(halves):
+    return [[(a, b, a + b) for a, b in half] for half in halves]
+
+
+def times_link(link, halves):
+    out = [[None] * 3 for _ in halves]
     for row in range(3):
-        re = im = None
+        totals = [None] * len(halves)
         for column in range(3):
-            u, v = link(row, column)
-            a, b = half[column]
-            re = u * a - v * b if re is None else re + u * a - v * b
-            im = u * b + v * a if im is None else im + u * b + v * a
-        out.append((re, im))
+            u, s, d = link(row, column)
+            for which, half in enumerate(halves):
+                a, b, ab = half[column]
+                terms = (u * ab, s * b, d * a)
+                old = totals[which]
+                totals[which] = terms if old is None else [x + y for x, y in zip(old, terms)]
+        for which, (both, re, im) in enumerate(totals):
+            out[which][row] = (both - re, both + im)
     return out
 
 
-def times_dagger(link, half):
-    out = []
+def times_dagger(link, halves):
+    out = [[None] * 3 for _ in halves]
     for row in range(3):
-        re = im = None
+        totals = [None] * len(halves)
         for column in range(3):
-            u, v = link(column, row)
-            a, b = half[column]
-            re = u * a + v * b if re is None else re + u * a + v * b
-            im = u * b - v * a if im is None else im + u * b - v * a
-        out.append((re, im))
+            u, s, d = link(column, row)
+            for which, half in enumerate(halves):
+                a, b, ab = half[column]
+                terms = (u * ab, d * b, s * a)
+                old = totals[which]
+                totals[which] = terms if old is None else [x + y for x, y in zip(old, terms)]
+        for which, (both, re, im) in enumerate(totals):
+            out[which][row] = (both + re, both - im)
     return out
 
 
@@ -138,10 +167,10 @@
 
 def pack_rim(lattice, spinor, links, direction, ahead_ref, behind_ref, vector):
     slices = lattice.slices
-    ahead, behind = [], []
-    for spin in range(2):
-        ahead += half_spinor(spinor, 3, spin, True)
-        behind += times_dagger(link_at(links, direction), half_spinor(spinor, 3, spin, False))
+    ahead = half_spinor(spinor, 3, 0, True) + half_spinor(spinor, 3, 1, True)
+    halves = [half_spinor(spinor, 3, spin, False) for spin in range(2)]
+    behind = times_dagger(link_at(links, direction), sums_of(halves))
+    behind = behind[0] + behind[1]
     for values, origin, ref in ((ahead, 0, ahead_ref), (behind, slices - 1, behind_ref)):
         flat = [part for pair in values for part in pair]
         for group in range(COMPS // slices):
@@ -165,8 +194,9 @@
 
 def open_kernel(
     lattice, groups, vectors, kept, ship,
-    psi_ref, links_ref, basis, ahead_ref, behind_ref, *refs,
+    psi_ref, links_ref, basis, *refs,
 ):
+    rims, refs = refs[: 2 * HALVES], refs[2 * HALVES :]
     pieces = refs[: groups - 1]
     psi, links, held, sems = refs[groups - 1 :]
     here = lax.axis_index("ba")
@@ -188,11 +218,15 @@
     links_in.wait()
     fields.wait()
 
-    def body(vector, carry):
-        pack_rim(lattice, load_spinor(psi, vector), links, 0, ahead_ref, behind_ref, vector)
-        return carry
-
-    lax.fori_loop(0, vectors, body, 0)
+    size = vectors // HALVES
+    for which in range(HALVES):
+
+        def body(vector, carry, which=which):
+            spinor = load_spinor(psi, which * size + vector)
+            pack_rim(lattice, spinor, links, 0, rims[2 * which], rims[2 * which + 1], vector)
+            return carry
+
+        lax.fori_loop(0, size, body, 0)
     for step, copy in enumerate(kept_in):
         copy.wait()
 
@@ -224,22 +258,29 @@
     lax.fori_loop(0, basis.shape[2] // rows, body, 0)
 
 
-def local_kernel(lattice, vectors, psi, links, clover, out):
+def local_kernel(lattice, vectors, base, psi, links, clover, out, link_sums, clover_sums):
     lattice.masks()
+    entry_sums(links, 9, link_sums)
+    entry_sums(clover, 36, clover_sums)
 
     def body(vector, carry):
-        spinor = load_spinor(psi, vector)
+        spinor = load_spinor(psi, base + vector)
         upper = [[None] * 3 for _ in range(2)]
         lower = [[None] * 3 for _ in range(2)]
         for direction in range(4):
-            link = link_at(links, direction)
+            link = summed_link_at(links, link_sums, direction)
+            halves = []
             for spin in range(2):
                 half = half_spinor(spinor, direction, spin, True)
-                half = [tuple(lattice.shift(p, direction, True) for p in h) for h in half]
-                ahead = times_link(link, half)
-                half = half_spinor(spinor, direction, spin, False)
-                behind = times_dagger(link, half)
-                behind = [tuple(lattice.shift(p, direction, False) for p in h) for h in behind]
+                halves.append([tuple(lattice.shift(p, direction, True) for p in h) for h in half])
+            aheads = times_link(link, sums_of(halves))
+            halves = [half_spinor(spinor, direction, spin, False) for spin in range(2)]
+            behinds = times_dagger(link, sums_of(halves))
+            for spin in range(2):
+                ahead = aheads[spin]
+                behind = [
+                    tuple(lattice.shift(p, direction, False) for p in h) for h in behinds[spin]
+                ]
                 place, phase = REBUILD[direction][spin]
                 for c in range(3):
                     total, diff = plus(ahead[c], behind[c]), minus(ahead[c], behind[c])
@@ -253,17 +294,23 @@
                     else:
                         lower[place][c] = add_phase(lower[place][c], diff, phase)
         for chiral, hops in ((0, upper), (1, lower)):
+            field = [spinor(2 * chiral + i // 3, i % 3) for i in range(6)]
+            field = [(x, y, x + y) for x, y in field]
             for row in range(6):
-                re = im = None
+                total = None
                 for column in range(6):
                     place = chiral * 72 + row * 6 + column
-                    u, v = clover[place], clover[place + 36]
-                    a, b = spinor(2 * chiral + column // 3, column % 3)
-                    re = u * a - v * b if re is None else re + u * a - v * b
-                    im = u * b + v * a if im is None else im + u * b + v * a
+                    a, b, ab = field[column]
+                    terms = (
+                        clover[place] * ab,
+                        clover_sums[place] * b,
+                        clover_sums[place + 36] * a,
+                    )
+                    total = terms if total is None else [x + y for x, y in zip(total, terms)]
+                both, re, im = total
                 place = vector * (2 * COMPS) + chiral * 6 + row
-                out[place] = re - HOPPING * hops[row // 3][row % 3][0]
-                out[place + COMPS] = im - HOPPING * hops[row // 3][row % 3][1]
+                out[place] = both - re - HOPPING * hops[row // 3][row % 3][0]
+                out[place + COMPS] = both + im - HOPPING * hops[row // 3][row % 3][1]
         return carry
 
     lax.fori_loop(0, vectors, body, 0)
@@ -278,8 +325,9 @@
 def finish(lattice, links, part, rim_ahead, rim_behind, vector, signs, store):
     ahead_all = unpack_rim(lattice, rim_ahead, vector, True, signs[0])
     behind_all = unpack_rim(lattice, rim_behind, vector, False, signs[1])
+    both = times_link(link_at(links, 3), sums_of([ahead_all[:3], ahead_all[3:]]))
     for spin in range(2):
-        ahead = times_link(link_at(links, 3), ahead_all[3 * spin : 3 * spin + 3])
+        ahead = both[spin]
         behind = behind_all[3 * spin : 3 * spin + 3]
         for c in range(3):
             for ri in range(2):
@@ -320,9 +368,9 @@
 
 
 def correlate_kernel(
-    lattice, vectors, kept, scale,
-    part, links, rim_ahead, rim_behind, basis, applied, over, field,
+    lattice, size, kept, scale, part, links, rim_ahead, rim_behind, basis, *refs,
 ):
+    earlier, (applied, over, field) = refs[:-3], refs[-3:]
     lattice.masks()
     signs = rim_signs()
     rows = lattice.rows
@@ -334,17 +382,18 @@
         finish(lattice, links, part, rim_ahead, rim_behind, vector, signs, store)
         return carry
 
-    lax.fori_loop(0, vectors, body, 0)
+    lax.fori_loop(0, size, body, 0)
 
     def add(comp, total):
         blocks_here = pl.ds(pl.multiple_of(comp * rows, rows), rows)
         for ri in range(2):
-            for first in range(0, vectors, 8):
+            for first in range(0, size, 8):
+                count = min(8, size - first)
                 tiles = jnp.stack(
-                    [field[(first + i) * 2 * COMPS + ri * COMPS + comp] for i in range(8)]
+                    [field[(first + i) * 2 * COMPS + ri * COMPS + comp] for i in range(count)]
                 )
-                start = ri * vectors + first
-                applied[blocks_here, start : start + 8, :] = jnp.swapaxes(tiles, 0, 1)
+                start = ri * size + first
+                applied[blocks_here, start : start + count, :] = jnp.swapaxes(tiles, 0, 1)
         for place in range(0, rows, 2):
             block = comp * rows + place
             total = total + lax.dot_general(
@@ -355,12 +404,20 @@
             )
         return total
 
-    total = lax.fori_loop(0, COMPS, add, jnp.zeros((4 * vectors, 4 * kept), jnp.float32))
-    total = total[: 2 * vectors] + total[2 * vectors :]
+    total = lax.fori_loop(0, COMPS, add, jnp.zeros((4 * size, 4 * kept), jnp.float32))
+    total = total[: 2 * size] + total[2 * size :]
     total = total[:, : 2 * kept] + total[:, 2 * kept :]
-    real, imag = total[:vectors], total[vectors:]
-    over[:vectors, :] = scale * (real[:, :kept] + imag[:, kept:])
-    over[vectors:, :] = scale * (imag[:, :kept] - real[:, kept:])
+    real, imag = total[:size], total[size:]
+    real, imag = (
+        scale * (real[:, :kept] + imag[:, kept:]),
+        scale * (imag[:, :kept] - real[:, kept:]),
+    )
+    shares = len(earlier) + 1
+    for which, ref in enumerate(earlier):
+        over[which * size : (which + 1) * size, :] = ref[:size, :]
+        over[(shares + which) * size : (shares + which + 1) * size, :] = ref[size:, :]
+    over[(shares - 1) * size : shares * size, :] = real
+    over[(2 * shares - 1) * size :, :] = imag
 
 
 def partner(here, step, count):
@@ -431,8 +488,10 @@
         outs[step][per - ship, :, :kept] = over[...]
 
 
-def rest_kernel(groups, vectors, kept, ship, scale, over, basis, applied, *refs):
+def rest_kernel(groups, vectors, kept, ship, scale, over, basis, *refs):
+    shares, refs = refs[:HALVES], refs[HALVES:]
     parts, refs = refs[:groups], refs[groups:]
+    size = vectors // HALVES
     pieces, (rest_ref, gram) = refs[:-2], refs[-2:]
     here = lax.axis_index("ba")
     per = basis.shape[0] // groups
@@ -453,7 +512,9 @@
                 for i in range(2)
             ]
             total = jnp.concatenate(total, axis=1)
-        rest = pair_of(applied, mine) - total
+        rows = [pair_of(share, mine) for share in shares]
+        rows = [r[:size] for r in rows] + [r[size:] for r in rows]
+        rest = jnp.concatenate(rows, axis=0) - total
         rest_ref[block] = rest[:, :LANES]
         rest_ref[block + 1] = rest[:, LANES:]
         both = jnp.concatenate(two_halves(rest), axis=0)
@@ -468,52 +529,70 @@
     gram[:, vectors:] = scale * (real[:, vectors:] - imag[:, :vectors])
 
 
-def ortho_kernel(groups, vectors, gram, rest, *outs):
+def ortho_kernel(groups, vectors, gram, rest, *refs):
     here = lax.axis_index("ba")
-    work = outs[-1]
-    outs = outs[:-1]
+    outs, work = refs[:-1], refs[-1]
     shape = (vectors, 2 * vectors)
     row = lax.broadcasted_iota(jnp.int32, shape, 0)
     lane = lax.broadcasted_iota(jnp.int32, shape, 1)
     unit = jnp.where(lane == row + vectors, 1.0, 0.0)
     re = jnp.where(lane < vectors, gram[...], unit)
     im = jnp.concatenate([gram[:, vectors:], jnp.zeros((vectors, vectors), jnp.float32)], axis=1)
+    pivots = jnp.ones(shape, jnp.float32)
     for pivot in range(vectors):
-        scale = 1.0 / jnp.sqrt(re[pivot : pivot + 1, pivot : pivot + 1])
-        row_re, row_im = re[pivot : pivot + 1] * scale, im[pivot : pivot + 1] * scale
-        col_re, col_im = re[:, pivot : pivot + 1] * scale, im[:, pivot : pivot + 1] * scale
+        row_re, row_im = re[pivot : pivot + 1], im[pivot : pivot + 1]
+        col_re = jnp.broadcast_to(re[:, pivot : pivot + 1], shape)
+        col_im = jnp.broadcast_to(im[:, pivot : pivot + 1], shape)
+        value = col_re[pivot : pivot + 1]
+        inverse = 1.0 / value
         below = row > pivot
-        new_re = re - (col_re * row_re - col_im * row_im)
-        new_im = im - (col_re * row_im + col_im * row_re)
-        re = jnp.where(below, new_re, jnp.where(row == pivot, row_re, re))
-        im = jnp.where(below, new_im, jnp.where(row == pivot, row_im, im))
-    inv_re, inv_im = re[:, vectors:], im[:, vectors:]
-    weight = weight_rows(inv_re, -inv_im)
+        col_re = jnp.where(below, col_re * inverse, 0.0)
+        col_im = jnp.where(below, col_im * inverse, 0.0)
+        pivots = jnp.where(row == pivot, value, pivots)
+        re, im = (
+            re - (col_re * row_re - col_im * row_im),
+            im - (col_re * row_im + col_im * row_re),
+        )
+    roots = 1.0 / jnp.sqrt(pivots)
+    inv_re, inv_im = (re * roots)[:, vectors:], (im * roots)[:, vectors:]
     own = vectors // groups
+    for group in range(groups):
+        rows = slice(group * own, (group + 1) * own)
+        work[group, :own, :vectors] = inv_re[rows]
+        work[group, :own, vectors:] = inv_im[rows]
+        work[group, own:, :vectors] = -inv_im[rows]
+        work[group, own:, vectors:] = inv_re[rows]
+    weight = jnp.concatenate(
+        [work[partner(here, step, groups)] for step in range(groups)], axis=0
+    )
+    high, low = two_halves(weight)
+    weight = jnp.concatenate(
+        [jnp.concatenate([high, high], axis=1), jnp.concatenate([low, low], axis=1)], axis=0
+    )
     for block in range(0, rest.shape[0], 2):
         full = weighted(weight, row_pairs(rest, block))
-        for i in range(2):
-            value = full[:, i * LANES : (i + 1) * LANES]
-            for group in range(groups):
-                for ri in range(2):
-                    start = ri * vectors + group * own
-                    work[group, block + i, ri * own : (ri + 1) * own, :] = value[
-                        start : start + own
-                    ]
-    for step in range(groups):
-        outs[step][...] = work[partner(here, step, groups)]
-
-
-def place_kernel(groups, own, blocks, *refs):
+        for step in range(groups):
+            rows = slice(step * 2 * own, (step + 1) * 2 * own)
+            outs[step][block] = full[rows, :LANES]
+            outs[step][block + 1] = full[rows, LANES:]
+
+
+def place_kernel(groups, own, rows, *refs):
     parts, out = refs[:groups], refs[groups]
     here = lax.axis_index("ba")
-    per = blocks // groups
+    per = parts[0].shape[0]
     for step in range(groups):
         first = source(here, step, groups) * per
-        for block in range(per):
-            for ri in range(2):
-                value = parts[step][block, ri * own : (ri + 1) * own, :]
-                out[pl.ds(first + block + ri * blocks, own, stride=2 * blocks), :] = value
+        if per % rows:
+            for block in range(per):
+                for ri in range(2):
+                    out[:, ri, first + block, :] = parts[step][block, ri * own : (ri + 1) * own, :]
+        else:
+            for block in range(0, per, rows):
+                tile = jnp.swapaxes(parts[step][block : block + rows], 0, 1)
+                there = pl.ds(pl.multiple_of(first + block, rows), rows)
+                for ri in range(2):
+                    out[:, ri, there, :] = tile[ri * own : (ri + 1) * own]
 
 
 def call(kernel, outs, *args, scratch=(), flops=0, grant=6, remote=()):
@@ -553,66 +632,84 @@
     scale = 1.0 / (2 * COMPS * slices * sites * places)
     psi = tiles_of(search_block, vectors * 2 * COMPS)
     basis = tiles_of(kept_basis, kept * 2 * COMPS).reshape(kept, 2, blocks, LANES)
-    ship = per // 2 if per % rows == 0 else 0
+    ship = per * 5 // 24 * 2 if per % rows == 0 else 0
     links = tiles_of(gauge_links, 72)
     clover = tiles_of(clover_term, 144)
-    local = functools.partial(local_kernel, lattice, vectors)
-    rim = shape_of(vectors * COMPS // slices, rows, LANES)
-    field = shape_of(vectors * 2 * COMPS, rows, LANES)
-    work = vectors * rows * LANES
+    size = vectors // HALVES
+    rim = shape_of(size * COMPS // slices, rows, LANES)
+    field = shape_of(size * 2 * COMPS, rows, LANES)
+    work = size * rows * LANES
+    in_hbm = functools.partial(pltpu.with_memory_space_constraint, memory_space=pltpu.HBM)
 
     def swap(ahead, behind):
         down = [(i, (i + places - 1) % places) for i in range(places)]
         up = [(i, (i + 1) % places) for i in range(places)]
         return lax.ppermute(ahead, "ta", down), lax.ppermute(behind, "ta", up)
 
-    ahead, behind, *pieces = call(
+    def local(values, base):
+        return call(
+            functools.partial(local_kernel, lattice, size, base),
+            (field,),
+            values,
+            links,
+            clover,
+            scratch=[pltpu.VMEM(links.shape, jnp.float32), pltpu.VMEM(clover.shape, jnp.float32)],
+            flops=2000 * work,
+        )[0]
+
+    opened = call(
         functools.partial(open_kernel, lattice, groups, vectors, kept, ship),
-        (rim, rim) + (shape_of(max(ship, 1), 2 * kept, LANES),) * (groups - 1),
-        psi,
-        links,
-        basis,
+        (rim,) * (2 * HALVES) + (shape_of(max(ship, 1), 2 * kept, LANES),) * (groups - 1),
+        in_hbm(psi),
+        in_hbm(links),
+        in_hbm(basis),
         scratch=[
             pltpu.VMEM(psi.shape, jnp.float32),
             pltpu.VMEM((18, rows, LANES), jnp.float32),
             pltpu.VMEM((groups - 1, kept, 2, -(-ship // rows) * rows or rows, LANES), jnp.float32),
             pltpu.SemaphoreType.DMA((groups + 1,)),
         ],
-        flops=200 * work,
-        grant=60,
+        flops=400 * work,
+        grant=8,
         remote=(0, 1, 2),
     )
-    rims = swap(ahead, behind)
-    if ship:
-        pieces = exchanged([None, *pieces], "ba")[1:]
-    else:
-        pieces = []
-    (part,) = call(local, (field,), psi, links, clover, flops=2000 * work)
-    first, ahead, behind = call(
-        functools.partial(middle_kernel, lattice, vectors),
-        (field, rim, rim),
-        part,
-        links,
-        *rims,
-        flops=400 * work,
-    )
-    rims = swap(ahead, behind)
-    (part,) = call(local, (field,), first, links, clover, flops=2000 * work)
+    rims = [swap(opened[2 * which], opened[2 * which + 1]) for which in range(HALVES)]
+    pieces = exchanged([None, *opened[2 * HALVES :]], "ba")[1:] if ship else []
+    parts = []
+    for which in range(HALVES):
+        part = local(psi, which * size)
+        first, ahead, behind = call(
+            functools.partial(middle_kernel, lattice, size),
+            (field, rim, rim),
+            part,
+            links,
+            *rims[which],
+            flops=400 * work,
+        )
+        rims[which] = swap(ahead, behind)
+        parts.append(first)
     (basis_rows,) = call(
         functools.partial(basis_kernel, rows, kept),
         (jax.ShapeDtypeStruct((blocks, 4 * kept, LANES), jnp.bfloat16),),
         basis,
     )
-    applied, over = call(
-        functools.partial(correlate_kernel, lattice, vectors, kept, scale),
-        (shape_of(blocks, 2 * vectors, LANES), shape_of(2 * vectors, kept)),
-        part,
-        links,
-        *rims,
-        basis_rows,
-        scratch=[pltpu.VMEM(psi.shape, jnp.float32)],
-        flops=400 * work,
-    )
+    parts = [local(first, 0) for first in parts]
+    applied, overs = [], []
+    for which in range(HALVES):
+        earlier = overs if which == HALVES - 1 else []
+        share, over = call(
+            functools.partial(correlate_kernel, lattice, size, kept, scale),
+            (shape_of(blocks, 2 * size, LANES), shape_of(2 * size * (len(earlier) + 1), kept)),
+            parts[which],
+            links,
+            *rims[which],
+            basis_rows,
+            *earlier,
+            scratch=[pltpu.VMEM((size * 2 * COMPS, rows, LANES), jnp.float32)],
+            flops=400 * work,
+        )
+        applied.append(share)
+        overs.append(over)
     over = summed(over, "ta", (2, 4))
     parts = call(
         functools.partial(project_kernel, groups, vectors, kept, ship),
@@ -626,7 +723,7 @@
         (shape_of(per, 2 * vectors, LANES), shape_of(vectors, 2 * vectors)),
         over,
         basis_rows,
-        applied,
+        *applied,
         *parts,
         *pieces,
     )
@@ -637,12 +734,12 @@
         (piece,) * groups,
         gram,
         rest,
-        scratch=[pltpu.VMEM((groups, per, 2 * own, LANES), jnp.float32)],
+        scratch=[pltpu.VMEM((groups, 2 * own, 2 * vectors), jnp.float32)],
     )
     pieces = exchanged(pieces, "ba")
     (ortho,) = call(
-        functools.partial(place_kernel, groups, own, blocks),
-        (shape_of(own * 2 * blocks, LANES),),
+        functools.partial(place_kernel, groups, own, rows),
+        (shape_of(own, 2, blocks, LANES),),
         *pieces,
     )
     ortho = ortho.reshape(own * 2 * COMPS, sites // LANES, slices, LANES).swapaxes(1, 2)
@@ -658,6 +755,7 @@
         P(None, None, None, None, "ta", None),
     )
 
+
     return jax.shard_map(
         per_device,
         mesh=mesh,

time: 122 us -> 117 us (0.959)
  waiting for transfers between devices: 64.1 us -> 53 us
  starting transfers between devices: 33.3 us -> 39.6 us
    ppermute x4 -> x8, waiting for transfers between devices: 8.79 us -> 0.51 us  [swap(): return (lax.ppermute(ahead, 'ta', down), lax.ppermute(behind, 'ta', up))]
    ppermute x4 -> x8, starting transfers between devices: 4.36 us -> 11 us  [swap(): return (lax.ppermute(ahead, 'ta', down), lax.ppermute(behind, 'ta', up))]
    ppermute x9, waiting for transfers between devices: 47.1 us -> 43.4 us  [exchanged(): out.append(lax.ppermute(values[step], axis, pairs))]
    pallas_call x10 -> x14, Pallas kernels: 23.2 us -> 23.8 us  [call(): pl.pallas_call(kernel, out_shape=tuple(outs), in_specs=[anywhere if i in...]
  transfers between devices with their start and end apart: 24 -> 28, of which waited for: 16 -> 13; matrix products, arithmetic and copies ran while one was open for 0% -> 0% of each run, Pallas kernels for 12% -> 15%
where the time goes in v4:
time: 117 us
  waiting for transfers between devices  53 us (45%)
  starting transfers between devices  39.6 us (34%)
  Pallas kernels  23.8 us (20%)
    ppermute x9, waiting for transfers between devices, exchanged(): out.append(lax.ppermute(values[step], axis, pairs))  43.4 us
    pallas_call x14, Pallas kernels, call(): pl.pallas_call(kernel, out_shape=tuple(outs), in_specs=[anywhere if i in...  23.8 us
    ppermute x11, starting transfers between devices, summed(): lax.ppermute(value, axis, [(i, i ^ step * stride) for i in range(count)])  14.5 us
    ppermute x9, starting transfers between devices, exchanged(): out.append(lax.ppermute(values[step], axis, pairs))  14.1 us
    ppermute x8, starting transfers between devices, swap(): return (lax.ppermute(ahead, 'ta', down), lax.ppermute(behind, 'ta', up))  11 us
    ppermute x11, waiting for transfers between devices, summed(): lax.ppermute(value, axis, [(i, i ^ step * stride) for i in range(count)])  9.04 us
  transfers between devices with their start and end apart: 28, of which 13 were waited for; matrix products, arithmetic and copies ran while one was open for 0% of the time, Pallas kernels for 15%

profile of v4, /device:TPU:0, one launch (start us, length us, event | category | flops | bytes accessed | tf_op | source)
XLA Modules:
  0.0 117.2 jit_solution(15109187584779028789)
XLA Ops:
  0.7 2.4 %shard_map.60 = (f32[48,8,128]{2,1,0:T(8,128)S(1)}, f32[48,8,128]{2,1,0:T(8,128)S(1)}, f32[48,8,128]{2,1,0:T(8,128)S(1)}, f32[48,8,128]{2,1,0:T(8,128)S(1)}, f32...) custom-call(f32[384,8,128]{2,1,0:T(8,128)} %bitcast.37, f32[72,8,128]{2,1,0:T(8,128)} %bitcast.28, ...), custom_call_target="tpu_custom_call" | custom-call | flops 3276800 | bytes 6782976 | tf_op jit(solution)/shard_map/pallas_call | solution.py:602
  3.0 3.4 %collective-permute-start.4 = (f32[48,8,128]{2,1,0:T(8,128)S(1)}, f32[48,8,128]{2,1,0:T(8,128)S(1)}, u32[]{:S(2)}, u32[]{:S(2)}) collective-permute-start(f32[48,8,128]{2,1,0:T(8,128)S(1)} %get-tuple-element.34), channel_id=1, source_target_pairs={{0,28},{4,0},{8,4},{12,8},{16,12},{20,16},{24,20},{28,24},{1,29},{... | collective-permute-start | bytes 589832 | tf_op jit(solution)/shard_map/ppermute | solution.py:647
  6.4 2.6 %collective-permute-start = (f32[48,8,128]{2,1,0:T(8,128)S(1)}, f32[48,8,128]{2,1,0:T(8,128)S(1)}, u32[]{:S(2)}, u32[]{:S(2)}) collective-permute-start(f32[48,8,128]{2,1,0:T(8,128)S(1)} %get-tuple-element.29), channel_id=1, source_target_pairs={{0,28},{4,0},{8,4},{12,8},{16,12},{20,16},{24,20},{28,24},{1,29},{... | collective-permute-start | bytes 589832 | tf_op jit(solution)/shard_map/ppermute | solution.py:647
  9.1 2.5 %shard_map.64.part = f32[192,8,128]{2,1,0:T(8,128)S(1)} custom-call(f32[384,8,128]{2,1,0:T(8,128)S(1)} %bitcast.38, f32[72,8,128]{2,1,0:T(8,128)S(1)} %bitcast.29, f32[144,8,128]{2,1,0:T(8,128)S(1)} %bitcast.42), custom_call_target="tpu_custom_call" | custom-call | flops 16384000 | bytes 3244032 | tf_op jit(solution)/shard_map/pallas_call | solution.py:602
  11.6 2.5 %shard_map.59.part = f32[192,8,128]{2,1,0:T(8,128)S(1)} custom-call(f32[384,8,128]{2,1,0:T(8,128)S(1)} %bitcast.39, f32[72,8,128]{2,1,0:T(8,128)S(1)} %bitcast.30, f32[144,8,128]{2,1,0:T(8,128)S(1)} %bitcast.43), custom_call_target="tpu_custom_call" | custom-call | flops 16384000 | bytes 3244032 | tf_op jit(solution)/shard_map/pallas_call | solution.py:602
  15.0 2.2 %collective-permute-start.6 = (f32[48,8,128]{2,1,0:T(8,128)S(1)}, f32[48,8,128]{2,1,0:T(8,128)S(1)}, u32[]{:S(2)}, u32[]{:S(2)}) collective-permute-start(f32[48,8,128]{2,1,0:T(8,128)S(1)} %get-tuple-element.37), channel_id=1, source_target_pairs={{0,28},{4,0},{8,4},{12,8},{16,12},{20,16},{24,20},{28,24},{1,29},{... | collective-permute-start | bytes 589832 | tf_op jit(solution)/shard_map/ppermute | solution.py:647
  17.8 2.7 %collective-permute-start.2 = (f32[48,8,128]{2,1,0:T(8,128)S(1)}, f32[48,8,128]{2,1,0:T(8,128)S(1)}, u32[]{:S(2)}, u32[]{:S(2)}) collective-permute-start(f32[48,8,128]{2,1,0:T(8,128)S(1)} %get-tuple-element.32), channel_id=1, source_target_pairs={{0,28},{4,0},{8,4},{12,8},{16,12},{20,16},{24,20},{28,24},{1,29},{... | collective-permute-start | bytes 589832 | tf_op jit(solution)/shard_map/ppermute | solution.py:647
  23.0 2.3 %shard_map.62.part = f32[192,8,128]{2,1,0:T(8,128)S(1)} custom-call(f32[192,8,128]{2,1,0:T(8,128)S(1)} %get-tuple-element.31.psi, f32[72,8,128]{2,1,0:T(8,128)S(1)} %bitcast.33, f32[144,8,128]{2,1,0:T(8,128)S(1)} %bitcast.44), custom_call_target="tpu_custom_call" | custom-call | flops 16384000 | bytes 2457600 | tf_op jit(solution)/shard_map/pallas_call | solution.py:602
  25.3 2.3 %shard_map.66.part = f32[192,8,128]{2,1,0:T(8,128)S(1)} custom-call(f32[192,8,128]{2,1,0:T(8,128)S(1)} %get-tuple-element.36.psi, f32[72,8,128]{2,1,0:T(8,128)S(1)} %bitcast.34, f32[144,8,128]{2,1,0:T(8,128)S(1)} %bitcast.45), custom_call_target="tpu_custom_call" | custom-call | flops 16384000 | bytes 2457600 | tf_op jit(solution)/shard_map/pallas_call | solution.py:602
  27.7 2.9 %shard_map.67 = (f32[96,16,128]{2,1,0:T(8,128)S(1)}, f32[16,32]{1,0:T(8,128)S(1)}) custom-call(f32[192,8,128]{2,1,0:T(8,128)S(1)} %shard_map.66.part, f32[72,8,128]{2,1,0:T(8,128)S(1)} %bitcast.35, f32[48,8,128]{2,1,0:T(8,128)S(1)} %collective-permute-done.6.rim_ahead, f32[48,8,128]{2,1,0:T(8,128)S(1)} %collective-permute-done.7.rim_behind, ...), custom_call_target="tpu_custom_call" | custom-call | flops 3276800 | bytes 5408768 | tf_op jit(solution)/shard_map/pallas_call | solution.py:602
  30.6 2.9 %shard_map.68 = (f32[96,16,128]{2,1,0:T(8,128)S(1)}, f32[32,32]{1,0:T(8,128)S(1)}) custom-call(f32[192,8,128]{2,1,0:T(8,128)S(1)} %shard_map.62.part, f32[72,8,128]{2,1,0:T(8,128)S(1)} %bitcast.36, f32[48,8,128]{2,1,0:T(8,128)S(1)} %collective-permute-done.2.rim_ahead, f32[48,8,128]{2,1,0:T(8,128)S(1)} %collective-permute-done.3.rim_behind, ...), custom_call_target="tpu_custom_call" | custom-call | flops 3276800 | bytes 5412864 | tf_op jit(solution)/shard_map/pallas_call | solution.py:602
  34.7 2.4 %collective-permute-start.11 = (f32[32,32]{1,0:T(8,128)S(1)}, f32[32,32]{1,0:T(8,128)S(1)}, u32[]{:S(2)}, u32[]{:S(2)}) collective-permute-start(f32[32,32]{1,0:T(8,128)S(1)} %add.33), channel_id=1, source_target_pairs={{0,24},{4,28},{8,16},{12,20},{16,8},{20,12},{24,0},{28,4},{1,25},{... | collective-permute-start | bytes 12296 | tf_op jit(solution)/shard_map/ppermute | solution.py:453
  38.2 2.6 %collective-permute-start.16 = (f32[10,64,128]{2,1,0:T(8,128)S(1)}, f32[10,64,128]{2,1,0:T(8,128)S(1)}, u32[]{:S(2)}, u32[]{:S(2)}) collective-permute-start(f32[10,64,128]{2,1,0:T(8,128)S(1)} %get-tuple-element.48), channel_id=1, source_target_pairs={{0,2},{1,3},{2,0},{3,1},{4,6},{5,7},{6,4},{7,5},{8,10},{9,11},{10,... | collective-permute-start | bytes 983048 | tf_op jit(solution)/shard_map/ppermute | solution.py:440
  43.1 2.7 %collective-permute-start.13 = (f32[15,32,128]{2,1,0:T(8,128)S(1)}, f32[15,32,128]{2,1,0:T(8,128)S(1)}, u32[]{:S(2)}, u32[]{:S(2)}) collective-permute-start(f32[15,32,128]{2,1,0:T(8,128)S(1)} %get-tuple-element.45), channel_id=1, source_target_pairs={{0,2},{1,3},{2,0},{3,1},{4,6},{5,7},{6,4},{7,5},{8,10},{9,11},{10,... | collective-permute-start | bytes 737288 | tf_op jit(solution)/shard_map/ppermute | solution.py:440
  46.8 25.8 %collective-permute-done.16.refs_7_ = f32[10,64,128]{2,1,0:T(8,128)S(1)} collective-permute-done((f32[10,64,128]{2,1,0:T(8,128)S(1)}, f32[10,64,128]{2,1,0:T(8,128)S(1)}, u32[]{:S(2)}, u32[]{:S(2)}) %collective-permute-start.16) | collective-permute-done | bytes 327712 | tf_op jit(solution)/shard_map/ppermute | solution.py:440
  72.7 12.3 %collective-permute-done.13.refs_4_ = f32[15,32,128]{2,1,0:T(8,128)S(1)} collective-permute-done((f32[15,32,128]{2,1,0:T(8,128)S(1)}, f32[15,32,128]{2,1,0:T(8,128)S(1)}, u32[]{:S(2)}, u32[]{:S(2)}) %collective-permute-start.13) | collective-permute-done | bytes 245792 | tf_op jit(solution)/shard_map/ppermute | solution.py:440
  87.3 2.6 %collective-permute-start.21 = (f32[16,32]{1,0:T(8,128)S(1)}, f32[16,32]{1,0:T(8,128)S(1)}, u32[]{:S(2)}, u32[]{:S(2)}) collective-permute-start(f32[16,32]{1,0:T(8,128)S(1)} %add.37), channel_id=1, source_target_pairs={{0,24},{4,28},{8,16},{12,20},{16,8},{20,12},{24,0},{28,4},{1,25},{... | collective-permute-start | bytes 6152 | tf_op jit(solution)/shard_map/ppermute | solution.py:453
  94.1 3.6 %collective-permute-start.24 = (f32[16,32]{1,0:T(8,128)S(1)}, f32[16,32]{1,0:T(8,128)S(1)}, u32[]{:S(2)}, u32[]{:S(2)}) collective-permute-start(f32[16,32]{1,0:T(8,128)S(1)} %add_add_fusion.2), channel_id=1, source_target_pairs={{0,3},{1,2},{2,1},{3,0},{4,7},{5,6},{6,5},{7,4},{8,11},{9,10},{10,... | collective-permute-start | bytes 6152 | tf_op jit(solution)/shard_map/ppermute | solution.py:453
  97.7 3.6 %collective-permute-start.23 = (f32[16,32]{1,0:T(8,128)S(1)}, f32[16,32]{1,0:T(8,128)S(1)}, u32[]{:S(2)}, u32[]{:S(2)}) collective-permute-start(f32[16,32]{1,0:T(8,128)S(1)} %add_add_fusion.2), channel_id=1, source_target_pairs={{0,2},{1,3},{2,0},{3,1},{4,6},{5,7},{6,4},{7,5},{8,10},{9,11},{10,... | collective-permute-start | bytes 6152 | tf_op jit(solution)/shard_map/ppermute | solution.py:453
  103.0 1.9 %collective-permute-done.22 = f32[16,32]{1,0:T(8,128)S(1)} collective-permute-done((f32[16,32]{1,0:T(8,128)S(1)}, f32[16,32]{1,0:T(8,128)S(1)}, u32[]{:S(2)}, u32[]{:S(2)}) %collective-permute-start.22) | collective-permute-done | bytes 2080 | tf_op jit(solution)/shard_map/ppermute | solution.py:453
  104.9 1.8 %shard_map.71 = (f32[24,8,128]{2,1,0:T(8,128)S(1)}, f32[24,8,128]{2,1,0:T(8,128)S(1)}, f32[24,8,128]{2,1,0:T(8,128)S(1)}, f32[24,8,128]{2,1,0:T(8,128)S(1)}) custom-call(f32[16,32]{1,0:T(8,128)S(1)} %add_add_fusion.1.gram, f32[24,32,128]{2,1,0:T(8,128)S(1)} %get-tuple-element.51.rest), custom_call_target="tpu_custom_call" | custom-call | bytes 788480 | tf_op jit(solution)/shard_map/pallas_call | solution.py:602
  107.9 2.0 %collective-permute-start.26 = (f32[24,8,128]{2,1,0:T(8,128)S(1)}, f32[24,8,128]{2,1,0:T(8,128)S(1)}, u32[]{:S(2)}, u32[]{:S(2)}) collective-permute-start(f32[24,8,128]{2,1,0:T(8,128)S(1)} %get-tuple-element.54), channel_id=1, source_target_pairs={{0,2},{1,3},{2,0},{3,1},{4,6},{5,7},{6,4},{7,5},{8,10},{9,11},{10,... | collective-permute-start | bytes 294920 | tf_op jit(solution)/shard_map/ppermute | solution.py:440
  111.1 1.7 %collective-permute-done.25.refs_1_ = f32[24,8,128]{2,1,0:T(8,128)S(1)} collective-permute-done((f32[24,8,128]{2,1,0:T(8,128)S(1)}, f32[24,8,128]{2,1,0:T(8,128)S(1)}, u32[]{:S(2)}, u32[]{:S(2)}) %collective-permute-start.25) | collective-permute-done | bytes 98336 | tf_op jit(solution)/shard_map/ppermute | solution.py:440
  114.4 2.0 %collective-permute-done.27.refs_3_ = f32[24,8,128]{2,1,0:T(8,128)S(1)} collective-permute-done((f32[24,8,128]{2,1,0:T(8,128)S(1)}, f32[24,8,128]{2,1,0:T(8,128)S(1)}, u32[]{:S(2)}, u32[]{:S(2)}) %collective-permute-start.27) | collective-permute-done | bytes 98336 | tf_op jit(solution)/shard_map/ppermute | solution.py:440
  (61 shorter events, 22.8 us)
Async XLA Ops:
  3.0 11.0 %collective-permute-start.4 = (f32[48,8,128]{2,1,0:T(8,128)S(1)}, f32[48,8,128]{2,1,0:T(8,128)S(1)}, u32[]{:S(2)}, u32[]{:S(2)}) collective-permute-start(f32[48,8,128]{2,1,0:T(8,128)S(1)} %get-tuple-element.34), channel_id=1, source_target_pairs={{0,28},{4,0},{8,4},{12,8},{16,12},{20,16},{24,20},{28,24},{1,29},{... | collective-permute-start | bytes 589832 | tf_op jit(solution)/shard_map/ppermute | solution.py:647
  6.4 8.1 %collective-permute-start.5 = (f32[48,8,128]{2,1,0:T(8,128)S(1)}, f32[48,8,128]{2,1,0:T(8,128)S(1)}, u32[]{:S(2)}, u32[]{:S(2)}) collective-permute-start(f32[48,8,128]{2,1,0:T(8,128)S(1)} %get-tuple-element.35), channel_id=1, source_target_pairs={{0,4},{4,8},{8,12},{12,16},{16,20},{20,24},{24,28},{28,0},{1,5},{5... | collective-permute-start | bytes 589832 | tf_op jit(solution)/shard_map/ppermute | solution.py:647
  6.4 10.8 %collective-permute-start = (f32[48,8,128]{2,1,0:T(8,128)S(1)}, f32[48,8,128]{2,1,0:T(8,128)S(1)}, u32[]{:S(2)}, u32[]{:S(2)}) collective-permute-start(f32[48,8,128]{2,1,0:T(8,128)S(1)} %get-tuple-element.29), channel_id=1, source_target_pairs={{0,28},{4,0},{8,4},{12,8},{16,12},{20,16},{24,20},{28,24},{1,29},{... | collective-permute-start | bytes 589832 | tf_op jit(solution)/shard_map/ppermute | solution.py:647
  9.1 8.2 %collective-permute-start.1 = (f32[48,8,128]{2,1,0:T(8,128)S(1)}, f32[48,8,128]{2,1,0:T(8,128)S(1)}, u32[]{:S(2)}, u32[]{:S(2)}) collective-permute-start(f32[48,8,128]{2,1,0:T(8,128)S(1)} %get-tuple-element.30), channel_id=1, source_target_pairs={{0,4},{4,8},{8,12},{12,16},{16,20},{20,24},{24,28},{28,0},{1,5},{5... | collective-permute-start | bytes 589832 | tf_op jit(solution)/shard_map/ppermute | solution.py:647
  15.0 12.6 %collective-permute-start.6 = (f32[48,8,128]{2,1,0:T(8,128)S(1)}, f32[48,8,128]{2,1,0:T(8,128)S(1)}, u32[]{:S(2)}, u32[]{:S(2)}) collective-permute-start(f32[48,8,128]{2,1,0:T(8,128)S(1)} %get-tuple-element.37), channel_id=1, source_target_pairs={{0,28},{4,0},{8,4},{12,8},{16,12},{20,16},{24,20},{28,24},{1,29},{... | collective-permute-start | bytes 589832 | tf_op jit(solution)/shard_map/ppermute | solution.py:647
  17.3 10.4 %collective-permute-start.7 = (f32[48,8,128]{2,1,0:T(8,128)S(1)}, f32[48,8,128]{2,1,0:T(8,128)S(1)}, u32[]{:S(2)}, u32[]{:S(2)}) collective-permute-start(f32[48,8,128]{2,1,0:T(8,128)S(1)} %get-tuple-element.38), channel_id=1, source_target_pairs={{0,4},{4,8},{8,12},{12,16},{16,20},{20,24},{24,28},{28,0},{1,5},{5... | collective-permute-start | bytes 589832 | tf_op jit(solution)/shard_map/ppermute | solution.py:647
  17.8 12.8 %collective-permute-start.2 = (f32[48,8,128]{2,1,0:T(8,128)S(1)}, f32[48,8,128]{2,1,0:T(8,128)S(1)}, u32[]{:S(2)}, u32[]{:S(2)}) collective-permute-start(f32[48,8,128]{2,1,0:T(8,128)S(1)} %get-tuple-element.32), channel_id=1, source_target_pairs={{0,28},{4,0},{8,4},{12,8},{16,12},{20,16},{24,20},{28,24},{1,29},{... | collective-permute-start | bytes 589832 | tf_op jit(solution)/shard_map/ppermute | solution.py:647
  20.5 10.1 %collective-permute-start.3 = (f32[48,8,128]{2,1,0:T(8,128)S(1)}, f32[48,8,128]{2,1,0:T(8,128)S(1)}, u32[]{:S(2)}, u32[]{:S(2)}) collective-permute-start(f32[48,8,128]{2,1,0:T(8,128)S(1)} %get-tuple-element.33), channel_id=1, source_target_pairs={{0,4},{4,8},{8,12},{12,16},{16,20},{20,24},{24,28},{28,0},{1,5},{5... | collective-permute-start | bytes 589832 | tf_op jit(solution)/shard_map/ppermute | solution.py:647
  20.5 25.3 %collective-permute-start.15 = (f32[10,64,128]{2,1,0:T(8,128)S(1)}, f32[10,64,128]{2,1,0:T(8,128)S(1)}, u32[]{:S(2)}, u32[]{:S(2)}) collective-permute-start(f32[10,64,128]{2,1,0:T(8,128)S(1)} %get-tuple-element.47), channel_id=1, source_target_pairs={{0,1},{1,0},{2,3},{3,2},{4,5},{5,4},{6,7},{7,6},{8,9},{9,8},{10,11... | collective-permute-start | bytes 983048 | tf_op jit(solution)/shard_map/ppermute | solution.py:440
  34.7 6.1 %collective-permute-start.11 = (f32[32,32]{1,0:T(8,128)S(1)}, f32[32,32]{1,0:T(8,128)S(1)}, u32[]{:S(2)}, u32[]{:S(2)}) collective-permute-start(f32[32,32]{1,0:T(8,128)S(1)} %add.33), channel_id=1, source_target_pairs={{0,24},{4,28},{8,16},{12,20},{16,8},{20,12},{24,0},{28,4},{1,25},{... | collective-permute-start | bytes 12296 | tf_op jit(solution)/shard_map/ppermute | solution.py:453
  37.1 4.7 %collective-permute-start.10 = (f32[32,32]{1,0:T(8,128)S(1)}, f32[32,32]{1,0:T(8,128)S(1)}, u32[]{:S(2)}, u32[]{:S(2)}) collective-permute-start(f32[32,32]{1,0:T(8,128)S(1)} %add.33), channel_id=1, source_target_pairs={{0,16},{4,20},{8,24},{12,28},{16,0},{20,4},{24,8},{28,12},{1,17},{... | collective-permute-start | bytes 12296 | tf_op jit(solution)/shard_map/ppermute | solution.py:453
  37.6 4.2 %collective-permute-start.9 = (f32[32,32]{1,0:T(8,128)S(1)}, f32[32,32]{1,0:T(8,128)S(1)}, u32[]{:S(2)}, u32[]{:S(2)}) collective-permute-start(f32[32,32]{1,0:T(8,128)S(1)} %add.33), channel_id=1, source_target_pairs={{0,8},{4,12},{8,0},{12,4},{16,24},{20,28},{24,16},{28,20},{1,9},{5... | collective-permute-start | bytes 12296 | tf_op jit(solution)/shard_map/ppermute | solution.py:453
  38.2 34.5 %collective-permute-start.16 = (f32[10,64,128]{2,1,0:T(8,128)S(1)}, f32[10,64,128]{2,1,0:T(8,128)S(1)}, u32[]{:S(2)}, u32[]{:S(2)}) collective-permute-start(f32[10,64,128]{2,1,0:T(8,128)S(1)} %get-tuple-element.48), channel_id=1, source_target_pairs={{0,2},{1,3},{2,0},{3,1},{4,6},{5,7},{6,4},{7,5},{8,10},{9,11},{10,... | collective-permute-start | bytes 983048 | tf_op jit(solution)/shard_map/ppermute | solution.py:440
  40.8 31.9 %collective-permute-start.17 = (f32[10,64,128]{2,1,0:T(8,128)S(1)}, f32[10,64,128]{2,1,0:T(8,128)S(1)}, u32[]{:S(2)}, u32[]{:S(2)}) collective-permute-start(f32[10,64,128]{2,1,0:T(8,128)S(1)} %get-tuple-element.49), channel_id=1, source_target_pairs={{0,3},{1,2},{2,1},{3,0},{4,7},{5,6},{6,5},{7,4},{8,11},{9,10},{10,... | collective-permute-start | bytes 983048 | tf_op jit(solution)/shard_map/ppermute | solution.py:440
  42.4 30.3 %collective-permute-start.12 = (f32[15,32,128]{2,1,0:T(8,128)S(1)}, f32[15,32,128]{2,1,0:T(8,128)S(1)}, u32[]{:S(2)}, u32[]{:S(2)}) collective-permute-start(f32[15,32,128]{2,1,0:T(8,128)S(1)} %get-tuple-element.44), channel_id=1, source_target_pairs={{0,1},{1,0},{2,3},{3,2},{4,5},{5,4},{6,7},{7,6},{8,9},{9,8},{10,11... | collective-permute-start | bytes 737288 | tf_op jit(solution)/shard_map/ppermute | solution.py:440
  43.1 41.8 %collective-permute-start.13 = (f32[15,32,128]{2,1,0:T(8,128)S(1)}, f32[15,32,128]{2,1,0:T(8,128)S(1)}, u32[]{:S(2)}, u32[]{:S(2)}) collective-permute-start(f32[15,32,128]{2,1,0:T(8,128)S(1)} %get-tuple-element.45), channel_id=1, source_target_pairs={{0,2},{1,3},{2,0},{3,1},{4,6},{5,7},{6,4},{7,5},{8,10},{9,11},{10,... | collective-permute-start | bytes 737288 | tf_op jit(solution)/shard_map/ppermute | solution.py:440
  45.8 39.2 %collective-permute-start.14 = (f32[15,32,128]{2,1,0:T(8,128)S(1)}, f32[15,32,128]{2,1,0:T(8,128)S(1)}, u32[]{:S(2)}, u32[]{:S(2)}) collective-permute-start(f32[15,32,128]{2,1,0:T(8,128)S(1)} %get-tuple-element.46), channel_id=1, source_target_pairs={{0,3},{1,2},{2,1},{3,0},{4,7},{5,6},{6,5},{7,4},{8,11},{9,10},{10,... | collective-permute-start | bytes 737288 | tf_op jit(solution)/shard_map/ppermute | solution.py:440
  87.3 4.5 %collective-permute-start.21 = (f32[16,32]{1,0:T(8,128)S(1)}, f32[16,32]{1,0:T(8,128)S(1)}, u32[]{:S(2)}, u32[]{:S(2)}) collective-permute-start(f32[16,32]{1,0:T(8,128)S(1)} %add.37), channel_id=1, source_target_pairs={{0,24},{4,28},{8,16},{12,20},{16,8},{20,12},{24,0},{28,4},{1,25},{... | collective-permute-start | bytes 6152 | tf_op jit(solution)/shard_map/ppermute | solution.py:453
  90.4 3.7 %collective-permute-start.19 = (f32[16,32]{1,0:T(8,128)S(1)}, f32[16,32]{1,0:T(8,128)S(1)}, u32[]{:S(2)}, u32[]{:S(2)}) collective-permute-start(f32[16,32]{1,0:T(8,128)S(1)} %add.37), channel_id=1, source_target_pairs={{0,8},{4,12},{8,0},{12,4},{16,24},{20,28},{24,16},{28,20},{1,9},{5... | collective-permute-start | bytes 6152 | tf_op jit(solution)/shard_map/ppermute | solution.py:453
  94.1 7.4 %collective-permute-start.24 = (f32[16,32]{1,0:T(8,128)S(1)}, f32[16,32]{1,0:T(8,128)S(1)}, u32[]{:S(2)}, u32[]{:S(2)}) collective-permute-start(f32[16,32]{1,0:T(8,128)S(1)} %add_add_fusion.2), channel_id=1, source_target_pairs={{0,3},{1,2},{2,1},{3,0},{4,7},{5,6},{6,5},{7,4},{8,11},{9,10},{10,... | collective-permute-start | bytes 6152 | tf_op jit(solution)/shard_map/ppermute | solution.py:453
  97.7 5.3 %collective-permute-start.23 = (f32[16,32]{1,0:T(8,128)S(1)}, f32[16,32]{1,0:T(8,128)S(1)}, u32[]{:S(2)}, u32[]{:S(2)}) collective-permute-start(f32[16,32]{1,0:T(8,128)S(1)} %add_add_fusion.2), channel_id=1, source_target_pairs={{0,2},{1,3},{2,0},{3,1},{4,6},{5,7},{6,4},{7,5},{8,10},{9,11},{10,... | collective-permute-start | bytes 6152 | tf_op jit(solution)/shard_map/ppermute | solution.py:453
  106.7 6.2 %collective-permute-start.25 = (f32[24,8,128]{2,1,0:T(8,128)S(1)}, f32[24,8,128]{2,1,0:T(8,128)S(1)}, u32[]{:S(2)}, u32[]{:S(2)}) collective-permute-start(f32[24,8,128]{2,1,0:T(8,128)S(1)} %get-tuple-element.53), channel_id=1, source_target_pairs={{0,1},{1,0},{2,3},{3,2},{4,5},{5,4},{6,7},{7,6},{8,9},{9,8},{10,11... | collective-permute-start | bytes 294920 | tf_op jit(solution)/shard_map/ppermute | solution.py:440
  107.9 6.6 %collective-permute-start.26 = (f32[24,8,128]{2,1,0:T(8,128)S(1)}, f32[24,8,128]{2,1,0:T(8,128)S(1)}, u32[]{:S(2)}, u32[]{:S(2)}) collective-permute-start(f32[24,8,128]{2,1,0:T(8,128)S(1)} %get-tuple-element.54), channel_id=1, source_target_pairs={{0,2},{1,3},{2,0},{3,1},{4,6},{5,7},{6,4},{7,5},{8,10},{9,11},{10,... | collective-permute-start | bytes 294920 | tf_op jit(solution)/shard_map/ppermute | solution.py:440
  109.9 6.5 %collective-permute-start.27 = (f32[24,8,128]{2,1,0:T(8,128)S(1)}, f32[24,8,128]{2,1,0:T(8,128)S(1)}, u32[]{:S(2)}, u32[]{:S(2)}) collective-permute-start(f32[24,8,128]{2,1,0:T(8,128)S(1)} %get-tuple-element.55), channel_id=1, source_target_pairs={{0,3},{1,2},{2,1},{3,0},{4,7},{5,6},{6,5},{7,4},{8,11},{9,10},{10,... | collective-permute-start | bytes 294920 | tf_op jit(solution)/shard_map/ppermute | solution.py:440
  (9 other events, 89.8 us)

commit v5 on v4

--- a/solution.py
+++ b/solution.py
@@ -10,7 +10,7 @@
 
 HOPPING = 0.13
 LANES = 128
-HALVES = 2
+HALVES = 1
 COMPS = 12
 PROJECT = (
     ((1, 1), (0, 1)),
@@ -368,9 +368,8 @@
 
 
 def correlate_kernel(
-    lattice, size, kept, scale, part, links, rim_ahead, rim_behind, basis, *refs,
+    lattice, size, kept, scale, part, links, rim_ahead, rim_behind, basis, applied, over, field,
 ):
-    earlier, (applied, over, field) = refs[:-3], refs[-3:]
     lattice.masks()
     signs = rim_signs()
     rows = lattice.rows
@@ -394,15 +393,14 @@
                 )
                 start = ri * size + first
                 applied[blocks_here, start : start + count, :] = jnp.swapaxes(tiles, 0, 1)
-        for place in range(0, rows, 2):
-            block = comp * rows + place
-            total = total + lax.dot_general(
-                row_pairs(applied, block),
-                pair_of(basis, block),
-                (((1,), (1,)), ((), ())),
-                preferred_element_type=jnp.float32,
-            )
-        return total
+        mine = jnp.concatenate([applied[comp * rows + i] for i in range(rows)], axis=1)
+        kept_rows = jnp.concatenate([basis[comp * rows + i] for i in range(rows)], axis=1)
+        return total + lax.dot_general(
+            jnp.concatenate(two_halves(mine), axis=0),
+            kept_rows,
+            (((1,), (1,)), ((), ())),
+            preferred_element_type=jnp.float32,
+        )
 
     total = lax.fori_loop(0, COMPS, add, jnp.zeros((4 * size, 4 * kept), jnp.float32))
     total = total[: 2 * size] + total[2 * size :]
@@ -412,12 +410,7 @@
         scale * (real[:, :kept] + imag[:, kept:]),
         scale * (imag[:, :kept] - real[:, kept:]),
     )
-    shares = len(earlier) + 1
-    for which, ref in enumerate(earlier):
-        over[which * size : (which + 1) * size, :] = ref[:size, :]
-        over[(shares + which) * size : (shares + which + 1) * size, :] = ref[size:, :]
-    over[(shares - 1) * size : shares * size, :] = real
-    over[(2 * shares - 1) * size :, :] = imag
+    over[...] = packed(jnp.concatenate([real, imag], axis=0))
 
 
 def partner(here, step, count):
@@ -458,6 +451,18 @@
     return value
 
 
+def packed(value):
+    count = LANES // value.shape[1]
+    size = value.shape[0] // count
+    return jnp.concatenate([value[i * size : (i + 1) * size] for i in range(count)], axis=1)
+
+
+def unpacked(value, width):
+    return jnp.concatenate(
+        [value[:, i * width : (i + 1) * width] for i in range(LANES // width)], axis=0
+    )
+
+
 def weight_rows(real, imag):
     weight = jnp.concatenate(
         [jnp.concatenate([real, -imag], axis=1), jnp.concatenate([imag, real], axis=1)], axis=0
@@ -477,27 +482,28 @@
 def project_kernel(groups, vectors, kept, ship, over, basis, *outs):
     here = lax.axis_index("ba")
     per = basis.shape[0] // groups
-    weight = weight_rows(over[:vectors, :], over[vectors:, :])
+    mine = unpacked(over[...], kept)
+    weight = weight_rows(mine[:vectors], mine[vectors:])
     for step in range(groups):
         first = partner(here, step, groups) * per + ship
+        size = 2 * vectors
         for block in range(0, per - ship, 2):
             value = weighted(weight, pair_of(basis, first + block))
-            outs[step][block] = value[:, :LANES]
-            outs[step][block + 1] = value[:, LANES:]
-        outs[step][per - ship] = jnp.zeros((2 * vectors, LANES), jnp.float32)
-        outs[step][per - ship, :, :kept] = over[...]
-
-
-def rest_kernel(groups, vectors, kept, ship, scale, over, basis, *refs):
-    shares, refs = refs[:HALVES], refs[HALVES:]
+            outs[step][block * size : (block + 1) * size, :] = value[:, :LANES]
+            outs[step][(block + 1) * size : (block + 2) * size, :] = value[:, LANES:]
+        outs[step][(per - ship) * size :, :] = over[...]
+
+
+def rest_kernel(groups, vectors, kept, ship, scale, over, basis, applied, *refs):
     parts, refs = refs[:groups], refs[groups:]
-    size = vectors // HALVES
     pieces, (rest_ref, gram) = refs[:-2], refs[-2:]
     here = lax.axis_index("ba")
     per = basis.shape[0] // groups
-    weights = [weight_rows(over[:vectors, :], over[vectors:, :])]
-    for part in parts[1:]:
-        there = part[per - ship, :, :kept]
+    tall = 2 * vectors
+    weights = []
+    for step in range(groups if ship else 1):
+        there = over[...] if step == 0 else parts[step][(per - ship) * tall :, :]
+        there = unpacked(there, kept)
         weights.append(weight_rows(there[:vectors], there[vectors:]))
     full = None
     for block in range(0, per, 2):
@@ -507,14 +513,12 @@
             for weight, piece in zip(weights[1:], pieces):
                 total = total + weighted(weight, row_pairs(piece, block))
         else:
-            total = [
-                sum((part[block + i - ship] for part in parts[1:]), parts[0][block + i - ship])
-                for i in range(2)
-            ]
-            total = jnp.concatenate(total, axis=1)
-        rows = [pair_of(share, mine) for share in shares]
-        rows = [r[:size] for r in rows] + [r[size:] for r in rows]
-        rest = jnp.concatenate(rows, axis=0) - total
+            start = (block - ship) * tall
+            total = parts[0][start : start + 2 * tall, :]
+            for part in parts[1:]:
+                total = total + part[start : start + 2 * tall, :]
+            total = jnp.concatenate([total[:tall], total[tall:]], axis=1)
+        rest = pair_of(applied, mine) - total
         rest_ref[block] = rest[:, :LANES]
         rest_ref[block + 1] = rest[:, LANES:]
         both = jnp.concatenate(two_halves(rest), axis=0)
@@ -632,7 +636,7 @@
     scale = 1.0 / (2 * COMPS * slices * sites * places)
     psi = tiles_of(search_block, vectors * 2 * COMPS)
     basis = tiles_of(kept_basis, kept * 2 * COMPS).reshape(kept, 2, blocks, LANES)
-    ship = per * 5 // 24 * 2 if per % rows == 0 else 0
+    ship = per // 4 * 2 if per % rows == 0 else 0
     links = tiles_of(gauge_links, 72)
     clover = tiles_of(clover_term, 144)
     size = vectors // HALVES
@@ -694,26 +698,20 @@
         basis,
     )
     parts = [local(first, 0) for first in parts]
-    applied, overs = [], []
-    for which in range(HALVES):
-        earlier = overs if which == HALVES - 1 else []
-        share, over = call(
-            functools.partial(correlate_kernel, lattice, size, kept, scale),
-            (shape_of(blocks, 2 * size, LANES), shape_of(2 * size * (len(earlier) + 1), kept)),
-            parts[which],
-            links,
-            *rims[which],
-            basis_rows,
-            *earlier,
-            scratch=[pltpu.VMEM((size * 2 * COMPS, rows, LANES), jnp.float32)],
-            flops=400 * work,
-        )
-        applied.append(share)
-        overs.append(over)
+    applied, over = call(
+        functools.partial(correlate_kernel, lattice, vectors, kept, scale),
+        (shape_of(blocks, 2 * vectors, LANES), shape_of(2 * vectors * kept // LANES, LANES)),
+        *parts,
+        links,
+        *rims[0],
+        basis_rows,
+        scratch=[pltpu.VMEM(psi.shape, jnp.float32)],
+        flops=400 * work,
+    )
     over = summed(over, "ta", (2, 4))
     parts = call(
         functools.partial(project_kernel, groups, vectors, kept, ship),
-        (shape_of(per - ship + 1, 2 * vectors, LANES),) * groups,
+        (shape_of((per - ship) * 2 * vectors + over.shape[0], LANES),) * groups,
         over,
         basis_rows,
     )
@@ -723,7 +721,7 @@
         (shape_of(per, 2 * vectors, LANES), shape_of(vectors, 2 * vectors)),
         over,
         basis_rows,
-        *applied,
+        applied,
         *parts,
         *pieces,
     )
@@ -744,6 +742,7 @@
     )
     ortho = ortho.reshape(own * 2 * COMPS, sites // LANES, slices, LANES).swapaxes(1, 2)
     ortho = ortho.reshape(own, *search_block.shape[1:])
+    over = over.reshape(over.shape[0], LANES // kept, kept).swapaxes(0, 1)
     return ortho, over.reshape(2, vectors, kept).swapaxes(1, 2)
 
 

time: 117 us -> 119 us (1.017)
  waiting for transfers between devices: 53 us -> 63.2 us
  starting transfers between devices: 39.6 us -> 32.8 us
  Pallas kernels: 23.8 us -> 21.4 us
    ppermute x8 -> x4, waiting for transfers between devices: 0.51 us -> 9.12 us  [swap(): return (lax.ppermute(ahead, 'ta', down), lax.ppermute(behind, 'ta', up))]
    ppermute x8 -> x4, starting transfers between devices: 11 us -> 4.36 us  [swap(): return (lax.ppermute(ahead, 'ta', down), lax.ppermute(behind, 'ta', up))]
    pallas_call x14 -> x10, Pallas kernels: 23.8 us -> 21.4 us  [call(): pl.pallas_call(kernel, out_shape=tuple(outs), in_specs=[anywhere if i in...]
    ppermute x9, waiting for transfers between devices: 43.4 us -> 45.8 us  [exchanged(): out.append(lax.ppermute(values[step], axis, pairs))]
  transfers between devices with their start and end apart: 28 -> 24, of which waited for: 13 -> 16; matrix products, arithmetic and copies ran while one was open for 0% -> 1% of each run, Pallas kernels for 15% -> 12%
where the time goes in v5:
time: 119 us
  waiting for transfers between devices  63.2 us (53%)
  starting transfers between devices  32.8 us (28%)
  Pallas kernels  21.4 us (18%)
    ppermute x9, waiting for transfers between devices, exchanged(): out.append(lax.ppermute(values[step], axis, pairs))  45.8 us
    pallas_call x10, Pallas kernels, call(): pl.pallas_call(kernel, out_shape=tuple(outs), in_specs=[anywhere if i in...  21.4 us
    ppermute x9, starting transfers between devices, exchanged(): out.append(lax.ppermute(values[step], axis, pairs))  15.1 us
    ppermute x11, starting transfers between devices, summed(): lax.ppermute(value, axis, [(i, i ^ step * stride) for i in range(count)])  13.4 us
    ppermute x4, waiting for transfers between devices, swap(): return (lax.ppermute(ahead, 'ta', down), lax.ppermute(behind, 'ta', up))  9.12 us
    ppermute x11, waiting for transfers between devices, summed(): lax.ppermute(value, axis, [(i, i ^ step * stride) for i in range(count)])  8.28 us
    ppermute x4, starting transfers between devices, swap(): return (lax.ppermute(ahead, 'ta', down), lax.ppermute(behind, 'ta', up))  4.36 us
  transfers between devices with their start and end apart: 24, of which 16 were waited for; matrix products, arithmetic and copies ran while one was open for 1% of the time, Pallas kernels for 12%

profile of v5, /device:TPU:0, one launch (start us, length us, event | category | flops | bytes accessed | tf_op | source)
XLA Modules:
  0.0 118.9 jit_solution(15322503013805060138)
XLA Ops:
  0.7 2.4 %shard_map.60 = (f32[96,8,128]{2,1,0:T(8,128)S(1)}, f32[96,8,128]{2,1,0:T(8,128)S(1)}, f32[12,64,128]{2,1,0:T(8,128)S(1)}, f32[12,64,128]{2,1,0:T(8,128)S(1)}, f32[12,64,128]{2,1,0:T(8,128)S(1)}) custom-call(f32[384,8,128]{2,1,0:T(8,128)} %bitcast.36, f32[72,8,128]{2,1,0:T(8,128)} %bitcast.31, f32[32,2,96,128]{3,2,1,0:T(8,128)} %bitcast.29), custom_call_target="tpu_custom_call" | custom-call | flops 6553600 | bytes 6979584 | tf_op jit(solution)/shard_map/pallas_call | solution.py:606
  3.1 3.4 %collective-permute-start = (f32[96,8,128]{2,1,0:T(8,128)S(1)}, f32[96,8,128]{2,1,0:T(8,128)S(1)}, u32[]{:S(2)}, u32[]{:S(2)}) collective-permute-start(f32[96,8,128]{2,1,0:T(8,128)S(1)} %get-tuple-element.22), channel_id=1, source_target_pairs={{0,28},{4,0},{8,4},{12,8},{16,12},{20,16},{24,20},{28,24},{1,29},{... | collective-permute-start | bytes 1179656 | tf_op jit(solution)/shard_map/ppermute | solution.py:651
  6.5 4.6 %shard_map.59.part = f32[384,8,128]{2,1,0:T(8,128)S(1)} custom-call(f32[384,8,128]{2,1,0:T(8,128)S(1)} %bitcast.37, f32[72,8,128]{2,1,0:T(8,128)S(1)} %bitcast.32, f32[144,8,128]{2,1,0:T(8,128)S(1)} %bitcast.38), custom_call_target="tpu_custom_call" | custom-call | flops 32768000 | bytes 4030464 | tf_op jit(solution)/shard_map/pallas_call | solution.py:606
  11.1 4.0 %collective-permute-done.rim_ahead = f32[96,8,128]{2,1,0:T(8,128)S(1)} collective-permute-done((f32[96,8,128]{2,1,0:T(8,128)S(1)}, f32[96,8,128]{2,1,0:T(8,128)S(1)}, u32[]{:S(2)}, u32[]{:S(2)}) %collective-permute-start) | collective-permute-done | bytes 393248 | tf_op jit(solution)/shard_map/ppermute | solution.py:651
  15.1 1.9 %collective-permute-done.1.rim_behind = f32[96,8,128]{2,1,0:T(8,128)S(1)} collective-permute-done((f32[96,8,128]{2,1,0:T(8,128)S(1)}, f32[96,8,128]{2,1,0:T(8,128)S(1)}, u32[]{:S(2)}, u32[]{:S(2)}) %collective-permute-start.1) | collective-permute-done | bytes 393248 | tf_op jit(solution)/shard_map/ppermute | solution.py:651
  21.4 4.8 %shard_map.62.part = f32[384,8,128]{2,1,0:T(8,128)S(1)} custom-call(f32[384,8,128]{2,1,0:T(8,128)S(1)} %get-tuple-element.24.psi, f32[72,8,128]{2,1,0:T(8,128)S(1)} %bitcast.34, f32[144,8,128]{2,1,0:T(8,128)S(1)} %bitcast.39), custom_call_target="tpu_custom_call" | custom-call | flops 32768000 | bytes 4030464 | tf_op jit(solution)/shard_map/pallas_call | solution.py:606
  27.4 2.0 %collective-permute-done.3.rim_behind = f32[96,8,128]{2,1,0:T(8,128)S(1)} collective-permute-done((f32[96,8,128]{2,1,0:T(8,128)S(1)}, f32[96,8,128]{2,1,0:T(8,128)S(1)}, u32[]{:S(2)}, u32[]{:S(2)}) %collective-permute-start.3) | collective-permute-done | bytes 393248 | tf_op jit(solution)/shard_map/ppermute | solution.py:651
  29.4 3.5 %shard_map.64 = (f32[96,32,128]{2,1,0:T(8,128)S(1)}, f32[8,128]{1,0:T(8,128)S(1)}) custom-call(f32[384,8,128]{2,1,0:T(8,128)S(1)} %shard_map.62.part, f32[72,8,128]{2,1,0:T(8,128)S(1)} %bitcast.35, f32[96,8,128]{2,1,0:T(8,128)S(1)} %collective-permute-done.2.rim_ahead, f32[96,8,128]{2,1,0:T(8,128)S(1)} %collective-permute-done.3.rim_behind, ...), custom_call_target="tpu_custom_call" | custom-call | flops 6553600 | bytes 7376896 | tf_op jit(solution)/shard_map/pallas_call | solution.py:606
  34.9 1.6 %collective-permute-start.6 = (f32[8,128]{1,0:T(8,128)S(1)}, f32[8,128]{1,0:T(8,128)S(1)}, u32[]{:S(2)}, u32[]{:S(2)}) collective-permute-start(f32[8,128]{1,0:T(8,128)S(1)} %add.33), channel_id=1, source_target_pairs={{0,16},{4,20},{8,24},{12,28},{16,0},{20,4},{24,8},{28,12},{1,17},{... | collective-permute-start | bytes 12296 | tf_op jit(solution)/shard_map/ppermute | solution.py:446
  37.5 2.6 %collective-permute-start.12 = (f32[12,64,128]{2,1,0:T(8,128)S(1)}, f32[12,64,128]{2,1,0:T(8,128)S(1)}, u32[]{:S(2)}, u32[]{:S(2)}) collective-permute-start(f32[12,64,128]{2,1,0:T(8,128)S(1)} %get-tuple-element.34), channel_id=1, source_target_pairs={{0,2},{1,3},{2,0},{3,1},{4,6},{5,7},{6,4},{7,5},{8,10},{9,11},{10,... | collective-permute-start | bytes 1179656 | tf_op jit(solution)/shard_map/ppermute | solution.py:433
  40.1 2.0 %collective-permute-start.13 = (f32[12,64,128]{2,1,0:T(8,128)S(1)}, f32[12,64,128]{2,1,0:T(8,128)S(1)}, u32[]{:S(2)}, u32[]{:S(2)}) collective-permute-start(f32[12,64,128]{2,1,0:T(8,128)S(1)} %get-tuple-element.35), channel_id=1, source_target_pairs={{0,3},{1,2},{2,1},{3,0},{4,7},{5,6},{6,5},{7,4},{8,11},{9,10},{10,... | collective-permute-start | bytes 1179656 | tf_op jit(solution)/shard_map/ppermute | solution.py:433
  42.8 2.3 %collective-permute-start.9 = (f32[392,128]{1,0:T(8,128)S(1)}, f32[392,128]{1,0:T(8,128)S(1)}, u32[]{:S(2)}, u32[]{:S(2)}) collective-permute-start(f32[392,128]{1,0:T(8,128)S(1)} %get-tuple-element.31), channel_id=1, source_target_pairs={{0,2},{1,3},{2,0},{3,1},{4,6},{5,7},{6,4},{7,5},{8,10},{9,11},{10,... | collective-permute-start | bytes 602120 | tf_op jit(solution)/shard_map/ppermute | solution.py:433
  45.1 2.0 %collective-permute-start.10 = (f32[392,128]{1,0:T(8,128)S(1)}, f32[392,128]{1,0:T(8,128)S(1)}, u32[]{:S(2)}, u32[]{:S(2)}) collective-permute-start(f32[392,128]{1,0:T(8,128)S(1)} %get-tuple-element.32), channel_id=1, source_target_pairs={{0,3},{1,2},{2,1},{3,0},{4,7},{5,6},{6,5},{7,4},{8,11},{9,10},{10,... | collective-permute-start | bytes 602120 | tf_op jit(solution)/shard_map/ppermute | solution.py:433
  47.2 28.2 %collective-permute-done.12.refs_5_ = f32[12,64,128]{2,1,0:T(8,128)S(1)} collective-permute-done((f32[12,64,128]{2,1,0:T(8,128)S(1)}, f32[12,64,128]{2,1,0:T(8,128)S(1)}, u32[]{:S(2)}, u32[]{:S(2)}) %collective-permute-start.12) | collective-permute-done | bytes 393248 | tf_op jit(solution)/shard_map/ppermute | solution.py:433
  75.3 12.7 %collective-permute-done.9.refs_2_ = f32[392,128]{1,0:T(8,128)S(1)} collective-permute-done((f32[392,128]{1,0:T(8,128)S(1)}, f32[392,128]{1,0:T(8,128)S(1)}, u32[]{:S(2)}, u32[]{:S(2)}) %collective-permute-start.9) | collective-permute-done | bytes 200736 | tf_op jit(solution)/shard_map/ppermute | solution.py:433
  91.5 1.6 %collective-permute-start.16 = (f32[16,32]{1,0:T(8,128)S(1)}, f32[16,32]{1,0:T(8,128)S(1)}, u32[]{:S(2)}, u32[]{:S(2)}) collective-permute-start(f32[16,32]{1,0:T(8,128)S(1)} %add.37), channel_id=1, source_target_pairs={{0,16},{4,20},{8,24},{12,28},{16,0},{20,4},{24,8},{28,12},{1,17},{... | collective-permute-start | bytes 6152 | tf_op jit(solution)/shard_map/ppermute | solution.py:446
  95.1 1.6 %collective-permute-done.15 = f32[16,32]{1,0:T(8,128)S(1)} collective-permute-done((f32[16,32]{1,0:T(8,128)S(1)}, f32[16,32]{1,0:T(8,128)S(1)}, u32[]{:S(2)}, u32[]{:S(2)}) %collective-permute-start.15) | collective-permute-done | bytes 2080 | tf_op jit(solution)/shard_map/ppermute | solution.py:446
  96.8 2.5 %collective-permute-start.20 = (f32[16,32]{1,0:T(8,128)S(1)}, f32[16,32]{1,0:T(8,128)S(1)}, u32[]{:S(2)}, u32[]{:S(2)}) collective-permute-start(f32[16,32]{1,0:T(8,128)S(1)} %add_add_fusion.1), channel_id=1, source_target_pairs={{0,3},{1,2},{2,1},{3,0},{4,7},{5,6},{6,5},{7,4},{8,11},{9,10},{10,... | collective-permute-start | bytes 6152 | tf_op jit(solution)/shard_map/ppermute | solution.py:446
  99.3 3.4 %collective-permute-start.19 = (f32[16,32]{1,0:T(8,128)S(1)}, f32[16,32]{1,0:T(8,128)S(1)}, u32[]{:S(2)}, u32[]{:S(2)}) collective-permute-start(f32[16,32]{1,0:T(8,128)S(1)} %add_add_fusion.1), channel_id=1, source_target_pairs={{0,2},{1,3},{2,0},{3,1},{4,6},{5,7},{6,4},{7,5},{8,10},{9,11},{10,... | collective-permute-start | bytes 6152 | tf_op jit(solution)/shard_map/ppermute | solution.py:446
  104.3 2.0 %collective-permute-done.18 = f32[16,32]{1,0:T(8,128)S(1)} collective-permute-done((f32[16,32]{1,0:T(8,128)S(1)}, f32[16,32]{1,0:T(8,128)S(1)}, u32[]{:S(2)}, u32[]{:S(2)}) %collective-permute-start.18) | collective-permute-done | bytes 2080 | tf_op jit(solution)/shard_map/ppermute | solution.py:446
  106.3 1.8 %shard_map.67 = (f32[24,8,128]{2,1,0:T(8,128)S(1)}, f32[24,8,128]{2,1,0:T(8,128)S(1)}, f32[24,8,128]{2,1,0:T(8,128)S(1)}, f32[24,8,128]{2,1,0:T(8,128)S(1)}) custom-call(f32[16,32]{1,0:T(8,128)S(1)} %add_add_fusion.gram, f32[24,32,128]{2,1,0:T(8,128)S(1)} %get-tuple-element.37.rest), custom_call_target="tpu_custom_call" | custom-call | bytes 788480 | tf_op jit(solution)/shard_map/pallas_call | solution.py:606
  109.5 2.0 %collective-permute-start.22 = (f32[24,8,128]{2,1,0:T(8,128)S(1)}, f32[24,8,128]{2,1,0:T(8,128)S(1)}, u32[]{:S(2)}, u32[]{:S(2)}) collective-permute-start(f32[24,8,128]{2,1,0:T(8,128)S(1)} %get-tuple-element.40), channel_id=1, source_target_pairs={{0,2},{1,3},{2,0},{3,1},{4,6},{5,7},{6,4},{7,5},{8,10},{9,11},{10,... | collective-permute-start | bytes 294920 | tf_op jit(solution)/shard_map/ppermute | solution.py:433
  114.0 2.1 %collective-permute-done.22.refs_2_ = f32[24,8,128]{2,1,0:T(8,128)S(1)} collective-permute-done((f32[24,8,128]{2,1,0:T(8,128)S(1)}, f32[24,8,128]{2,1,0:T(8,128)S(1)}, u32[]{:S(2)}, u32[]{:S(2)}) %collective-permute-start.22) | collective-permute-done | bytes 98336 | tf_op jit(solution)/shard_map/ppermute | solution.py:433
  116.1 1.9 %collective-permute-done.23.refs_3_ = f32[24,8,128]{2,1,0:T(8,128)S(1)} collective-permute-done((f32[24,8,128]{2,1,0:T(8,128)S(1)}, f32[24,8,128]{2,1,0:T(8,128)S(1)}, u32[]{:S(2)}, u32[]{:S(2)}) %collective-permute-start.23) | collective-permute-done | bytes 98336 | tf_op jit(solution)/shard_map/ppermute | solution.py:433
  (49 shorter events, 21.1 us)
Async XLA Ops:
  3.1 12.0 %collective-permute-start = (f32[96,8,128]{2,1,0:T(8,128)S(1)}, f32[96,8,128]{2,1,0:T(8,128)S(1)}, u32[]{:S(2)}, u32[]{:S(2)}) collective-permute-start(f32[96,8,128]{2,1,0:T(8,128)S(1)} %get-tuple-element.22), channel_id=1, source_target_pairs={{0,28},{4,0},{8,4},{12,8},{16,12},{20,16},{24,20},{28,24},{1,29},{... | collective-permute-start | bytes 1179656 | tf_op jit(solution)/shard_map/ppermute | solution.py:651
  6.5 10.5 %collective-permute-start.1 = (f32[96,8,128]{2,1,0:T(8,128)S(1)}, f32[96,8,128]{2,1,0:T(8,128)S(1)}, u32[]{:S(2)}, u32[]{:S(2)}) collective-permute-start(f32[96,8,128]{2,1,0:T(8,128)S(1)} %get-tuple-element.23), channel_id=1, source_target_pairs={{0,4},{4,8},{8,12},{12,16},{16,20},{20,24},{24,28},{28,0},{1,5},{5... | collective-permute-start | bytes 1179656 | tf_op jit(solution)/shard_map/ppermute | solution.py:651
  18.0 9.4 %collective-permute-start.2 = (f32[96,8,128]{2,1,0:T(8,128)S(1)}, f32[96,8,128]{2,1,0:T(8,128)S(1)}, u32[]{:S(2)}, u32[]{:S(2)}) collective-permute-start(f32[96,8,128]{2,1,0:T(8,128)S(1)} %get-tuple-element.25), channel_id=1, source_target_pairs={{0,28},{4,0},{8,4},{12,8},{16,12},{20,16},{24,20},{28,24},{1,29},{... | collective-permute-start | bytes 1179656 | tf_op jit(solution)/shard_map/ppermute | solution.py:651
  18.9 10.5 %collective-permute-start.3 = (f32[96,8,128]{2,1,0:T(8,128)S(1)}, f32[96,8,128]{2,1,0:T(8,128)S(1)}, u32[]{:S(2)}, u32[]{:S(2)}) collective-permute-start(f32[96,8,128]{2,1,0:T(8,128)S(1)} %get-tuple-element.26), channel_id=1, source_target_pairs={{0,4},{4,8},{8,12},{12,16},{16,20},{20,24},{24,28},{28,0},{1,5},{5... | collective-permute-start | bytes 1179656 | tf_op jit(solution)/shard_map/ppermute | solution.py:651
  18.9 26.2 %collective-permute-start.11 = (f32[12,64,128]{2,1,0:T(8,128)S(1)}, f32[12,64,128]{2,1,0:T(8,128)S(1)}, u32[]{:S(2)}, u32[]{:S(2)}) collective-permute-start(f32[12,64,128]{2,1,0:T(8,128)S(1)} %get-tuple-element.33), channel_id=1, source_target_pairs={{0,1},{1,0},{2,3},{3,2},{4,5},{5,4},{6,7},{7,6},{8,9},{9,8},{10,11... | collective-permute-start | bytes 1179656 | tf_op jit(solution)/shard_map/ppermute | solution.py:433
  32.9 1.2 collective-permute-start.4
  34.0 6.1 %collective-permute-start.7 = (f32[8,128]{1,0:T(8,128)S(1)}, f32[8,128]{1,0:T(8,128)S(1)}, u32[]{:S(2)}, u32[]{:S(2)}) collective-permute-start(f32[8,128]{1,0:T(8,128)S(1)} %add.33), channel_id=1, source_target_pairs={{0,24},{4,28},{8,16},{12,20},{16,8},{20,12},{24,0},{28,4},{1,25},{... | collective-permute-start | bytes 12296 | tf_op jit(solution)/shard_map/ppermute | solution.py:446
  34.9 7.3 %collective-permute-start.6 = (f32[8,128]{1,0:T(8,128)S(1)}, f32[8,128]{1,0:T(8,128)S(1)}, u32[]{:S(2)}, u32[]{:S(2)}) collective-permute-start(f32[8,128]{1,0:T(8,128)S(1)} %add.33), channel_id=1, source_target_pairs={{0,16},{4,20},{8,24},{12,28},{16,0},{20,4},{24,8},{28,12},{1,17},{... | collective-permute-start | bytes 12296 | tf_op jit(solution)/shard_map/ppermute | solution.py:446
  36.5 5.7 %collective-permute-start.5 = (f32[8,128]{1,0:T(8,128)S(1)}, f32[8,128]{1,0:T(8,128)S(1)}, u32[]{:S(2)}, u32[]{:S(2)}) collective-permute-start(f32[8,128]{1,0:T(8,128)S(1)} %add.33), channel_id=1, source_target_pairs={{0,8},{4,12},{8,0},{12,4},{16,24},{20,28},{24,16},{28,20},{1,9},{5... | collective-permute-start | bytes 12296 | tf_op jit(solution)/shard_map/ppermute | solution.py:446
  37.5 37.8 %collective-permute-start.12 = (f32[12,64,128]{2,1,0:T(8,128)S(1)}, f32[12,64,128]{2,1,0:T(8,128)S(1)}, u32[]{:S(2)}, u32[]{:S(2)}) collective-permute-start(f32[12,64,128]{2,1,0:T(8,128)S(1)} %get-tuple-element.34), channel_id=1, source_target_pairs={{0,2},{1,3},{2,0},{3,1},{4,6},{5,7},{6,4},{7,5},{8,10},{9,11},{10,... | collective-permute-start | bytes 1179656 | tf_op jit(solution)/shard_map/ppermute | solution.py:433
  40.1 35.2 %collective-permute-start.13 = (f32[12,64,128]{2,1,0:T(8,128)S(1)}, f32[12,64,128]{2,1,0:T(8,128)S(1)}, u32[]{:S(2)}, u32[]{:S(2)}) collective-permute-start(f32[12,64,128]{2,1,0:T(8,128)S(1)} %get-tuple-element.35), channel_id=1, source_target_pairs={{0,3},{1,2},{2,1},{3,0},{4,7},{5,6},{6,5},{7,4},{8,11},{9,10},{10,... | collective-permute-start | bytes 1179656 | tf_op jit(solution)/shard_map/ppermute | solution.py:433
  42.7 32.6 %collective-permute-start.8 = (f32[392,128]{1,0:T(8,128)S(1)}, f32[392,128]{1,0:T(8,128)S(1)}, u32[]{:S(2)}, u32[]{:S(2)}) collective-permute-start(f32[392,128]{1,0:T(8,128)S(1)} %get-tuple-element.30), channel_id=1, source_target_pairs={{0,1},{1,0},{2,3},{3,2},{4,5},{5,4},{6,7},{7,6},{8,9},{9,8},{10,11... | collective-permute-start | bytes 602120 | tf_op jit(solution)/shard_map/ppermute | solution.py:433
  42.8 45.3 %collective-permute-start.9 = (f32[392,128]{1,0:T(8,128)S(1)}, f32[392,128]{1,0:T(8,128)S(1)}, u32[]{:S(2)}, u32[]{:S(2)}) collective-permute-start(f32[392,128]{1,0:T(8,128)S(1)} %get-tuple-element.31), channel_id=1, source_target_pairs={{0,2},{1,3},{2,0},{3,1},{4,6},{5,7},{6,4},{7,5},{8,10},{9,11},{10,... | collective-permute-start | bytes 602120 | tf_op jit(solution)/shard_map/ppermute | solution.py:433
  45.1 42.9 %collective-permute-start.10 = (f32[392,128]{1,0:T(8,128)S(1)}, f32[392,128]{1,0:T(8,128)S(1)}, u32[]{:S(2)}, u32[]{:S(2)}) collective-permute-start(f32[392,128]{1,0:T(8,128)S(1)} %get-tuple-element.32), channel_id=1, source_target_pairs={{0,3},{1,2},{2,1},{3,0},{4,7},{5,6},{6,5},{7,4},{8,11},{9,10},{10,... | collective-permute-start | bytes 602120 | tf_op jit(solution)/shard_map/ppermute | solution.py:433
  89.3 1.2 %collective-permute-start.14 = (f32[16,32]{1,0:T(8,128)S(1)}, f32[16,32]{1,0:T(8,128)S(1)}, u32[]{:S(2)}, u32[]{:S(2)}) collective-permute-start(f32[16,32]{1,0:T(8,128)S(1)} %get-tuple-element.36), channel_id=1, source_target_pairs={{0,4},{4,0},{8,12},{12,8},{16,20},{20,16},{24,28},{28,24},{1,5},{5... | collective-permute-start | bytes 6152 | tf_op jit(solution)/shard_map/ppermute | solution.py:446
  90.5 4.5 %collective-permute-start.17 = (f32[16,32]{1,0:T(8,128)S(1)}, f32[16,32]{1,0:T(8,128)S(1)}, u32[]{:S(2)}, u32[]{:S(2)}) collective-permute-start(f32[16,32]{1,0:T(8,128)S(1)} %add.37), channel_id=1, source_target_pairs={{0,24},{4,28},{8,16},{12,20},{16,8},{20,12},{24,0},{28,4},{1,25},{... | collective-permute-start | bytes 6152 | tf_op jit(solution)/shard_map/ppermute | solution.py:446
  91.5 3.7 %collective-permute-start.16 = (f32[16,32]{1,0:T(8,128)S(1)}, f32[16,32]{1,0:T(8,128)S(1)}, u32[]{:S(2)}, u32[]{:S(2)}) collective-permute-start(f32[16,32]{1,0:T(8,128)S(1)} %add.37), channel_id=1, source_target_pairs={{0,16},{4,20},{8,24},{12,28},{16,0},{20,4},{24,8},{28,12},{1,17},{... | collective-permute-start | bytes 6152 | tf_op jit(solution)/shard_map/ppermute | solution.py:446
  93.1 3.7 %collective-permute-start.15 = (f32[16,32]{1,0:T(8,128)S(1)}, f32[16,32]{1,0:T(8,128)S(1)}, u32[]{:S(2)}, u32[]{:S(2)}) collective-permute-start(f32[16,32]{1,0:T(8,128)S(1)} %add.37), channel_id=1, source_target_pairs={{0,8},{4,12},{8,0},{12,4},{16,24},{20,28},{24,16},{28,20},{1,9},{5... | collective-permute-start | bytes 6152 | tf_op jit(solution)/shard_map/ppermute | solution.py:446
  96.8 6.4 %collective-permute-start.20 = (f32[16,32]{1,0:T(8,128)S(1)}, f32[16,32]{1,0:T(8,128)S(1)}, u32[]{:S(2)}, u32[]{:S(2)}) collective-permute-start(f32[16,32]{1,0:T(8,128)S(1)} %add_add_fusion.1), channel_id=1, source_target_pairs={{0,3},{1,2},{2,1},{3,0},{4,7},{5,6},{6,5},{7,4},{8,11},{9,10},{10,... | collective-permute-start | bytes 6152 | tf_op jit(solution)/shard_map/ppermute | solution.py:446
  99.3 5.0 %collective-permute-start.19 = (f32[16,32]{1,0:T(8,128)S(1)}, f32[16,32]{1,0:T(8,128)S(1)}, u32[]{:S(2)}, u32[]{:S(2)}) collective-permute-start(f32[16,32]{1,0:T(8,128)S(1)} %add_add_fusion.1), channel_id=1, source_target_pairs={{0,2},{1,3},{2,0},{3,1},{4,6},{5,7},{6,4},{7,5},{8,10},{9,11},{10,... | collective-permute-start | bytes 6152 | tf_op jit(solution)/shard_map/ppermute | solution.py:446
  102.6 3.7 %collective-permute-start.18 = (f32[16,32]{1,0:T(8,128)S(1)}, f32[16,32]{1,0:T(8,128)S(1)}, u32[]{:S(2)}, u32[]{:S(2)}) collective-permute-start(f32[16,32]{1,0:T(8,128)S(1)} %add_add_fusion.1), channel_id=1, source_target_pairs={{0,1},{1,0},{2,3},{3,2},{4,5},{5,4},{6,7},{7,6},{8,9},{9,8},{10,11... | collective-permute-start | bytes 6152 | tf_op jit(solution)/shard_map/ppermute | solution.py:446
  108.1 6.0 %collective-permute-start.21 = (f32[24,8,128]{2,1,0:T(8,128)S(1)}, f32[24,8,128]{2,1,0:T(8,128)S(1)}, u32[]{:S(2)}, u32[]{:S(2)}) collective-permute-start(f32[24,8,128]{2,1,0:T(8,128)S(1)} %get-tuple-element.39), channel_id=1, source_target_pairs={{0,1},{1,0},{2,3},{3,2},{4,5},{5,4},{6,7},{7,6},{8,9},{9,8},{10,11... | collective-permute-start | bytes 294920 | tf_op jit(solution)/shard_map/ppermute | solution.py:433
  109.5 6.6 %collective-permute-start.22 = (f32[24,8,128]{2,1,0:T(8,128)S(1)}, f32[24,8,128]{2,1,0:T(8,128)S(1)}, u32[]{:S(2)}, u32[]{:S(2)}) collective-permute-start(f32[24,8,128]{2,1,0:T(8,128)S(1)} %get-tuple-element.40), channel_id=1, source_target_pairs={{0,2},{1,3},{2,0},{3,1},{4,6},{5,7},{6,4},{7,5},{8,10},{9,11},{10,... | collective-permute-start | bytes 294920 | tf_op jit(solution)/shard_map/ppermute | solution.py:433
  111.5 6.5 %collective-permute-start.23 = (f32[24,8,128]{2,1,0:T(8,128)S(1)}, f32[24,8,128]{2,1,0:T(8,128)S(1)}, u32[]{:S(2)}, u32[]{:S(2)}) collective-permute-start(f32[24,8,128]{2,1,0:T(8,128)S(1)} %get-tuple-element.41), channel_id=1, source_target_pairs={{0,3},{1,2},{2,1},{3,0},{4,7},{5,6},{6,5},{7,4},{8,11},{9,10},{10,... | collective-permute-start | bytes 294920 | tf_op jit(solution)/shard_map/ppermute | solution.py:433
  (4 other events, 31.5 us)

commit v6 on v5

--- a/solution.py
+++ b/solution.py
@@ -10,7 +10,6 @@
 
 HOPPING = 0.13
 LANES = 128
-HALVES = 1
 COMPS = 12
 PROJECT = (
     ((1, 1), (0, 1)),
@@ -165,11 +164,11 @@
     return [add_phase(spinor(spin, c), spinor(2 + other, c), phase) for c in range(3)]
 
 
-def pack_rim(lattice, spinor, links, direction, ahead_ref, behind_ref, vector):
+def pack_rim(lattice, spinor, links, ahead_ref, behind_ref, vector):
     slices = lattice.slices
     ahead = half_spinor(spinor, 3, 0, True) + half_spinor(spinor, 3, 1, True)
     halves = [half_spinor(spinor, 3, spin, False) for spin in range(2)]
-    behind = times_dagger(link_at(links, direction), sums_of(halves))
+    behind = times_dagger(link_at(links, 3), sums_of(halves))
     behind = behind[0] + behind[1]
     for values, origin, ref in ((ahead, 0, ahead_ref), (behind, slices - 1, behind_ref)):
         flat = [part for pair in values for part in pair]
@@ -196,14 +195,13 @@
     lattice, groups, vectors, kept, ship,
     psi_ref, links_ref, basis, *refs,
 ):
-    rims, refs = refs[: 2 * HALVES], refs[2 * HALVES :]
-    pieces = refs[: groups - 1]
-    psi, links, held, sems = refs[groups - 1 :]
+    psi, links, ahead_ref, behind_ref = refs[:4]
+    pieces = refs[4 : groups + 3]
+    held, sems = refs[groups + 3 :]
     here = lax.axis_index("ba")
     rows, per = lattice.rows, basis.shape[2] // groups
-    count = links.shape[0]
     fields = pltpu.make_async_copy(psi_ref, psi, sems.at[0])
-    links_in = pltpu.make_async_copy(links_ref.at[pl.ds(3 * count, count)], links, sems.at[1])
+    links_in = pltpu.make_async_copy(links_ref, links, sems.at[1])
     kept_in = []
     for step in range(1, groups if ship else 1):
         start = pl.multiple_of(partner(here, step, groups) * per, rows)
@@ -218,15 +216,11 @@
     links_in.wait()
     fields.wait()
 
-    size = vectors // HALVES
-    for which in range(HALVES):
-
-        def body(vector, carry, which=which):
-            spinor = load_spinor(psi, which * size + vector)
-            pack_rim(lattice, spinor, links, 0, rims[2 * which], rims[2 * which + 1], vector)
-            return carry
-
-        lax.fori_loop(0, size, body, 0)
+    def body(vector, carry):
+        pack_rim(lattice, load_spinor(psi, vector), links, ahead_ref, behind_ref, vector)
+        return carry
+
+    lax.fori_loop(0, vectors, body, 0, unroll=2)
     for step, copy in enumerate(kept_in):
         copy.wait()
 
@@ -258,13 +252,13 @@
     lax.fori_loop(0, basis.shape[2] // rows, body, 0)
 
 
-def local_kernel(lattice, vectors, base, psi, links, clover, out, link_sums, clover_sums):
+def local_kernel(lattice, vectors, psi, links, clover, out, link_sums, clover_sums):
     lattice.masks()
     entry_sums(links, 9, link_sums)
     entry_sums(clover, 36, clover_sums)
 
     def body(vector, carry):
-        spinor = load_spinor(psi, base + vector)
+        spinor = load_spinor(psi, vector)
         upper = [[None] * 3 for _ in range(2)]
         lower = [[None] * 3 for _ in range(2)]
         for direction in range(4):
@@ -348,7 +342,7 @@
             out[place] = value
 
         finish(lattice, links, part, rim_ahead, rim_behind, vector, signs, store)
-        pack_rim(lattice, load_spinor(out, vector), links, 3, ahead_ref, behind_ref, vector)
+        pack_rim(lattice, load_spinor(out, vector), links, ahead_ref, behind_ref, vector)
         return carry
 
     lax.fori_loop(0, vectors, body, 0)
@@ -359,12 +353,16 @@
     return high, (value - high.astype(jnp.float32)).astype(jnp.bfloat16)
 
 
-def pair_of(ref, block):
-    return jnp.concatenate([ref[block], ref[block + 1]], axis=1)
-
-
-def row_pairs(ref, block):
-    return jnp.concatenate(two_halves(pair_of(ref, block)), axis=0)
+def spans(first, last):
+    return [(i, min(2, last - i)) for i in range(first, last, 2)]
+
+
+def beside(ref, block, count):
+    return jnp.concatenate([ref[block + i] for i in range(count)], axis=1)
+
+
+def halves_beside(ref, block, count):
+    return jnp.concatenate(two_halves(beside(ref, block, count)), axis=0)
 
 
 def correlate_kernel(
@@ -381,10 +379,11 @@
         finish(lattice, links, part, rim_ahead, rim_behind, vector, signs, store)
         return carry
 
-    lax.fori_loop(0, size, body, 0)
-
-    def add(comp, total):
-        blocks_here = pl.ds(pl.multiple_of(comp * rows, rows), rows)
+    lax.fori_loop(0, size, body, 0, unroll=2)
+
+    total = jnp.zeros((4 * size, 4 * kept), jnp.float32)
+    for comp in range(COMPS):
+        blocks_here = slice(comp * rows, (comp + 1) * rows)
         for ri in range(2):
             for first in range(0, size, 8):
                 count = min(8, size - first)
@@ -395,14 +394,12 @@
                 applied[blocks_here, start : start + count, :] = jnp.swapaxes(tiles, 0, 1)
         mine = jnp.concatenate([applied[comp * rows + i] for i in range(rows)], axis=1)
         kept_rows = jnp.concatenate([basis[comp * rows + i] for i in range(rows)], axis=1)
-        return total + lax.dot_general(
+        total = total + lax.dot_general(
             jnp.concatenate(two_halves(mine), axis=0),
             kept_rows,
             (((1,), (1,)), ((), ())),
             preferred_element_type=jnp.float32,
         )
-
-    total = lax.fori_loop(0, COMPS, add, jnp.zeros((4 * size, 4 * kept), jnp.float32))
     total = total[: 2 * size] + total[2 * size :]
     total = total[:, : 2 * kept] + total[:, 2 * kept :]
     real, imag = total[:size], total[size:]
@@ -443,9 +440,8 @@
         size, radix = min(radix[0], count // stride), radix[1:] or radix
         total = value
         for step in range(1, size):
-            total = total + lax.ppermute(
-                value, axis, [(i, i ^ (step * stride)) for i in range(count)]
-            )
+            moved = lax.ppermute(value, axis, [(i, i ^ (step * stride)) for i in range(count)])
+            total = total + moved
         value = total
         stride *= size
     return value
@@ -484,13 +480,14 @@
     per = basis.shape[0] // groups
     mine = unpacked(over[...], kept)
     weight = weight_rows(mine[:vectors], mine[vectors:])
+    size = 2 * vectors
     for step in range(groups):
         first = partner(here, step, groups) * per + ship
-        size = 2 * vectors
-        for block in range(0, per - ship, 2):
-            value = weighted(weight, pair_of(basis, first + block))
-            outs[step][block * size : (block + 1) * size, :] = value[:, :LANES]
-            outs[step][(block + 1) * size : (block + 2) * size, :] = value[:, LANES:]
+        for block, count in spans(0, per - ship):
+            value = weighted(weight, beside(basis, first + block, count))
+            for i in range(count):
+                start = (block + i) * size
+                outs[step][start : start + size, :] = value[:, i * LANES : (i + 1) * LANES]
         outs[step][(per - ship) * size :, :] = over[...]
 
 
@@ -506,21 +503,23 @@
         there = unpacked(there, kept)
         weights.append(weight_rows(there[:vectors], there[vectors:]))
     full = None
-    for block in range(0, per, 2):
+    for block, count in spans(0, ship) + spans(ship, per):
         mine = here * per + block
         if block < ship:
-            total = weighted(weights[0], pair_of(basis, mine))
+            total = weighted(weights[0], beside(basis, mine, count))
             for weight, piece in zip(weights[1:], pieces):
-                total = total + weighted(weight, row_pairs(piece, block))
+                total = total + weighted(weight, halves_beside(piece, block, count))
         else:
-            start = (block - ship) * tall
-            total = parts[0][start : start + 2 * tall, :]
+            here_rows = slice((block - ship) * tall, (block - ship + count) * tall)
+            total = parts[0][here_rows, :]
             for part in parts[1:]:
-                total = total + part[start : start + 2 * tall, :]
-            total = jnp.concatenate([total[:tall], total[tall:]], axis=1)
-        rest = pair_of(applied, mine) - total
-        rest_ref[block] = rest[:, :LANES]
-        rest_ref[block + 1] = rest[:, LANES:]
+                total = total + part[here_rows, :]
+            total = jnp.concatenate(
+                [total[i * tall : (i + 1) * tall] for i in range(count)], axis=1
+            )
+        rest = beside(applied, mine, count) - total
+        for i in range(count):
+            rest_ref[block + i] = rest[:, i * LANES : (i + 1) * LANES]
         both = jnp.concatenate(two_halves(rest), axis=0)
         term = lax.dot_general(
             both, both, (((1,), (1,)), ((), ())), preferred_element_type=jnp.float32
@@ -543,20 +542,37 @@
     re = jnp.where(lane < vectors, gram[...], unit)
     im = jnp.concatenate([gram[:, vectors:], jnp.zeros((vectors, vectors), jnp.float32)], axis=1)
     pivots = jnp.ones(shape, jnp.float32)
-    for pivot in range(vectors):
-        row_re, row_im = re[pivot : pivot + 1], im[pivot : pivot + 1]
-        col_re = jnp.broadcast_to(re[:, pivot : pivot + 1], shape)
-        col_im = jnp.broadcast_to(im[:, pivot : pivot + 1], shape)
-        value = col_re[pivot : pivot + 1]
-        inverse = 1.0 / value
-        below = row > pivot
-        col_re = jnp.where(below, col_re * inverse, 0.0)
-        col_im = jnp.where(below, col_im * inverse, 0.0)
-        pivots = jnp.where(row == pivot, value, pivots)
+    link_re = link_im = jnp.zeros(shape, jnp.float32)
+    for first in range(0, vectors, 2):
+        second = first + 1
+        row0 = re[first:second], im[first:second]
+        row1 = re[second : second + 1], im[second : second + 1]
+        x0 = [jnp.broadcast_to(x[:, first:second], shape) for x in (re, im)]
+        x1 = [jnp.broadcast_to(x[:, second : second + 1], shape) for x in (re, im)]
+        top, low = x0[0][first:second], x1[0][second : second + 1]
+        b_re, b_im = x1[0][first:second], x1[1][first:second]
+        square = b_re * b_re + b_im * b_im
+        inverse = jnp.where(row > second, 1.0 / (top * low - square), 0.0)
+        f0_re = (x0[0] * low - (x1[0] * b_re + x1[1] * b_im)) * inverse
+        f0_im = (x0[1] * low - (x1[1] * b_re - x1[0] * b_im)) * inverse
+        f1_re = (x1[0] * top - (x0[0] * b_re - x0[1] * b_im)) * inverse
+        f1_im = (x1[1] * top - (x0[0] * b_im + x0[1] * b_re)) * inverse
+        here_first, here_second = row == first, row == second
+        share = 1.0 / top
+        pivots = jnp.where(
+            here_first, top, jnp.where(here_second, low - square * share, pivots)
+        )
+        link_re = jnp.where(here_second, b_re * share, link_re)
+        link_im = jnp.where(here_second, -b_im * share, link_im)
         re, im = (
-            re - (col_re * row_re - col_im * row_im),
-            im - (col_re * row_im + col_im * row_re),
+            re - ((f0_re * row0[0] - f0_im * row0[1]) + (f1_re * row1[0] - f1_im * row1[1])),
+            im - ((f0_re * row0[1] + f0_im * row0[0]) + (f1_re * row1[1] + f1_im * row1[0])),
         )
+    above_re, above_im = pltpu.roll(re, 1, 0), pltpu.roll(im, 1, 0)
+    re, im = (
+        re - (link_re * above_re - link_im * above_im),
+        im - (link_re * above_im + link_im * above_re),
+    )
     roots = 1.0 / jnp.sqrt(pivots)
     inv_re, inv_im = (re * roots)[:, vectors:], (im * roots)[:, vectors:]
     own = vectors // groups
@@ -573,12 +589,12 @@
     weight = jnp.concatenate(
         [jnp.concatenate([high, high], axis=1), jnp.concatenate([low, low], axis=1)], axis=0
     )
-    for block in range(0, rest.shape[0], 2):
-        full = weighted(weight, row_pairs(rest, block))
+    for block, count in spans(0, rest.shape[0]):
+        full = weighted(weight, halves_beside(rest, block, count))
         for step in range(groups):
             rows = slice(step * 2 * own, (step + 1) * 2 * own)
-            outs[step][block] = full[rows, :LANES]
-            outs[step][block + 1] = full[rows, LANES:]
+            for i in range(count):
+                outs[step][block + i] = full[rows, i * LANES : (i + 1) * LANES]
 
 
 def place_kernel(groups, own, rows, *refs):
@@ -636,13 +652,12 @@
     scale = 1.0 / (2 * COMPS * slices * sites * places)
     psi = tiles_of(search_block, vectors * 2 * COMPS)
     basis = tiles_of(kept_basis, kept * 2 * COMPS).reshape(kept, 2, blocks, LANES)
-    ship = per // 4 * 2 if per % rows == 0 else 0
+    ship = per * 11 // 24 if per % rows == 0 else 0
     links = tiles_of(gauge_links, 72)
     clover = tiles_of(clover_term, 144)
-    size = vectors // HALVES
-    rim = shape_of(size * COMPS // slices, rows, LANES)
-    field = shape_of(size * 2 * COMPS, rows, LANES)
-    work = size * rows * LANES
+    rim = shape_of(vectors * COMPS // slices, rows, LANES)
+    field = shape_of(vectors * 2 * COMPS, rows, LANES)
+    work = vectors * rows * LANES
     in_hbm = functools.partial(pltpu.with_memory_space_constraint, memory_space=pltpu.HBM)
 
     def swap(ahead, behind):
@@ -650,9 +665,9 @@
         up = [(i, (i + 1) % places) for i in range(places)]
         return lax.ppermute(ahead, "ta", down), lax.ppermute(behind, "ta", up)
 
-    def local(values, base):
+    def local(values):
         return call(
-            functools.partial(local_kernel, lattice, size, base),
+            functools.partial(local_kernel, lattice, vectors),
             (field,),
             values,
             links,
@@ -661,15 +676,14 @@
             flops=2000 * work,
         )[0]
 
-    opened = call(
+    psi, links, ahead, behind, *pieces = call(
         functools.partial(open_kernel, lattice, groups, vectors, kept, ship),
-        (rim,) * (2 * HALVES) + (shape_of(max(ship, 1), 2 * kept, LANES),) * (groups - 1),
+        (field, shape_of(*links.shape), rim, rim)
+        + (shape_of(max(ship, 1), 2 * kept, LANES),) * (groups - 1),
         in_hbm(psi),
         in_hbm(links),
         in_hbm(basis),
         scratch=[
-            pltpu.VMEM(psi.shape, jnp.float32),
-            pltpu.VMEM((18, rows, LANES), jnp.float32),
             pltpu.VMEM((groups - 1, kept, 2, -(-ship // rows) * rows or rows, LANES), jnp.float32),
             pltpu.SemaphoreType.DMA((groups + 1,)),
         ],
@@ -677,33 +691,30 @@
         grant=8,
         remote=(0, 1, 2),
     )
-    rims = [swap(opened[2 * which], opened[2 * which + 1]) for which in range(HALVES)]
-    pieces = exchanged([None, *opened[2 * HALVES :]], "ba")[1:] if ship else []
-    parts = []
-    for which in range(HALVES):
-        part = local(psi, which * size)
-        first, ahead, behind = call(
-            functools.partial(middle_kernel, lattice, size),
-            (field, rim, rim),
-            part,
-            links,
-            *rims[which],
-            flops=400 * work,
-        )
-        rims[which] = swap(ahead, behind)
-        parts.append(first)
+    rims = swap(ahead, behind)
+    pieces = exchanged([None, *pieces], "ba")[1:] if ship else []
+    part = local(psi)
+    first, ahead, behind = call(
+        functools.partial(middle_kernel, lattice, vectors),
+        (field, rim, rim),
+        part,
+        links,
+        *rims,
+        flops=400 * work,
+    )
+    rims = swap(ahead, behind)
     (basis_rows,) = call(
         functools.partial(basis_kernel, rows, kept),
         (jax.ShapeDtypeStruct((blocks, 4 * kept, LANES), jnp.bfloat16),),
         basis,
     )
-    parts = [local(first, 0) for first in parts]
+    part = local(first)
     applied, over = call(
         functools.partial(correlate_kernel, lattice, vectors, kept, scale),
         (shape_of(blocks, 2 * vectors, LANES), shape_of(2 * vectors * kept // LANES, LANES)),
-        *parts,
+        part,
         links,
-        *rims[0],
+        *rims,
         basis_rows,
         scratch=[pltpu.VMEM(psi.shape, jnp.float32)],
         flops=400 * work,
@@ -725,7 +736,8 @@
         *parts,
         *pieces,
     )
-    gram = summed(summed(gram, "ta", (2, 4)), "ba", (4,))
+    gram = summed(gram, "ta", (2, 4))
+    gram = summed(gram, "ba", (4,))
     piece = shape_of(per, 2 * own, LANES)
     pieces = call(
         functools.partial(ortho_kernel, groups, vectors),

time: 119 us -> 117 us (0.983)
  waiting for transfers between devices: 63.2 us -> 65.9 us
  starting transfers between devices: 32.8 us -> 30.2 us
  Pallas kernels: 21.4 us -> 19.3 us
    pallas_call x10, Pallas kernels: 21.4 us -> 19.3 us  [call(): pl.pallas_call(kernel, out_shape=tuple(outs), in_specs=[anywhere if i in...]
    ppermute x11, starting transfers between devices: 13.4 us -> 11.4 us  [summed(): lax.ppermute(value, axis, [(i, i ^ step * stride) for i in range(count)])]
    ppermute x11, waiting for transfers between devices: 8.28 us -> 10.2 us  [summed(): lax.ppermute(value, axis, [(i, i ^ step * stride) for i in range(count)])]
  transfers between devices with their start and end apart: 24 -> 24, of which waited for: 16 -> 15; matrix products, arithmetic and copies ran while one was open for 1% -> 1% of each run, Pallas kernels for 12% -> 11%
where the time goes in v6:
time: 117 us
  waiting for transfers between devices  65.9 us (56%)
  starting transfers between devices  30.2 us (26%)
  Pallas kernels  19.3 us (16%)
    ppermute x9, waiting for transfers between devices, exchanged(): out.append(lax.ppermute(values[step], axis, pairs))  46.4 us
    pallas_call x10, Pallas kernels, call(): pl.pallas_call(kernel, out_shape=tuple(outs), in_specs=[anywhere if i in...  19.3 us
    ppermute x9, starting transfers between devices, exchanged(): out.append(lax.ppermute(values[step], axis, pairs))  14.4 us
    ppermute x11, starting transfers between devices, summed(): lax.ppermute(value, axis, [(i, i ^ step * stride) for i in range(count)])  11.4 us
    ppermute x11, waiting for transfers between devices, summed(): lax.ppermute(value, axis, [(i, i ^ step * stride) for i in range(count)])  10.2 us
    ppermute x4, waiting for transfers between devices, swap(): return (lax.ppermute(ahead, 'ta', down), lax.ppermute(behind, 'ta', up))  9.34 us
    ppermute x4, starting transfers between devices, swap(): return (lax.ppermute(ahead, 'ta', down), lax.ppermute(behind, 'ta', up))  4.36 us
  transfers between devices with their start and end apart: 24, of which 15 were waited for; matrix products, arithmetic and copies ran while one was open for 1% of the time, Pallas kernels for 11%

profile of v6, /device:TPU:0, one launch (start us, length us, event | category | flops | bytes accessed | tf_op | source)
XLA Modules:
  0.0 116.9 jit_solution(5122858007999522051)
XLA Ops:
  0.6 2.3 %shard_map.59 = (f32[384,8,128]{2,1,0:T(8,128)S(1)}, f32[72,8,128]{2,1,0:T(8,128)S(1)}, f32[96,8,128]{2,1,0:T(8,128)S(1)}, f32[96,8,128]{2,1,0:T(8,128)S(1)}, f3...) custom-call(f32[384,8,128]{2,1,0:T(8,128)} %bitcast.33, f32[72,8,128]{2,1,0:T(8,128)} %bitcast.35, ...), custom_call_target="tpu_custom_call" | custom-call | flops 6553600 | bytes 8749056 | tf_op jit(solution)/shard_map/pallas_call | solution.py:622
  2.9 3.4 %collective-permute-start = (f32[96,8,128]{2,1,0:T(8,128)S(1)}, f32[96,8,128]{2,1,0:T(8,128)S(1)}, u32[]{:S(2)}, u32[]{:S(2)}) collective-permute-start(f32[96,8,128]{2,1,0:T(8,128)S(1)} %get-tuple-element.26), channel_id=1, source_target_pairs={{0,28},{4,0},{8,4},{12,8},{16,12},{20,16},{24,20},{28,24},{1,29},{... | collective-permute-start | bytes 1179656 | tf_op jit(solution)/shard_map/ppermute | solution.py:666
  6.4 4.6 %shard_map.60.part = f32[384,8,128]{2,1,0:T(8,128)S(1)} custom-call(f32[384,8,128]{2,1,0:T(8,128)S(1)} %get-tuple-element.24.psi, f32[72,8,128]{2,1,0:T(8,128)S(1)} %get-tuple-element.25.links, f32[144,8,128]{2,1,0:T(8,128)S(1)} %bitcast.31), custom_call_target="tpu_custom_call" | custom-call | flops 32768000 | bytes 4030464 | tf_op jit(solution)/shard_map/pallas_call | solution.py:622
  10.9 4.0 %collective-permute-done.rim_ahead = f32[96,8,128]{2,1,0:T(8,128)S(1)} collective-permute-done((f32[96,8,128]{2,1,0:T(8,128)S(1)}, f32[96,8,128]{2,1,0:T(8,128)S(1)}, u32[]{:S(2)}, u32[]{:S(2)}) %collective-permute-start) | collective-permute-done | bytes 393248 | tf_op jit(solution)/shard_map/ppermute | solution.py:666
  14.9 1.9 %collective-permute-done.1.rim_behind = f32[96,8,128]{2,1,0:T(8,128)S(1)} collective-permute-done((f32[96,8,128]{2,1,0:T(8,128)S(1)}, f32[96,8,128]{2,1,0:T(8,128)S(1)}, u32[]{:S(2)}, u32[]{:S(2)}) %collective-permute-start.1) | collective-permute-done | bytes 393248 | tf_op jit(solution)/shard_map/ppermute | solution.py:666
  18.8 1.6 %collective-permute-start.11 = (f32[11,64,128]{2,1,0:T(8,128)S(1)}, f32[11,64,128]{2,1,0:T(8,128)S(1)}, u32[]{:S(2)}, u32[]{:S(2)}) collective-permute-start(f32[11,64,128]{2,1,0:T(8,128)S(1)} %get-tuple-element.37), channel_id=1, source_target_pairs={{0,1},{1,0},{2,3},{3,2},{4,5},{5,4},{6,7},{7,6},{8,9},{9,8},{10,11... | collective-permute-start | bytes 1081352 | tf_op jit(solution)/shard_map/ppermute | solution.py:430
  21.3 4.6 %shard_map.62.part = f32[384,8,128]{2,1,0:T(8,128)S(1)} custom-call(f32[384,8,128]{2,1,0:T(8,128)S(1)} %get-tuple-element.28.psi, f32[72,8,128]{2,1,0:T(8,128)S(1)} %get-tuple-element.25.links, f32[144,8,128]{2,1,0:T(8,128)S(1)} %bitcast.32), custom_call_target="tpu_custom_call" | custom-call | flops 32768000 | bytes 4030464 | tf_op jit(solution)/shard_map/pallas_call | solution.py:622
  25.9 1.3 %collective-permute-done.2.rim_ahead = f32[96,8,128]{2,1,0:T(8,128)S(1)} collective-permute-done((f32[96,8,128]{2,1,0:T(8,128)S(1)}, f32[96,8,128]{2,1,0:T(8,128)S(1)}, u32[]{:S(2)}, u32[]{:S(2)}) %collective-permute-start.2) | collective-permute-done | bytes 393248 | tf_op jit(solution)/shard_map/ppermute | solution.py:666
  27.2 2.0 %collective-permute-done.3.rim_behind = f32[96,8,128]{2,1,0:T(8,128)S(1)} collective-permute-done((f32[96,8,128]{2,1,0:T(8,128)S(1)}, f32[96,8,128]{2,1,0:T(8,128)S(1)}, u32[]{:S(2)}, u32[]{:S(2)}) %collective-permute-start.3) | collective-permute-done | bytes 393248 | tf_op jit(solution)/shard_map/ppermute | solution.py:666
  29.3 2.0 %shard_map.64 = (f32[96,32,128]{2,1,0:T(8,128)S(1)}, f32[8,128]{1,0:T(8,128)S(1)}) custom-call(f32[384,8,128]{2,1,0:T(8,128)S(1)} %shard_map.62.part, f32[72,8,128]{2,1,0:T(8,128)S(1)} %get-tuple-element.25.links, f32[96,8,128]{2,1,0:T(8,128)S(1)} %collective-permute-done.2.rim_ahead, f32[96,8,128]{2,1,0:T(8,128)S(1)} %collective-permute-done.3.rim_behind, ...), custom_call_target="tpu_custom_call" | custom-call | flops 6553600 | bytes 7376896 | tf_op jit(solution)/shard_map/pallas_call | solution.py:622
  33.9 2.1 %collective-permute-start.7 = (f32[8,128]{1,0:T(8,128)S(1)}, f32[8,128]{1,0:T(8,128)S(1)}, u32[]{:S(2)}, u32[]{:S(2)}) collective-permute-start(f32[8,128]{1,0:T(8,128)S(1)} %add.33), channel_id=1, source_target_pairs={{0,24},{4,28},{8,16},{12,20},{16,8},{20,12},{24,0},{28,4},{1,25},{... | collective-permute-start | bytes 12296 | tf_op jit(solution)/shard_map/ppermute | solution.py:443
  36.0 2.6 %collective-permute-start.12 = (f32[11,64,128]{2,1,0:T(8,128)S(1)}, f32[11,64,128]{2,1,0:T(8,128)S(1)}, u32[]{:S(2)}, u32[]{:S(2)}) collective-permute-start(f32[11,64,128]{2,1,0:T(8,128)S(1)} %get-tuple-element.38), channel_id=1, source_target_pairs={{0,2},{1,3},{2,0},{3,1},{4,6},{5,7},{6,4},{7,5},{8,10},{9,11},{10,... | collective-permute-start | bytes 1081352 | tf_op jit(solution)/shard_map/ppermute | solution.py:430
  38.6 1.3 %collective-permute-start.13 = (f32[11,64,128]{2,1,0:T(8,128)S(1)}, f32[11,64,128]{2,1,0:T(8,128)S(1)}, u32[]{:S(2)}, u32[]{:S(2)}) collective-permute-start(f32[11,64,128]{2,1,0:T(8,128)S(1)} %get-tuple-element.39), channel_id=1, source_target_pairs={{0,3},{1,2},{2,1},{3,0},{4,7},{5,6},{6,5},{7,4},{8,11},{9,10},{10,... | collective-permute-start | bytes 1081352 | tf_op jit(solution)/shard_map/ppermute | solution.py:430
  40.5 2.5 %collective-permute-start.10 = (f32[424,128]{1,0:T(8,128)S(1)}, f32[424,128]{1,0:T(8,128)S(1)}, u32[]{:S(2)}, u32[]{:S(2)}) collective-permute-start(f32[424,128]{1,0:T(8,128)S(1)} %get-tuple-element.36), channel_id=1, source_target_pairs={{0,3},{1,2},{2,1},{3,0},{4,7},{5,6},{6,5},{7,4},{8,11},{9,10},{10,... | collective-permute-start | bytes 651272 | tf_op jit(solution)/shard_map/ppermute | solution.py:430
  43.1 1.9 %collective-permute-start.9 = (f32[424,128]{1,0:T(8,128)S(1)}, f32[424,128]{1,0:T(8,128)S(1)}, u32[]{:S(2)}, u32[]{:S(2)}) collective-permute-start(f32[424,128]{1,0:T(8,128)S(1)} %get-tuple-element.35), channel_id=1, source_target_pairs={{0,2},{1,3},{2,0},{3,1},{4,6},{5,7},{6,4},{7,5},{8,10},{9,11},{10,... | collective-permute-start | bytes 651272 | tf_op jit(solution)/shard_map/ppermute | solution.py:430
  45.0 27.5 %collective-permute-done.12.refs_5_ = f32[11,64,128]{2,1,0:T(8,128)S(1)} collective-permute-done((f32[11,64,128]{2,1,0:T(8,128)S(1)}, f32[11,64,128]{2,1,0:T(8,128)S(1)}, u32[]{:S(2)}, u32[]{:S(2)}) %collective-permute-start.12) | collective-permute-done | bytes 360480 | tf_op jit(solution)/shard_map/ppermute | solution.py:430
  72.5 15.9 %collective-permute-done.9.refs_2_ = f32[424,128]{1,0:T(8,128)S(1)} collective-permute-done((f32[424,128]{1,0:T(8,128)S(1)}, f32[424,128]{1,0:T(8,128)S(1)}, u32[]{:S(2)}, u32[]{:S(2)}) %collective-permute-start.9) | collective-permute-done | bytes 217120 | tf_op jit(solution)/shard_map/ppermute | solution.py:430
  92.3 1.9 %collective-permute-start.17 = (f32[16,32]{1,0:T(8,128)S(1)}, f32[16,32]{1,0:T(8,128)S(1)}, u32[]{:S(2)}, u32[]{:S(2)}) collective-permute-start(f32[16,32]{1,0:T(8,128)S(1)} %add.37), channel_id=1, source_target_pairs={{0,24},{4,28},{8,16},{12,20},{16,8},{20,12},{24,0},{28,4},{1,25},{... | collective-permute-start | bytes 6152 | tf_op jit(solution)/shard_map/ppermute | solution.py:443
  95.6 1.3 %collective-permute-done.17 = f32[16,32]{1,0:T(8,128)S(1)} collective-permute-done((f32[16,32]{1,0:T(8,128)S(1)}, f32[16,32]{1,0:T(8,128)S(1)}, u32[]{:S(2)}, u32[]{:S(2)}) %collective-permute-start.17) | collective-permute-done | bytes 2080 | tf_op jit(solution)/shard_map/ppermute | solution.py:443
  97.5 3.4 %collective-permute-start.19 = (f32[16,32]{1,0:T(8,128)S(1)}, f32[16,32]{1,0:T(8,128)S(1)}, u32[]{:S(2)}, u32[]{:S(2)}) collective-permute-start(f32[16,32]{1,0:T(8,128)S(1)} %add_add_fusion.1), channel_id=1, source_target_pairs={{0,2},{1,3},{2,0},{3,1},{4,6},{5,7},{6,4},{7,5},{8,10},{9,11},{10,... | collective-permute-start | bytes 6152 | tf_op jit(solution)/shard_map/ppermute | solution.py:443
  102.5 3.9 %collective-permute-done.20 = f32[16,32]{1,0:T(8,128)S(1)} collective-permute-done((f32[16,32]{1,0:T(8,128)S(1)}, f32[16,32]{1,0:T(8,128)S(1)}, u32[]{:S(2)}, u32[]{:S(2)}) %collective-permute-start.20) | collective-permute-done | bytes 2080 | tf_op jit(solution)/shard_map/ppermute | solution.py:443
  106.4 1.4 %shard_map.67 = (f32[24,8,128]{2,1,0:T(8,128)S(1)}, f32[24,8,128]{2,1,0:T(8,128)S(1)}, f32[24,8,128]{2,1,0:T(8,128)S(1)}, f32[24,8,128]{2,1,0:T(8,128)S(1)}) custom-call(f32[16,32]{1,0:T(8,128)S(1)} %add_add_fusion.gram, f32[24,32,128]{2,1,0:T(8,128)S(1)} %get-tuple-element.41.rest), custom_call_target="tpu_custom_call" | custom-call | bytes 788480 | tf_op jit(solution)/shard_map/pallas_call | solution.py:622
  108.8 3.5 %collective-permute-start.23 = (f32[24,8,128]{2,1,0:T(8,128)S(1)}, f32[24,8,128]{2,1,0:T(8,128)S(1)}, u32[]{:S(2)}, u32[]{:S(2)}) collective-permute-start(f32[24,8,128]{2,1,0:T(8,128)S(1)} %get-tuple-element.45), channel_id=1, source_target_pairs={{0,3},{1,2},{2,1},{3,0},{4,7},{5,6},{6,5},{7,4},{8,11},{9,10},{10,... | collective-permute-start | bytes 294920 | tf_op jit(solution)/shard_map/ppermute | solution.py:430
  114.3 1.8 %collective-permute-done.23.refs_3_ = f32[24,8,128]{2,1,0:T(8,128)S(1)} collective-permute-done((f32[24,8,128]{2,1,0:T(8,128)S(1)}, f32[24,8,128]{2,1,0:T(8,128)S(1)}, u32[]{:S(2)}, u32[]{:S(2)}) %collective-permute-start.23) | collective-permute-done | bytes 98336 | tf_op jit(solution)/shard_map/ppermute | solution.py:430
  (45 shorter events, 17.3 us)
Async XLA Ops:
  2.9 12.0 %collective-permute-start = (f32[96,8,128]{2,1,0:T(8,128)S(1)}, f32[96,8,128]{2,1,0:T(8,128)S(1)}, u32[]{:S(2)}, u32[]{:S(2)}) collective-permute-start(f32[96,8,128]{2,1,0:T(8,128)S(1)} %get-tuple-element.26), channel_id=1, source_target_pairs={{0,28},{4,0},{8,4},{12,8},{16,12},{20,16},{24,20},{28,24},{1,29},{... | collective-permute-start | bytes 1179656 | tf_op jit(solution)/shard_map/ppermute | solution.py:666
  6.3 10.5 %collective-permute-start.1 = (f32[96,8,128]{2,1,0:T(8,128)S(1)}, f32[96,8,128]{2,1,0:T(8,128)S(1)}, u32[]{:S(2)}, u32[]{:S(2)}) collective-permute-start(f32[96,8,128]{2,1,0:T(8,128)S(1)} %get-tuple-element.27), channel_id=1, source_target_pairs={{0,4},{4,8},{8,12},{12,16},{16,20},{20,24},{24,28},{28,0},{1,5},{5... | collective-permute-start | bytes 1179656 | tf_op jit(solution)/shard_map/ppermute | solution.py:666
  17.9 9.4 %collective-permute-start.2 = (f32[96,8,128]{2,1,0:T(8,128)S(1)}, f32[96,8,128]{2,1,0:T(8,128)S(1)}, u32[]{:S(2)}, u32[]{:S(2)}) collective-permute-start(f32[96,8,128]{2,1,0:T(8,128)S(1)} %get-tuple-element.29), channel_id=1, source_target_pairs={{0,28},{4,0},{8,4},{12,8},{16,12},{20,16},{24,20},{28,24},{1,29},{... | collective-permute-start | bytes 1179656 | tf_op jit(solution)/shard_map/ppermute | solution.py:666
  18.8 10.5 %collective-permute-start.3 = (f32[96,8,128]{2,1,0:T(8,128)S(1)}, f32[96,8,128]{2,1,0:T(8,128)S(1)}, u32[]{:S(2)}, u32[]{:S(2)}) collective-permute-start(f32[96,8,128]{2,1,0:T(8,128)S(1)} %get-tuple-element.30), channel_id=1, source_target_pairs={{0,4},{4,8},{8,12},{12,16},{16,20},{20,24},{24,28},{28,0},{1,5},{5... | collective-permute-start | bytes 1179656 | tf_op jit(solution)/shard_map/ppermute | solution.py:666
  18.8 24.3 %collective-permute-start.11 = (f32[11,64,128]{2,1,0:T(8,128)S(1)}, f32[11,64,128]{2,1,0:T(8,128)S(1)}, u32[]{:S(2)}, u32[]{:S(2)}) collective-permute-start(f32[11,64,128]{2,1,0:T(8,128)S(1)} %get-tuple-element.37), channel_id=1, source_target_pairs={{0,1},{1,0},{2,3},{3,2},{4,5},{5,4},{6,7},{7,6},{8,9},{9,8},{10,11... | collective-permute-start | bytes 1081352 | tf_op jit(solution)/shard_map/ppermute | solution.py:430
  31.3 1.2 %collective-permute-start.4 = (f32[8,128]{1,0:T(8,128)S(1)}, f32[8,128]{1,0:T(8,128)S(1)}, u32[]{:S(2)}, u32[]{:S(2)}) collective-permute-start(f32[8,128]{1,0:T(8,128)S(1)} %get-tuple-element.31), channel_id=1, source_target_pairs={{0,4},{4,0},{8,12},{12,8},{16,20},{20,16},{24,28},{28,24},{1,5},{5... | collective-permute-start | bytes 12296 | tf_op jit(solution)/shard_map/ppermute | solution.py:443
  32.5 6.1 %collective-permute-start.5 = (f32[8,128]{1,0:T(8,128)S(1)}, f32[8,128]{1,0:T(8,128)S(1)}, u32[]{:S(2)}, u32[]{:S(2)}) collective-permute-start(f32[8,128]{1,0:T(8,128)S(1)} %add.33), channel_id=1, source_target_pairs={{0,8},{4,12},{8,0},{12,4},{16,24},{20,28},{24,16},{28,20},{1,9},{5... | collective-permute-start | bytes 12296 | tf_op jit(solution)/shard_map/ppermute | solution.py:443
  33.5 6.4 %collective-permute-start.6 = (f32[8,128]{1,0:T(8,128)S(1)}, f32[8,128]{1,0:T(8,128)S(1)}, u32[]{:S(2)}, u32[]{:S(2)}) collective-permute-start(f32[8,128]{1,0:T(8,128)S(1)} %add.33), channel_id=1, source_target_pairs={{0,16},{4,20},{8,24},{12,28},{16,0},{20,4},{24,8},{28,12},{1,17},{... | collective-permute-start | bytes 12296 | tf_op jit(solution)/shard_map/ppermute | solution.py:443
  33.9 6.1 %collective-permute-start.7 = (f32[8,128]{1,0:T(8,128)S(1)}, f32[8,128]{1,0:T(8,128)S(1)}, u32[]{:S(2)}, u32[]{:S(2)}) collective-permute-start(f32[8,128]{1,0:T(8,128)S(1)} %add.33), channel_id=1, source_target_pairs={{0,24},{4,28},{8,16},{12,20},{16,8},{20,12},{24,0},{28,4},{1,25},{... | collective-permute-start | bytes 12296 | tf_op jit(solution)/shard_map/ppermute | solution.py:443
  36.0 36.5 %collective-permute-start.12 = (f32[11,64,128]{2,1,0:T(8,128)S(1)}, f32[11,64,128]{2,1,0:T(8,128)S(1)}, u32[]{:S(2)}, u32[]{:S(2)}) collective-permute-start(f32[11,64,128]{2,1,0:T(8,128)S(1)} %get-tuple-element.38), channel_id=1, source_target_pairs={{0,2},{1,3},{2,0},{3,1},{4,6},{5,7},{6,4},{7,5},{8,10},{9,11},{10,... | collective-permute-start | bytes 1081352 | tf_op jit(solution)/shard_map/ppermute | solution.py:430
  38.6 33.9 %collective-permute-start.13 = (f32[11,64,128]{2,1,0:T(8,128)S(1)}, f32[11,64,128]{2,1,0:T(8,128)S(1)}, u32[]{:S(2)}, u32[]{:S(2)}) collective-permute-start(f32[11,64,128]{2,1,0:T(8,128)S(1)} %get-tuple-element.39), channel_id=1, source_target_pairs={{0,3},{1,2},{2,1},{3,0},{4,7},{5,6},{6,5},{7,4},{8,11},{9,10},{10,... | collective-permute-start | bytes 1081352 | tf_op jit(solution)/shard_map/ppermute | solution.py:430
  40.5 31.9 %collective-permute-start.10 = (f32[424,128]{1,0:T(8,128)S(1)}, f32[424,128]{1,0:T(8,128)S(1)}, u32[]{:S(2)}, u32[]{:S(2)}) collective-permute-start(f32[424,128]{1,0:T(8,128)S(1)} %get-tuple-element.36), channel_id=1, source_target_pairs={{0,3},{1,2},{2,1},{3,0},{4,7},{5,6},{6,5},{7,4},{8,11},{9,10},{10,... | collective-permute-start | bytes 651272 | tf_op jit(solution)/shard_map/ppermute | solution.py:430
  43.1 29.4 %collective-permute-start.8 = (f32[424,128]{1,0:T(8,128)S(1)}, f32[424,128]{1,0:T(8,128)S(1)}, u32[]{:S(2)}, u32[]{:S(2)}) collective-permute-start(f32[424,128]{1,0:T(8,128)S(1)} %get-tuple-element.34), channel_id=1, source_target_pairs={{0,1},{1,0},{2,3},{3,2},{4,5},{5,4},{6,7},{7,6},{8,9},{9,8},{10,11... | collective-permute-start | bytes 651272 | tf_op jit(solution)/shard_map/ppermute | solution.py:430
  43.1 45.3 %collective-permute-start.9 = (f32[424,128]{1,0:T(8,128)S(1)}, f32[424,128]{1,0:T(8,128)S(1)}, u32[]{:S(2)}, u32[]{:S(2)}) collective-permute-start(f32[424,128]{1,0:T(8,128)S(1)} %get-tuple-element.35), channel_id=1, source_target_pairs={{0,2},{1,3},{2,0},{3,1},{4,6},{5,7},{6,4},{7,5},{8,10},{9,11},{10,... | collective-permute-start | bytes 651272 | tf_op jit(solution)/shard_map/ppermute | solution.py:430
  89.6 1.2 %collective-permute-start.14 = (f32[16,32]{1,0:T(8,128)S(1)}, f32[16,32]{1,0:T(8,128)S(1)}, u32[]{:S(2)}, u32[]{:S(2)}) collective-permute-start(f32[16,32]{1,0:T(8,128)S(1)} %get-tuple-element.40), channel_id=1, source_target_pairs={{0,4},{4,0},{8,12},{12,8},{16,20},{20,16},{24,28},{28,24},{1,5},{5... | collective-permute-start | bytes 6152 | tf_op jit(solution)/shard_map/ppermute | solution.py:443
  90.8 3.7 %collective-permute-start.15 = (f32[16,32]{1,0:T(8,128)S(1)}, f32[16,32]{1,0:T(8,128)S(1)}, u32[]{:S(2)}, u32[]{:S(2)}) collective-permute-start(f32[16,32]{1,0:T(8,128)S(1)} %add.37), channel_id=1, source_target_pairs={{0,8},{4,12},{8,0},{12,4},{16,24},{20,28},{24,16},{28,20},{1,9},{5... | collective-permute-start | bytes 6152 | tf_op jit(solution)/shard_map/ppermute | solution.py:443
  91.9 3.7 %collective-permute-start.16 = (f32[16,32]{1,0:T(8,128)S(1)}, f32[16,32]{1,0:T(8,128)S(1)}, u32[]{:S(2)}, u32[]{:S(2)}) collective-permute-start(f32[16,32]{1,0:T(8,128)S(1)} %add.37), channel_id=1, source_target_pairs={{0,16},{4,20},{8,24},{12,28},{16,0},{20,4},{24,8},{28,12},{1,17},{... | collective-permute-start | bytes 6152 | tf_op jit(solution)/shard_map/ppermute | solution.py:443
  92.3 4.5 %collective-permute-start.17 = (f32[16,32]{1,0:T(8,128)S(1)}, f32[16,32]{1,0:T(8,128)S(1)}, u32[]{:S(2)}, u32[]{:S(2)}) collective-permute-start(f32[16,32]{1,0:T(8,128)S(1)} %add.37), channel_id=1, source_target_pairs={{0,24},{4,28},{8,16},{12,20},{16,8},{20,12},{24,0},{28,4},{1,25},{... | collective-permute-start | bytes 6152 | tf_op jit(solution)/shard_map/ppermute | solution.py:443
  96.9 4.4 %collective-permute-start.18 = (f32[16,32]{1,0:T(8,128)S(1)}, f32[16,32]{1,0:T(8,128)S(1)}, u32[]{:S(2)}, u32[]{:S(2)}) collective-permute-start(f32[16,32]{1,0:T(8,128)S(1)} %add_add_fusion.1), channel_id=1, source_target_pairs={{0,1},{1,0},{2,3},{3,2},{4,5},{5,4},{6,7},{7,6},{8,9},{9,8},{10,11... | collective-permute-start | bytes 6152 | tf_op jit(solution)/shard_map/ppermute | solution.py:443
  97.5 5.0 %collective-permute-start.19 = (f32[16,32]{1,0:T(8,128)S(1)}, f32[16,32]{1,0:T(8,128)S(1)}, u32[]{:S(2)}, u32[]{:S(2)}) collective-permute-start(f32[16,32]{1,0:T(8,128)S(1)} %add_add_fusion.1), channel_id=1, source_target_pairs={{0,2},{1,3},{2,0},{3,1},{4,6},{5,7},{6,4},{7,5},{8,10},{9,11},{10,... | collective-permute-start | bytes 6152 | tf_op jit(solution)/shard_map/ppermute | solution.py:443
  100.9 5.5 %collective-permute-start.20 = (f32[16,32]{1,0:T(8,128)S(1)}, f32[16,32]{1,0:T(8,128)S(1)}, u32[]{:S(2)}, u32[]{:S(2)}) collective-permute-start(f32[16,32]{1,0:T(8,128)S(1)} %add_add_fusion.1), channel_id=1, source_target_pairs={{0,3},{1,2},{2,1},{3,0},{4,7},{5,6},{6,5},{7,4},{8,11},{9,10},{10,... | collective-permute-start | bytes 6152 | tf_op jit(solution)/shard_map/ppermute | solution.py:443
  107.9 6.4 %collective-permute-start.21 = (f32[24,8,128]{2,1,0:T(8,128)S(1)}, f32[24,8,128]{2,1,0:T(8,128)S(1)}, u32[]{:S(2)}, u32[]{:S(2)}) collective-permute-start(f32[24,8,128]{2,1,0:T(8,128)S(1)} %get-tuple-element.43), channel_id=1, source_target_pairs={{0,1},{1,0},{2,3},{3,2},{4,5},{5,4},{6,7},{7,6},{8,9},{9,8},{10,11... | collective-permute-start | bytes 294920 | tf_op jit(solution)/shard_map/ppermute | solution.py:430
  107.9 6.3 %collective-permute-start.22 = (f32[24,8,128]{2,1,0:T(8,128)S(1)}, f32[24,8,128]{2,1,0:T(8,128)S(1)}, u32[]{:S(2)}, u32[]{:S(2)}) collective-permute-start(f32[24,8,128]{2,1,0:T(8,128)S(1)} %get-tuple-element.44), channel_id=1, source_target_pairs={{0,2},{1,3},{2,0},{3,1},{4,6},{5,7},{6,4},{7,5},{8,10},{9,11},{10,... | collective-permute-start | bytes 294920 | tf_op jit(solution)/shard_map/ppermute | solution.py:430
  108.8 7.3 %collective-permute-start.23 = (f32[24,8,128]{2,1,0:T(8,128)S(1)}, f32[24,8,128]{2,1,0:T(8,128)S(1)}, u32[]{:S(2)}, u32[]{:S(2)}) collective-permute-start(f32[24,8,128]{2,1,0:T(8,128)S(1)} %get-tuple-element.45), channel_id=1, source_target_pairs={{0,3},{1,2},{2,1},{3,0},{4,7},{5,6},{6,5},{7,4},{8,11},{9,10},{10,... | collective-permute-start | bytes 294920 | tf_op jit(solution)/shard_map/ppermute | solution.py:430
  (2 other events, 19.7 us)

commit v7 on v6

--- a/solution.py
+++ b/solution.py
@@ -10,6 +10,7 @@
 
 HOPPING = 0.13
 LANES = 128
+CHUNKS = 4
 COMPS = 12
 PROJECT = (
     ((1, 1), (0, 1)),
@@ -200,27 +201,36 @@
     held, sems = refs[groups + 3 :]
     here = lax.axis_index("ba")
     rows, per = lattice.rows, basis.shape[2] // groups
-    fields = pltpu.make_async_copy(psi_ref, psi, sems.at[0])
-    links_in = pltpu.make_async_copy(links_ref, links, sems.at[1])
+    vectors_each = vectors // CHUNKS if vectors % CHUNKS == 0 else vectors
+    chunks = vectors // vectors_each
+    size = vectors_each * 2 * COMPS
+    fields = [
+        pltpu.make_async_copy(
+            psi_ref.at[pl.ds(i * size, size)], psi.at[pl.ds(i * size, size)], sems.at[groups + i]
+        )
+        for i in range(chunks)
+    ]
+    links_in = pltpu.make_async_copy(links_ref, links, sems.at[0])
     kept_in = []
     for step in range(1, groups if ship else 1):
         start = pl.multiple_of(partner(here, step, groups) * per, rows)
         kept_in.append(
             pltpu.make_async_copy(
-                basis.at[:, :, pl.ds(start, held.shape[3]), :], held.at[step - 1], sems.at[1 + step]
+                basis.at[:, :, pl.ds(start, held.shape[3]), :], held.at[step - 1], sems.at[step]
             )
         )
-    for copy in (links_in, fields, *kept_in):
+    for copy in (links_in, *fields, *kept_in):
         copy.start()
     lattice.masks()
     links_in.wait()
-    fields.wait()
 
     def body(vector, carry):
         pack_rim(lattice, load_spinor(psi, vector), links, ahead_ref, behind_ref, vector)
         return carry
 
-    lax.fori_loop(0, vectors, body, 0, unroll=2)
+    for i, copy in enumerate(fields):
+        copy.wait()
+        lax.fori_loop(i * vectors_each, (i + 1) * vectors_each, body, 0, unroll=2)
     for step, copy in enumerate(kept_in):
         copy.wait()
 
@@ -345,7 +355,7 @@
         pack_rim(lattice, load_spinor(out, vector), links, ahead_ref, behind_ref, vector)
         return carry
 
-    lax.fori_loop(0, vectors, body, 0)
+    lax.fori_loop(0, vectors, body, 0, unroll=2)
 
 
 def two_halves(value):
@@ -663,7 +673,8 @@
     def swap(ahead, behind):
         down = [(i, (i + places - 1) % places) for i in range(places)]
         up = [(i, (i + 1) % places) for i in range(places)]
-        return lax.ppermute(ahead, "ta", down), lax.ppermute(behind, "ta", up)
+        second = lax.ppermute(behind, "ta", up)
+        return lax.ppermute(ahead, "ta", down), second
 
     def local(values):
         return call(
@@ -685,7 +696,7 @@
         in_hbm(basis),
         scratch=[
             pltpu.VMEM((groups - 1, kept, 2, -(-ship // rows) * rows or rows, LANES), jnp.float32),
-            pltpu.SemaphoreType.DMA((groups + 1,)),
+            pltpu.SemaphoreType.DMA((groups + CHUNKS,)),
         ],
         flops=400 * work,
         grant=8,

time: 117 us -> 117 us (level)
  no operation moved by 1% of the time
where the time goes in v7:
time: 117 us
  waiting for transfers between devices  65.9 us (56%)
  starting transfers between devices  30.1 us (26%)
  Pallas kernels  19.2 us (16%)
    ppermute x9, waiting for transfers between devices, exchanged(): out.append(lax.ppermute(values[step], axis, pairs))  46.4 us
    pallas_call x10, Pallas kernels, call(): pl.pallas_call(kernel, out_shape=tuple(outs), in_specs=[anywhere if i in...  19.2 us
    ppermute x9, starting transfers between devices, exchanged(): out.append(lax.ppermute(values[step], axis, pairs))  14.4 us
    ppermute x11, starting transfers between devices, summed(): lax.ppermute(value, axis, [(i, i ^ step * stride) for i in range(count)])  11.4 us
    ppermute x11, waiting for transfers between devices, summed(): lax.ppermute(value, axis, [(i, i ^ step * stride) for i in range(count)])  10.1 us
    ppermute x2, waiting for transfers between devices, swap(): return (lax.ppermute(ahead, 'ta', down), second)  5.37 us
    ppermute x2, starting transfers between devices, swap(): return (lax.ppermute(ahead, 'ta', down), second)  4.35 us
    ppermute x2, waiting for transfers between devices, swap(): second = lax.ppermute(behind, 'ta', up)  3.96 us
  transfers between devices with their start and end apart: 24, of which 15 were waited for; matrix products, arithmetic and copies ran while one was open for 1% of the time, Pallas kernels for 11%

profile of v7, /device:TPU:0, one launch (start us, length us, event | category | flops | bytes accessed | tf_op | source)
XLA Modules:
  0.0 116.7 jit_solution(18011746501492885932)
XLA Ops:
  0.6 2.1 %shard_map.59 = (f32[384,8,128]{2,1,0:T(8,128)S(1)}, f32[72,8,128]{2,1,0:T(8,128)S(1)}, f32[96,8,128]{2,1,0:T(8,128)S(1)}, f32[96,8,128]{2,1,0:T(8,128)S(1)}, f3...) custom-call(f32[384,8,128]{2,1,0:T(8,128)} %bitcast.33, f32[72,8,128]{2,1,0:T(8,128)} %bitcast.35, ...), custom_call_target="tpu_custom_call" | custom-call | flops 6553600 | bytes 8749056 | tf_op jit(solution)/shard_map/pallas_call | solution.py:632
  2.8 3.4 %collective-permute-start = (f32[96,8,128]{2,1,0:T(8,128)S(1)}, f32[96,8,128]{2,1,0:T(8,128)S(1)}, u32[]{:S(2)}, u32[]{:S(2)}) collective-permute-start(f32[96,8,128]{2,1,0:T(8,128)S(1)} %get-tuple-element.26), channel_id=1, source_target_pairs={{0,28},{4,0},{8,4},{12,8},{16,12},{20,16},{24,20},{28,24},{1,29},{... | collective-permute-start | bytes 1179656 | tf_op jit(solution)/shard_map/ppermute | solution.py:677
  6.2 4.6 %shard_map.60.part = f32[384,8,128]{2,1,0:T(8,128)S(1)} custom-call(f32[384,8,128]{2,1,0:T(8,128)S(1)} %get-tuple-element.24.psi, f32[72,8,128]{2,1,0:T(8,128)S(1)} %get-tuple-element.25.links, f32[144,8,128]{2,1,0:T(8,128)S(1)} %bitcast.31), custom_call_target="tpu_custom_call" | custom-call | flops 32768000 | bytes 4030464 | tf_op jit(solution)/shard_map/pallas_call | solution.py:632
  10.8 4.0 %collective-permute-done.rim_ahead = f32[96,8,128]{2,1,0:T(8,128)S(1)} collective-permute-done((f32[96,8,128]{2,1,0:T(8,128)S(1)}, f32[96,8,128]{2,1,0:T(8,128)S(1)}, u32[]{:S(2)}, u32[]{:S(2)}) %collective-permute-start) | collective-permute-done | bytes 393248 | tf_op jit(solution)/shard_map/ppermute | solution.py:677
  14.8 1.9 %collective-permute-done.1.rim_behind = f32[96,8,128]{2,1,0:T(8,128)S(1)} collective-permute-done((f32[96,8,128]{2,1,0:T(8,128)S(1)}, f32[96,8,128]{2,1,0:T(8,128)S(1)}, u32[]{:S(2)}, u32[]{:S(2)}) %collective-permute-start.1) | collective-permute-done | bytes 393248 | tf_op jit(solution)/shard_map/ppermute | solution.py:676
  18.6 1.6 %collective-permute-start.11 = (f32[11,64,128]{2,1,0:T(8,128)S(1)}, f32[11,64,128]{2,1,0:T(8,128)S(1)}, u32[]{:S(2)}, u32[]{:S(2)}) collective-permute-start(f32[11,64,128]{2,1,0:T(8,128)S(1)} %get-tuple-element.37), channel_id=1, source_target_pairs={{0,1},{1,0},{2,3},{3,2},{4,5},{5,4},{6,7},{7,6},{8,9},{9,8},{10,11... | collective-permute-start | bytes 1081352 | tf_op jit(solution)/shard_map/ppermute | solution.py:440
  21.2 4.6 %shard_map.62.part = f32[384,8,128]{2,1,0:T(8,128)S(1)} custom-call(f32[384,8,128]{2,1,0:T(8,128)S(1)} %get-tuple-element.28.psi, f32[72,8,128]{2,1,0:T(8,128)S(1)} %get-tuple-element.25.links, f32[144,8,128]{2,1,0:T(8,128)S(1)} %bitcast.32), custom_call_target="tpu_custom_call" | custom-call | flops 32768000 | bytes 4030464 | tf_op jit(solution)/shard_map/pallas_call | solution.py:632
  25.7 1.3 %collective-permute-done.2.rim_ahead = f32[96,8,128]{2,1,0:T(8,128)S(1)} collective-permute-done((f32[96,8,128]{2,1,0:T(8,128)S(1)}, f32[96,8,128]{2,1,0:T(8,128)S(1)}, u32[]{:S(2)}, u32[]{:S(2)}) %collective-permute-start.2) | collective-permute-done | bytes 393248 | tf_op jit(solution)/shard_map/ppermute | solution.py:677
  27.1 2.0 %collective-permute-done.3.rim_behind = f32[96,8,128]{2,1,0:T(8,128)S(1)} collective-permute-done((f32[96,8,128]{2,1,0:T(8,128)S(1)}, f32[96,8,128]{2,1,0:T(8,128)S(1)}, u32[]{:S(2)}, u32[]{:S(2)}) %collective-permute-start.3) | collective-permute-done | bytes 393248 | tf_op jit(solution)/shard_map/ppermute | solution.py:676
  29.1 2.0 %shard_map.64 = (f32[96,32,128]{2,1,0:T(8,128)S(1)}, f32[8,128]{1,0:T(8,128)S(1)}) custom-call(f32[384,8,128]{2,1,0:T(8,128)S(1)} %shard_map.62.part, f32[72,8,128]{2,1,0:T(8,128)S(1)} %get-tuple-element.25.links, f32[96,8,128]{2,1,0:T(8,128)S(1)} %collective-permute-done.2.rim_ahead, f32[96,8,128]{2,1,0:T(8,128)S(1)} %collective-permute-done.3.rim_behind, ...), custom_call_target="tpu_custom_call" | custom-call | flops 6553600 | bytes 7376896 | tf_op jit(solution)/shard_map/pallas_call | solution.py:632
  33.7 2.1 %collective-permute-start.7 = (f32[8,128]{1,0:T(8,128)S(1)}, f32[8,128]{1,0:T(8,128)S(1)}, u32[]{:S(2)}, u32[]{:S(2)}) collective-permute-start(f32[8,128]{1,0:T(8,128)S(1)} %add.33), channel_id=1, source_target_pairs={{0,24},{4,28},{8,16},{12,20},{16,8},{20,12},{24,0},{28,4},{1,25},{... | collective-permute-start | bytes 12296 | tf_op jit(solution)/shard_map/ppermute | solution.py:453
  35.8 2.6 %collective-permute-start.12 = (f32[11,64,128]{2,1,0:T(8,128)S(1)}, f32[11,64,128]{2,1,0:T(8,128)S(1)}, u32[]{:S(2)}, u32[]{:S(2)}) collective-permute-start(f32[11,64,128]{2,1,0:T(8,128)S(1)} %get-tuple-element.38), channel_id=1, source_target_pairs={{0,2},{1,3},{2,0},{3,1},{4,6},{5,7},{6,4},{7,5},{8,10},{9,11},{10,... | collective-permute-start | bytes 1081352 | tf_op jit(solution)/shard_map/ppermute | solution.py:440
  38.4 1.3 %collective-permute-start.13 = (f32[11,64,128]{2,1,0:T(8,128)S(1)}, f32[11,64,128]{2,1,0:T(8,128)S(1)}, u32[]{:S(2)}, u32[]{:S(2)}) collective-permute-start(f32[11,64,128]{2,1,0:T(8,128)S(1)} %get-tuple-element.39), channel_id=1, source_target_pairs={{0,3},{1,2},{2,1},{3,0},{4,7},{5,6},{6,5},{7,4},{8,11},{9,10},{10,... | collective-permute-start | bytes 1081352 | tf_op jit(solution)/shard_map/ppermute | solution.py:440
  40.4 2.5 %collective-permute-start.10 = (f32[424,128]{1,0:T(8,128)S(1)}, f32[424,128]{1,0:T(8,128)S(1)}, u32[]{:S(2)}, u32[]{:S(2)}) collective-permute-start(f32[424,128]{1,0:T(8,128)S(1)} %get-tuple-element.36), channel_id=1, source_target_pairs={{0,3},{1,2},{2,1},{3,0},{4,7},{5,6},{6,5},{7,4},{8,11},{9,10},{10,... | collective-permute-start | bytes 651272 | tf_op jit(solution)/shard_map/ppermute | solution.py:440
  42.9 1.9 %collective-permute-start.9 = (f32[424,128]{1,0:T(8,128)S(1)}, f32[424,128]{1,0:T(8,128)S(1)}, u32[]{:S(2)}, u32[]{:S(2)}) collective-permute-start(f32[424,128]{1,0:T(8,128)S(1)} %get-tuple-element.35), channel_id=1, source_target_pairs={{0,2},{1,3},{2,0},{3,1},{4,6},{5,7},{6,4},{7,5},{8,10},{9,11},{10,... | collective-permute-start | bytes 651272 | tf_op jit(solution)/shard_map/ppermute | solution.py:440
  44.8 27.5 %collective-permute-done.12.refs_5_ = f32[11,64,128]{2,1,0:T(8,128)S(1)} collective-permute-done((f32[11,64,128]{2,1,0:T(8,128)S(1)}, f32[11,64,128]{2,1,0:T(8,128)S(1)}, u32[]{:S(2)}, u32[]{:S(2)}) %collective-permute-start.12) | collective-permute-done | bytes 360480 | tf_op jit(solution)/shard_map/ppermute | solution.py:440
  72.3 15.9 %collective-permute-done.9.refs_2_ = f32[424,128]{1,0:T(8,128)S(1)} collective-permute-done((f32[424,128]{1,0:T(8,128)S(1)}, f32[424,128]{1,0:T(8,128)S(1)}, u32[]{:S(2)}, u32[]{:S(2)}) %collective-permute-start.9) | collective-permute-done | bytes 217120 | tf_op jit(solution)/shard_map/ppermute | solution.py:440
  92.2 1.9 %collective-permute-start.17 = (f32[16,32]{1,0:T(8,128)S(1)}, f32[16,32]{1,0:T(8,128)S(1)}, u32[]{:S(2)}, u32[]{:S(2)}) collective-permute-start(f32[16,32]{1,0:T(8,128)S(1)} %add.37), channel_id=1, source_target_pairs={{0,24},{4,28},{8,16},{12,20},{16,8},{20,12},{24,0},{28,4},{1,25},{... | collective-permute-start | bytes 6152 | tf_op jit(solution)/shard_map/ppermute | solution.py:453
  95.5 1.3 %collective-permute-done.17 = f32[16,32]{1,0:T(8,128)S(1)} collective-permute-done((f32[16,32]{1,0:T(8,128)S(1)}, f32[16,32]{1,0:T(8,128)S(1)}, u32[]{:S(2)}, u32[]{:S(2)}) %collective-permute-start.17) | collective-permute-done | bytes 2080 | tf_op jit(solution)/shard_map/ppermute | solution.py:453
  97.4 3.4 %collective-permute-start.19 = (f32[16,32]{1,0:T(8,128)S(1)}, f32[16,32]{1,0:T(8,128)S(1)}, u32[]{:S(2)}, u32[]{:S(2)}) collective-permute-start(f32[16,32]{1,0:T(8,128)S(1)} %add_add_fusion.1), channel_id=1, source_target_pairs={{0,2},{1,3},{2,0},{3,1},{4,6},{5,7},{6,4},{7,5},{8,10},{9,11},{10,... | collective-permute-start | bytes 6152 | tf_op jit(solution)/shard_map/ppermute | solution.py:453
  102.4 3.9 %collective-permute-done.20 = f32[16,32]{1,0:T(8,128)S(1)} collective-permute-done((f32[16,32]{1,0:T(8,128)S(1)}, f32[16,32]{1,0:T(8,128)S(1)}, u32[]{:S(2)}, u32[]{:S(2)}) %collective-permute-start.20) | collective-permute-done | bytes 2080 | tf_op jit(solution)/shard_map/ppermute | solution.py:453
  106.3 1.4 %shard_map.67 = (f32[24,8,128]{2,1,0:T(8,128)S(1)}, f32[24,8,128]{2,1,0:T(8,128)S(1)}, f32[24,8,128]{2,1,0:T(8,128)S(1)}, f32[24,8,128]{2,1,0:T(8,128)S(1)}) custom-call(f32[16,32]{1,0:T(8,128)S(1)} %add_add_fusion.gram, f32[24,32,128]{2,1,0:T(8,128)S(1)} %get-tuple-element.41.rest), custom_call_target="tpu_custom_call" | custom-call | bytes 788480 | tf_op jit(solution)/shard_map/pallas_call | solution.py:632
  108.6 3.5 %collective-permute-start.23 = (f32[24,8,128]{2,1,0:T(8,128)S(1)}, f32[24,8,128]{2,1,0:T(8,128)S(1)}, u32[]{:S(2)}, u32[]{:S(2)}) collective-permute-start(f32[24,8,128]{2,1,0:T(8,128)S(1)} %get-tuple-element.45), channel_id=1, source_target_pairs={{0,3},{1,2},{2,1},{3,0},{4,7},{5,6},{6,5},{7,4},{8,11},{9,10},{10,... | collective-permute-start | bytes 294920 | tf_op jit(solution)/shard_map/ppermute | solution.py:440
  114.1 1.8 %collective-permute-done.23.refs_3_ = f32[24,8,128]{2,1,0:T(8,128)S(1)} collective-permute-done((f32[24,8,128]{2,1,0:T(8,128)S(1)}, f32[24,8,128]{2,1,0:T(8,128)S(1)}, u32[]{:S(2)}, u32[]{:S(2)}) %collective-permute-start.23) | collective-permute-done | bytes 98336 | tf_op jit(solution)/shard_map/ppermute | solution.py:440
  (45 shorter events, 17.3 us)
Async XLA Ops:
  2.8 12.0 %collective-permute-start = (f32[96,8,128]{2,1,0:T(8,128)S(1)}, f32[96,8,128]{2,1,0:T(8,128)S(1)}, u32[]{:S(2)}, u32[]{:S(2)}) collective-permute-start(f32[96,8,128]{2,1,0:T(8,128)S(1)} %get-tuple-element.26), channel_id=1, source_target_pairs={{0,28},{4,0},{8,4},{12,8},{16,12},{20,16},{24,20},{28,24},{1,29},{... | collective-permute-start | bytes 1179656 | tf_op jit(solution)/shard_map/ppermute | solution.py:677
  6.2 10.5 %collective-permute-start.1 = (f32[96,8,128]{2,1,0:T(8,128)S(1)}, f32[96,8,128]{2,1,0:T(8,128)S(1)}, u32[]{:S(2)}, u32[]{:S(2)}) collective-permute-start(f32[96,8,128]{2,1,0:T(8,128)S(1)} %get-tuple-element.27), channel_id=1, source_target_pairs={{0,4},{4,8},{8,12},{12,16},{16,20},{20,24},{24,28},{28,0},{1,5},{5... | collective-permute-start | bytes 1179656 | tf_op jit(solution)/shard_map/ppermute | solution.py:676
  17.7 9.4 %collective-permute-start.2 = (f32[96,8,128]{2,1,0:T(8,128)S(1)}, f32[96,8,128]{2,1,0:T(8,128)S(1)}, u32[]{:S(2)}, u32[]{:S(2)}) collective-permute-start(f32[96,8,128]{2,1,0:T(8,128)S(1)} %get-tuple-element.29), channel_id=1, source_target_pairs={{0,28},{4,0},{8,4},{12,8},{16,12},{20,16},{24,20},{28,24},{1,29},{... | collective-permute-start | bytes 1179656 | tf_op jit(solution)/shard_map/ppermute | solution.py:677
  18.6 10.5 %collective-permute-start.3 = (f32[96,8,128]{2,1,0:T(8,128)S(1)}, f32[96,8,128]{2,1,0:T(8,128)S(1)}, u32[]{:S(2)}, u32[]{:S(2)}) collective-permute-start(f32[96,8,128]{2,1,0:T(8,128)S(1)} %get-tuple-element.30), channel_id=1, source_target_pairs={{0,4},{4,8},{8,12},{12,16},{16,20},{20,24},{24,28},{28,0},{1,5},{5... | collective-permute-start | bytes 1179656 | tf_op jit(solution)/shard_map/ppermute | solution.py:676
  18.6 24.3 %collective-permute-start.11 = (f32[11,64,128]{2,1,0:T(8,128)S(1)}, f32[11,64,128]{2,1,0:T(8,128)S(1)}, u32[]{:S(2)}, u32[]{:S(2)}) collective-permute-start(f32[11,64,128]{2,1,0:T(8,128)S(1)} %get-tuple-element.37), channel_id=1, source_target_pairs={{0,1},{1,0},{2,3},{3,2},{4,5},{5,4},{6,7},{7,6},{8,9},{9,8},{10,11... | collective-permute-start | bytes 1081352 | tf_op jit(solution)/shard_map/ppermute | solution.py:440
  31.1 1.2 %collective-permute-start.4 = (f32[8,128]{1,0:T(8,128)S(1)}, f32[8,128]{1,0:T(8,128)S(1)}, u32[]{:S(2)}, u32[]{:S(2)}) collective-permute-start(f32[8,128]{1,0:T(8,128)S(1)} %get-tuple-element.31), channel_id=1, source_target_pairs={{0,4},{4,0},{8,12},{12,8},{16,20},{20,16},{24,28},{28,24},{1,5},{5... | collective-permute-start | bytes 12296 | tf_op jit(solution)/shard_map/ppermute | solution.py:453
  32.4 6.1 %collective-permute-start.5 = (f32[8,128]{1,0:T(8,128)S(1)}, f32[8,128]{1,0:T(8,128)S(1)}, u32[]{:S(2)}, u32[]{:S(2)}) collective-permute-start(f32[8,128]{1,0:T(8,128)S(1)} %add.33), channel_id=1, source_target_pairs={{0,8},{4,12},{8,0},{12,4},{16,24},{20,28},{24,16},{28,20},{1,9},{5... | collective-permute-start | bytes 12296 | tf_op jit(solution)/shard_map/ppermute | solution.py:453
  33.4 6.4 %collective-permute-start.6 = (f32[8,128]{1,0:T(8,128)S(1)}, f32[8,128]{1,0:T(8,128)S(1)}, u32[]{:S(2)}, u32[]{:S(2)}) collective-permute-start(f32[8,128]{1,0:T(8,128)S(1)} %add.33), channel_id=1, source_target_pairs={{0,16},{4,20},{8,24},{12,28},{16,0},{20,4},{24,8},{28,12},{1,17},{... | collective-permute-start | bytes 12296 | tf_op jit(solution)/shard_map/ppermute | solution.py:453
  33.7 6.1 %collective-permute-start.7 = (f32[8,128]{1,0:T(8,128)S(1)}, f32[8,128]{1,0:T(8,128)S(1)}, u32[]{:S(2)}, u32[]{:S(2)}) collective-permute-start(f32[8,128]{1,0:T(8,128)S(1)} %add.33), channel_id=1, source_target_pairs={{0,24},{4,28},{8,16},{12,20},{16,8},{20,12},{24,0},{28,4},{1,25},{... | collective-permute-start | bytes 12296 | tf_op jit(solution)/shard_map/ppermute | solution.py:453
  35.8 36.4 %collective-permute-start.12 = (f32[11,64,128]{2,1,0:T(8,128)S(1)}, f32[11,64,128]{2,1,0:T(8,128)S(1)}, u32[]{:S(2)}, u32[]{:S(2)}) collective-permute-start(f32[11,64,128]{2,1,0:T(8,128)S(1)} %get-tuple-element.38), channel_id=1, source_target_pairs={{0,2},{1,3},{2,0},{3,1},{4,6},{5,7},{6,4},{7,5},{8,10},{9,11},{10,... | collective-permute-start | bytes 1081352 | tf_op jit(solution)/shard_map/ppermute | solution.py:440
  38.4 33.9 %collective-permute-start.13 = (f32[11,64,128]{2,1,0:T(8,128)S(1)}, f32[11,64,128]{2,1,0:T(8,128)S(1)}, u32[]{:S(2)}, u32[]{:S(2)}) collective-permute-start(f32[11,64,128]{2,1,0:T(8,128)S(1)} %get-tuple-element.39), channel_id=1, source_target_pairs={{0,3},{1,2},{2,1},{3,0},{4,7},{5,6},{6,5},{7,4},{8,11},{9,10},{10,... | collective-permute-start | bytes 1081352 | tf_op jit(solution)/shard_map/ppermute | solution.py:440
  40.4 31.9 %collective-permute-start.10 = (f32[424,128]{1,0:T(8,128)S(1)}, f32[424,128]{1,0:T(8,128)S(1)}, u32[]{:S(2)}, u32[]{:S(2)}) collective-permute-start(f32[424,128]{1,0:T(8,128)S(1)} %get-tuple-element.36), channel_id=1, source_target_pairs={{0,3},{1,2},{2,1},{3,0},{4,7},{5,6},{6,5},{7,4},{8,11},{9,10},{10,... | collective-permute-start | bytes 651272 | tf_op jit(solution)/shard_map/ppermute | solution.py:440
  42.9 29.4 %collective-permute-start.8 = (f32[424,128]{1,0:T(8,128)S(1)}, f32[424,128]{1,0:T(8,128)S(1)}, u32[]{:S(2)}, u32[]{:S(2)}) collective-permute-start(f32[424,128]{1,0:T(8,128)S(1)} %get-tuple-element.34), channel_id=1, source_target_pairs={{0,1},{1,0},{2,3},{3,2},{4,5},{5,4},{6,7},{7,6},{8,9},{9,8},{10,11... | collective-permute-start | bytes 651272 | tf_op jit(solution)/shard_map/ppermute | solution.py:440
  42.9 45.3 %collective-permute-start.9 = (f32[424,128]{1,0:T(8,128)S(1)}, f32[424,128]{1,0:T(8,128)S(1)}, u32[]{:S(2)}, u32[]{:S(2)}) collective-permute-start(f32[424,128]{1,0:T(8,128)S(1)} %get-tuple-element.35), channel_id=1, source_target_pairs={{0,2},{1,3},{2,0},{3,1},{4,6},{5,7},{6,4},{7,5},{8,10},{9,11},{10,... | collective-permute-start | bytes 651272 | tf_op jit(solution)/shard_map/ppermute | solution.py:440
  89.4 1.2 %collective-permute-start.14 = (f32[16,32]{1,0:T(8,128)S(1)}, f32[16,32]{1,0:T(8,128)S(1)}, u32[]{:S(2)}, u32[]{:S(2)}) collective-permute-start(f32[16,32]{1,0:T(8,128)S(1)} %get-tuple-element.40), channel_id=1, source_target_pairs={{0,4},{4,0},{8,12},{12,8},{16,20},{20,16},{24,28},{28,24},{1,5},{5... | collective-permute-start | bytes 6152 | tf_op jit(solution)/shard_map/ppermute | solution.py:453
  90.6 3.7 %collective-permute-start.15 = (f32[16,32]{1,0:T(8,128)S(1)}, f32[16,32]{1,0:T(8,128)S(1)}, u32[]{:S(2)}, u32[]{:S(2)}) collective-permute-start(f32[16,32]{1,0:T(8,128)S(1)} %add.37), channel_id=1, source_target_pairs={{0,8},{4,12},{8,0},{12,4},{16,24},{20,28},{24,16},{28,20},{1,9},{5... | collective-permute-start | bytes 6152 | tf_op jit(solution)/shard_map/ppermute | solution.py:453
  91.8 3.7 %collective-permute-start.16 = (f32[16,32]{1,0:T(8,128)S(1)}, f32[16,32]{1,0:T(8,128)S(1)}, u32[]{:S(2)}, u32[]{:S(2)}) collective-permute-start(f32[16,32]{1,0:T(8,128)S(1)} %add.37), channel_id=1, source_target_pairs={{0,16},{4,20},{8,24},{12,28},{16,0},{20,4},{24,8},{28,12},{1,17},{... | collective-permute-start | bytes 6152 | tf_op jit(solution)/shard_map/ppermute | solution.py:453
  92.2 4.5 %collective-permute-start.17 = (f32[16,32]{1,0:T(8,128)S(1)}, f32[16,32]{1,0:T(8,128)S(1)}, u32[]{:S(2)}, u32[]{:S(2)}) collective-permute-start(f32[16,32]{1,0:T(8,128)S(1)} %add.37), channel_id=1, source_target_pairs={{0,24},{4,28},{8,16},{12,20},{16,8},{20,12},{24,0},{28,4},{1,25},{... | collective-permute-start | bytes 6152 | tf_op jit(solution)/shard_map/ppermute | solution.py:453
  96.7 4.4 %collective-permute-start.18 = (f32[16,32]{1,0:T(8,128)S(1)}, f32[16,32]{1,0:T(8,128)S(1)}, u32[]{:S(2)}, u32[]{:S(2)}) collective-permute-start(f32[16,32]{1,0:T(8,128)S(1)} %add_add_fusion.1), channel_id=1, source_target_pairs={{0,1},{1,0},{2,3},{3,2},{4,5},{5,4},{6,7},{7,6},{8,9},{9,8},{10,11... | collective-permute-start | bytes 6152 | tf_op jit(solution)/shard_map/ppermute | solution.py:453
  97.4 5.0 %collective-permute-start.19 = (f32[16,32]{1,0:T(8,128)S(1)}, f32[16,32]{1,0:T(8,128)S(1)}, u32[]{:S(2)}, u32[]{:S(2)}) collective-permute-start(f32[16,32]{1,0:T(8,128)S(1)} %add_add_fusion.1), channel_id=1, source_target_pairs={{0,2},{1,3},{2,0},{3,1},{4,6},{5,7},{6,4},{7,5},{8,10},{9,11},{10,... | collective-permute-start | bytes 6152 | tf_op jit(solution)/shard_map/ppermute | solution.py:453
  100.8 5.5 %collective-permute-start.20 = (f32[16,32]{1,0:T(8,128)S(1)}, f32[16,32]{1,0:T(8,128)S(1)}, u32[]{:S(2)}, u32[]{:S(2)}) collective-permute-start(f32[16,32]{1,0:T(8,128)S(1)} %add_add_fusion.1), channel_id=1, source_target_pairs={{0,3},{1,2},{2,1},{3,0},{4,7},{5,6},{6,5},{7,4},{8,11},{9,10},{10,... | collective-permute-start | bytes 6152 | tf_op jit(solution)/shard_map/ppermute | solution.py:453
  107.7 6.4 %collective-permute-start.21 = (f32[24,8,128]{2,1,0:T(8,128)S(1)}, f32[24,8,128]{2,1,0:T(8,128)S(1)}, u32[]{:S(2)}, u32[]{:S(2)}) collective-permute-start(f32[24,8,128]{2,1,0:T(8,128)S(1)} %get-tuple-element.43), channel_id=1, source_target_pairs={{0,1},{1,0},{2,3},{3,2},{4,5},{5,4},{6,7},{7,6},{8,9},{9,8},{10,11... | collective-permute-start | bytes 294920 | tf_op jit(solution)/shard_map/ppermute | solution.py:440
  107.8 6.3 %collective-permute-start.22 = (f32[24,8,128]{2,1,0:T(8,128)S(1)}, f32[24,8,128]{2,1,0:T(8,128)S(1)}, u32[]{:S(2)}, u32[]{:S(2)}) collective-permute-start(f32[24,8,128]{2,1,0:T(8,128)S(1)} %get-tuple-element.44), channel_id=1, source_target_pairs={{0,2},{1,3},{2,0},{3,1},{4,6},{5,7},{6,4},{7,5},{8,10},{9,11},{10,... | collective-permute-start | bytes 294920 | tf_op jit(solution)/shard_map/ppermute | solution.py:440
  108.6 7.3 %collective-permute-start.23 = (f32[24,8,128]{2,1,0:T(8,128)S(1)}, f32[24,8,128]{2,1,0:T(8,128)S(1)}, u32[]{:S(2)}, u32[]{:S(2)}) collective-permute-start(f32[24,8,128]{2,1,0:T(8,128)S(1)} %get-tuple-element.45), channel_id=1, source_target_pairs={{0,3},{1,2},{2,1},{3,0},{4,7},{5,6},{6,5},{7,4},{8,11},{9,10},{10,... | collective-permute-start | bytes 294920 | tf_op jit(solution)/shard_map/ppermute | solution.py:440
  (2 other events, 19.6 us)
